TPU v7x, 32 devices: a whole 2x2x4 slice. The times are simulated.
32 devices in a mesh: dp: 16 (over z, y, x), mp: 2 (over core).
Axes of the slice: x: 2, y: 2, z: 4, core: 2. Of those that a mesh axis runs over, the one named last changes fastest.
Arguments:
- tokens: bfloat16 [8192, 2048], P('dp'), may hold values from -6 to 6
- cotangent: bfloat16 [8192, 2048], P('dp'), may hold values from -6 to 6
- lengths: int32 [64], replicated, may hold values from 0 to 512, as said below
- seq_deal: int32 [64], replicated, may hold values from 0 to 63, as said below
- token_order: int32 [8192], replicated, may hold values from 0 to 8191, as said below
- gain_attn: float32 [2048], P('dp'), may hold values from 0.5 to 1.5
- w_query: float32 [2048, 2048], P('dp', 'mp'), may hold values from -0.125 to 0.125
- key_weight: float32 [2048, 1024], P('dp', 'mp'), may hold values from -0.125 to 0.125
- value_weight: float32 [2048, 1024], P('dp', 'mp'), may hold values from -0.125 to 0.125
- w_out: float32 [2048, 2048], P('mp', 'dp'), may hold values from -1 to 1
- gain_ffn: float32 [2048], P('dp'), may hold values from 0.5 to 1.5
- w_gate: float32 [2048, 8192], P('dp', 'mp'), may hold values from -0.125 to 0.125
- w_up: float32 [2048, 8192], P('dp', 'mp'), may hold values from -0.125 to 0.125
- w_down: float32 [8192, 2048], P('mp', 'dp'), may hold values from -0.0625 to 0.0625
- moment_gain_attn: float32 [2048], P('dp'), may hold values from -6 to 6
- moment_w_query: float32 [2048, 2048], P('dp', 'mp'), may hold values from -6 to 6
- key_weight_momentum: float32 [2048, 1024], P('dp', 'mp'), may hold values from -6 to 6
- value_weight_momentum: float32 [2048, 1024], P('dp', 'mp'), may hold values from -6 to 6
- moment_w_out: float32 [2048, 2048], P('mp', 'dp'), may hold values from -6 to 6
- moment_gain_ffn: float32 [2048], P('dp'), may hold values from -6 to 6
- moment_w_gate: float32 [2048, 8192], P('dp', 'mp'), may hold values from -6 to 6
- moment_w_up: float32 [2048, 8192], P('dp', 'mp'), may hold values from -6 to 6
- moment_w_down: float32 [8192, 2048], P('mp', 'dp'), may hold values from -6 to 6
Outputs:
- activations: bfloat16 [8192, 2048], P('dp')
- input_grad: bfloat16 [8192, 2048], P('dp')
- grad_norm: float32 [], replicated
- next_moment_gain_attn: float32 [2048], P('dp')
- next_moment_w_query: float32 [2048, 2048], P('dp', 'mp')
- next_moment_w_key: float32 [2048, 1024], P('dp', 'mp')
- next_moment_w_value: float32 [2048, 1024], P('dp', 'mp')
- next_moment_w_out: float32 [2048, 2048], P('mp', 'dp')
- next_moment_gain_ffn: float32 [2048], P('dp')
- next_moment_w_gate: float32 [2048, 8192], P('dp', 'mp')
- next_moment_w_up: float32 [2048, 8192], P('dp', 'mp')
- next_moment_w_down: float32 [8192, 2048], P('mp', 'dp')
- next_gain_attn: float32 [2048], P('dp')
- next_w_query: float32 [2048, 2048], P('dp', 'mp')
- next_w_key: float32 [2048, 1024], P('dp', 'mp')
- next_w_value: float32 [2048, 1024], P('dp', 'mp')
- next_w_out: float32 [2048, 2048], P('mp', 'dp')
- next_gain_ffn: float32 [2048], P('dp')
- next_w_gate: float32 [2048, 8192], P('dp', 'mp')
- next_w_up: float32 [2048, 8192], P('dp', 'mp')
- next_w_down: float32 [8192, 2048], P('mp', 'dp')
Inputs may be any that keep to these rules, and one draw needn't show every extreme that they name: The 4 sequences of each aligned group of 4 dealt slots have lengths that sum to 512; some sequence has exactly 512 tokens; lengths of 0 occur. `seq_deal`: A permutation of the 64 sequence numbers. `token_order`: A permutation of the 8192 rows; the 512 dealt positions of each aligned block take exactly 32 rows from each aligned block of 512 rows of tokens.
All inputs are finite; a program needn't handle non-finite values.
Results may differ from a plain program's by a relative error of at most 0.014.
Values may be sent and summed in bfloat16 or wider, within the bound.
A program may use at most 320 MiB of HBM per device.

v0:
```python
import math

import jax
import jax.numpy as jnp
from jax import lax
from jax.sharding import PartitionSpec as P

HEAD_SIZE = 256
PARAMS = 62918656


EPS = 1e-06
THETA = 1000042.0
LEARN = 0.5
DECAY = 0.1


def angles(position, head):
    half = head // 2
    freq = THETA ** (-(2.0 * jnp.arange(half, dtype=jnp.float32)) / head)
    turned = position[:, None] * freq[None, :]
    return (jnp.cos(turned)[:, None, :], jnp.sin(turned)[:, None, :])


def apply_rotary(value_matrix, cosine_table, sine_table):
    half = value_matrix.shape[-1] // 2
    first = value_matrix[..., :half]
    second = value_matrix[..., half:]
    return jnp.concatenate(
        [first * cosine_table - second * sine_table, second * cosine_table + first * sine_table],
        axis=-1,
    )


def unrotate(grads, cosine_table, sine_table):
    half = grads.shape[-1] // 2
    first = grads[..., :half]
    second = grads[..., half:]
    return jnp.concatenate(
        [first * cosine_table + second * sine_table, second * cosine_table - first * sine_table],
        axis=-1,
    )


def layout(block_len, row_count_local):
    ends = jnp.cumsum(block_len)
    starts = ends - block_len
    index = jnp.arange(row_count_local, dtype=jnp.int32)
    inside = (index[:, None] >= starts[None, :]) & (index[:, None] < ends[None, :])
    slots = jnp.arange(block_len.shape[0], dtype=jnp.int32)
    segment = jnp.sum(jnp.where(inside, slots[None, :], 0), axis=1)
    position = jnp.sum(jnp.where(inside, index[:, None] - starts[None, :], 0), axis=1)
    mask = (segment[:, None] == segment[None, :]) & (index[None, :] <= index[:, None])
    return (position.astype(jnp.float32), mask)


def normalize(value_matrix):
    scale_inv = lax.rsqrt(jnp.mean(value_matrix * value_matrix, axis=-1, keepdims=True) + EPS)
    return (value_matrix * scale_inv, scale_inv)


def norm_back(grad_normed, normed, scale_inv, gain):
    scaled = grad_normed * gain
    return scale_inv * (scaled - normed * jnp.mean(scaled * normed, axis=-1, keepdims=True))


def mat_nt(left, right):
    return lax.dot_general(
        left, right, (((1,), (1,)), ((), ())), preferred_element_type=jnp.float32
    )


def mat_tn(left, right):
    return lax.dot_general(
        left, right, (((0,), (0,)), ((), ())), preferred_element_type=jnp.float32
    )


def head_sum(partial_value):
    return lax.psum(partial_value, "mp")


def fetch_attn(gain_attn, w_query, key_weight, value_weight, w_out):
    return (
        lax.all_gather(gain_attn.astype(jnp.bfloat16), "dp", axis=0, tiled=True),
        lax.all_gather(w_query.astype(jnp.bfloat16), "dp", axis=0, tiled=True),
        lax.all_gather(key_weight.astype(jnp.bfloat16), "dp", axis=0, tiled=True),
        lax.all_gather(value_weight.astype(jnp.bfloat16), "dp", axis=0, tiled=True),
        lax.all_gather(w_out.astype(jnp.bfloat16), "dp", axis=1, tiled=True),
    )


def fetch_ffn(gain_ffn, w_gate, w_up, w_down):
    return (
        lax.all_gather(gain_ffn.astype(jnp.bfloat16), "dp", axis=0, tiled=True),
        lax.all_gather(w_gate.astype(jnp.bfloat16), "dp", axis=0, tiled=True),
        lax.all_gather(w_up.astype(jnp.bfloat16), "dp", axis=0, tiled=True),
        lax.all_gather(w_down.astype(jnp.bfloat16), "dp", axis=1, tiled=True),
    )


def attn_scores(query_rotated, key_rot, mask):
    scores = jnp.einsum(
        "rhgd,chd->hgrc", query_rotated, key_rot, preferred_element_type=jnp.float32
    ) * HEAD_SIZE ** (-0.5)
    return jnp.where(mask[None, None], scores, -1e30)


def on_device(
    tokens,
    cotangent,
    lengths,
    seq_deal,
    token_order,
    gain_attn,
    w_query,
    key_weight,
    value_weight,
    w_out,
    gain_ffn,
    w_gate,
    w_up,
    w_down,
    moment_gain_attn,
    moment_w_query,
    key_weight_momentum,
    value_weight_momentum,
    moment_w_out,
    moment_gain_ffn,
    moment_w_gate,
    moment_w_up,
    moment_w_down,
):
    row_count_local = tokens.shape[0]
    total_rows = token_order.shape[0]
    device = lax.axis_index("dp")
    place = (
        jnp.zeros((total_rows,), jnp.int32)
        .at[token_order]
        .set(jnp.arange(total_rows, dtype=jnp.int32))
    )
    own_place = lax.dynamic_slice_in_dim(place, device * row_count_local, row_count_local)
    send_order = jnp.argsort(own_place)
    wanted = lax.dynamic_slice_in_dim(token_order, device * row_count_local, row_count_local)
    arrival = jnp.argsort(
        wanted // row_count_local * row_count_local + jnp.arange(row_count_local, dtype=jnp.int32)
    )
    arrival_rank = jnp.argsort(arrival)
    got_tokens, got_cot = (
        lax.all_to_all(tokens[send_order], "dp", split_axis=0, concat_axis=0, tiled=True),
        lax.all_to_all(cotangent[send_order], "dp", split_axis=0, concat_axis=0, tiled=True),
    )
    dealt = got_tokens[arrival_rank]
    dealt_cot = got_cot[arrival_rank]
    seq_dev = seq_deal.shape[0] // lax.axis_size("dp")
    mine = lax.dynamic_slice_in_dim(seq_deal, device * seq_dev, seq_dev)
    block_len = lengths[mine]
    position, mask = layout(block_len, row_count_local)
    cosine_table, sine_table = angles(position, HEAD_SIZE)
    gain_a, query_w, key_w, value_w, out_w = fetch_attn(
        gain_attn, w_query, key_weight, value_weight, w_out
    )
    gain_f, gate_w, up_w, down_w = fetch_ffn(gain_ffn, w_gate, w_up, w_down)
    heads_q = query_w.shape[1] // HEAD_SIZE
    heads_kv = key_w.shape[1] // HEAD_SIZE
    head_group = heads_q // heads_kv
    inputs = dealt.astype(jnp.float32)
    normed1, scale1 = normalize(inputs)
    hidden_after_attention = (normed1 * gain_a).astype(jnp.bfloat16)
    query_matrix = jnp.dot(
        hidden_after_attention, query_w, preferred_element_type=jnp.float32
    ).reshape(row_count_local, heads_q, HEAD_SIZE)
    key_matrix = jnp.dot(hidden_after_attention, key_w, preferred_element_type=jnp.float32).reshape(
        row_count_local, heads_kv, HEAD_SIZE
    )
    value_matrix = (
        jnp.dot(hidden_after_attention, value_w, preferred_element_type=jnp.float32)
        .astype(jnp.bfloat16)
        .reshape(row_count_local, heads_kv, HEAD_SIZE)
    )
    query_rotated = (
        apply_rotary(query_matrix, cosine_table, sine_table)
        .astype(jnp.bfloat16)
        .reshape(row_count_local, heads_kv, head_group, HEAD_SIZE)
    )
    key_rot = apply_rotary(key_matrix, cosine_table, sine_table).astype(jnp.bfloat16)
    scores = attn_scores(query_rotated, key_rot, mask)
    top = jnp.max(scores, axis=-1, keepdims=True)
    expo = jnp.exp(scores - top)
    total = jnp.sum(expo, axis=-1, keepdims=True)
    lse = top + jnp.log(total)
    prob_low = (expo / total).astype(jnp.bfloat16)
    mixed_low = (
        jnp.einsum("hgrc,chd->rhgd", prob_low, value_matrix, preferred_element_type=jnp.float32)
        .reshape(row_count_local, heads_q * HEAD_SIZE)
        .astype(jnp.bfloat16)
    )
    middle = inputs + head_sum(jnp.dot(mixed_low, out_w, preferred_element_type=jnp.float32))
    normed2, scale2 = normalize(middle)
    hidden2 = (normed2 * gain_f).astype(jnp.bfloat16)
    gate = jnp.dot(hidden2, gate_w, preferred_element_type=jnp.float32)
    upper = jnp.dot(hidden2, up_w, preferred_element_type=jnp.float32)
    activ = jax.nn.silu(gate)
    inner = (activ * upper).astype(jnp.bfloat16)
    result = middle + head_sum(jnp.dot(inner, down_w, preferred_element_type=jnp.float32))
    grad_out = dealt_cot.astype(jnp.float32)
    grad_inner = mat_nt(dealt_cot, down_w)
    grad_wd = mat_tn(inner, dealt_cot)
    sigma = jax.nn.sigmoid(gate)
    grad_gate = (grad_inner * upper * (sigma * (1.0 + gate * (1.0 - sigma)))).astype(jnp.bfloat16)
    grad_up = (grad_inner * activ).astype(jnp.bfloat16)
    grad_wg = mat_tn(hidden2, grad_gate)
    grad_wu = mat_tn(hidden2, grad_up)
    grad_h2 = head_sum(mat_nt(grad_gate, gate_w) + mat_nt(grad_up, up_w))
    grad_gf = jnp.sum(grad_h2 * normed2, axis=0)
    grad_mid = grad_out + norm_back(grad_h2, normed2, scale2, gain_f)
    owned_ffn = (grad_gf, grad_wg, grad_wu, grad_wd)
    mid_low = grad_mid.astype(jnp.bfloat16)
    grad_wo = mat_tn(mixed_low, mid_low)
    grad_mixed = (
        mat_nt(mid_low, out_w)
        .astype(jnp.bfloat16)
        .reshape(row_count_local, heads_kv, head_group, HEAD_SIZE)
    )
    prob = jnp.exp(attn_scores(query_rotated, key_rot, mask) - lse)
    prob_back = prob.astype(jnp.bfloat16)
    grad_prob = jnp.einsum(
        "rhgd,chd->hgrc", grad_mixed, value_matrix, preferred_element_type=jnp.float32
    )
    delta = jnp.sum(prob * grad_prob, axis=-1, keepdims=True)
    grad_scores = (prob * (grad_prob - delta)).astype(jnp.bfloat16)
    grad_qrot = jnp.einsum(
        "hgrc,chd->rhgd", grad_scores, key_rot, preferred_element_type=jnp.float32
    ) * HEAD_SIZE ** (-0.5)
    grad_krot = jnp.einsum(
        "hgrc,rhgd->chd", grad_scores, query_rotated, preferred_element_type=jnp.float32
    ) * HEAD_SIZE ** (-0.5)
    grad_values = jnp.einsum(
        "hgrc,rhgd->chd", prob_back, grad_mixed, preferred_element_type=jnp.float32
    )
    grad_query = (
        unrotate(grad_qrot.reshape(row_count_local, heads_q, HEAD_SIZE), cosine_table, sine_table)
        .reshape(row_count_local, heads_q * HEAD_SIZE)
        .astype(jnp.bfloat16)
    )
    grad_keys = (
        unrotate(grad_krot, cosine_table, sine_table)
        .reshape(row_count_local, heads_kv * HEAD_SIZE)
        .astype(jnp.bfloat16)
    )
    grad_vlow = grad_values.reshape(row_count_local, heads_kv * HEAD_SIZE).astype(jnp.bfloat16)
    grad_h1 = head_sum(
        mat_nt(grad_query, query_w) + mat_nt(grad_keys, key_w) + mat_nt(grad_vlow, value_w)
    )
    grad_wq = mat_tn(hidden_after_attention, grad_query)
    grad_wk = mat_tn(hidden_after_attention, grad_keys)
    grad_wv = mat_tn(hidden_after_attention, grad_vlow)
    grad_ga = jnp.sum(grad_h1 * normed1, axis=0)
    grad_in = grad_mid + norm_back(grad_h1, normed1, scale1, gain_a)
    owned = (
        lax.psum_scatter(grad_ga, "dp", scatter_dimension=0, tiled=True),
        lax.psum_scatter(grad_wq, "dp", scatter_dimension=0, tiled=True),
        lax.psum_scatter(grad_wk, "dp", scatter_dimension=0, tiled=True),
        lax.psum_scatter(grad_wv, "dp", scatter_dimension=0, tiled=True),
        lax.psum_scatter(grad_wo, "dp", scatter_dimension=1, tiled=True),
        lax.psum_scatter(owned_ffn[0], "dp", scatter_dimension=0, tiled=True),
        lax.psum_scatter(owned_ffn[1], "dp", scatter_dimension=0, tiled=True),
        lax.psum_scatter(owned_ffn[2], "dp", scatter_dimension=0, tiled=True),
        lax.psum_scatter(owned_ffn[3], "dp", scatter_dimension=1, tiled=True),
    )
    back_out, back_grad = (
        lax.all_to_all(
            result.astype(jnp.bfloat16)[arrival], "dp", split_axis=0, concat_axis=0, tiled=True
        ),
        lax.all_to_all(
            grad_in.astype(jnp.bfloat16)[arrival], "dp", split_axis=0, concat_axis=0, tiled=True
        ),
    )
    send_rank = jnp.argsort(send_order)
    activations = back_out[send_rank]
    input_grad = back_grad[send_rank]
    share = 0.5 * (jnp.sum(owned[0] * owned[0]) + jnp.sum(owned[5] * owned[5]))
    for position_index in (1, 2, 3, 4, 6, 7, 8):
        share = share + jnp.sum(owned[position_index] * owned[position_index])
    grad_norm = jnp.sqrt(lax.psum(share, ("dp", "mp")))
    factor = jnp.minimum(1.0, math.sqrt(PARAMS) / grad_norm)
    weights = (gain_attn, w_query, key_weight, value_weight, w_out, gain_ffn, w_gate, w_up, w_down)
    moments = (
        moment_gain_attn,
        moment_w_query,
        key_weight_momentum,
        value_weight_momentum,
        moment_w_out,
        moment_gain_ffn,
        moment_w_gate,
        moment_w_up,
        moment_w_down,
    )
    new_moments = tuple(
        (0.5 * m_old + 0.5 * factor * g_new for m_old, g_new in zip(moments, owned))
    )
    new_weights = tuple(
        (w_old - LEARN * (m_new + DECAY * w_old) for w_old, m_new in zip(weights, new_moments))
    )
    return (
        activations,
        input_grad,
        grad_norm,
        new_moments[0],
        new_moments[1],
        new_moments[2],
        new_moments[3],
        new_moments[4],
        new_moments[5],
        new_moments[6],
        new_moments[7],
        new_moments[8],
        new_weights[0],
        new_weights[1],
        new_weights[2],
        new_weights[3],
        new_weights[4],
        new_weights[5],
        new_weights[6],
        new_weights[7],
        new_weights[8],
    )


def solution(mesh):
    in_specs = (
        P("dp", None),
        P("dp", None),
        P(),
        P(),
        P(),
        P("dp"),
        P("dp", "mp"),
        P("dp", "mp"),
        P("dp", "mp"),
        P("mp", "dp"),
        P("dp"),
        P("dp", "mp"),
        P("dp", "mp"),
        P("mp", "dp"),
        P("dp"),
        P("dp", "mp"),
        P("dp", "mp"),
        P("dp", "mp"),
        P("mp", "dp"),
        P("dp"),
        P("dp", "mp"),
        P("dp", "mp"),
        P("mp", "dp"),
    )
    out_specs = (
        P("dp", None),
        P("dp", None),
        P(),
        P("dp"),
        P("dp", "mp"),
        P("dp", "mp"),
        P("dp", "mp"),
        P("mp", "dp"),
        P("dp"),
        P("dp", "mp"),
        P("dp", "mp"),
        P("mp", "dp"),
        P("dp"),
        P("dp", "mp"),
        P("dp", "mp"),
        P("dp", "mp"),
        P("mp", "dp"),
        P("dp"),
        P("dp", "mp"),
        P("dp", "mp"),
        P("mp", "dp"),
    )
    return jax.shard_map(
        on_device, mesh=mesh, in_specs=in_specs, out_specs=out_specs, check_vma=False
    )
```

profile of v0, /device:TPU:0, one launch (start us, length us, event | category | flops | bytes accessed | tf_op | source)
XLA Modules:
  0.0 3951.0 jit_solution(3383638167860689898)
XLA Ops:
  13.4 30.5 scatter_custom_fusion
  43.9 3.8 sort.59
  51.6 8.5 all-to-all-start
  62.0 74.4 %all-gather = bf16[16,1,128]{2,1,0:T(2,128)(2,1)S(1)} all-gather(bf16[1,1,128]{2,1,0:T(2,128)(2,1)S(1)} %convert_bitcast_fusion.1), channel_id=1, replica_groups=mesh['dp'=16,'mp'=2] {'dp'}, dimensions={0}, use_global_device_ids=true | all-gather | bytes 4352 | tf_op jit(solution)/shard_map/all_gather | solution.py:85
  137.2 3.8 sort.60
  141.0 3.8 sort.61
  162.5 3.8 convolution_convert_fusion.1
  166.3 74.2 %all-gather.14.cloned.1.call-done = bf16[2048,1024]{1,0:T(8,128)(2,1)} async-done(((bf16[128,1024]{1,0:T(8,128)(2,1)}), bf16[2048,1024]{1,0:T(8,128)(2,1)}) %all-gather.14.cloned.1.call-update) | async-done | bytes 4194320 | tf_op jit(solution)/shard_map/all_gather | solution.py:86
  240.5 5.9 fusion.51
  253.3 78.2 %all-gather.16.cloned.1.call-done = bf16[1024,2048]{1,0:T(8,128)(2,1)} async-done(((bf16[1024,128]{1,0:T(8,128)(2,1)}), bf16[1024,2048]{1,0:T(8,128)(2,1)}) %all-gather.16.cloned.1.call-update) | async-done | bytes 4194320 | tf_op jit(solution)/shard_map/all_gather | solution.py:89
  331.5 6.5 fusion.59
  350.6 3.9 all-to-all-start.2
  354.5 77.4 %all-gather.1 = bf16[16,1,128]{2,1,0:T(2,128)(2,1)S(1)} all-gather(bf16[1,1,128]{2,1,0:T(2,128)(2,1)S(1)} %convert_bitcast_fusion), channel_id=1, replica_groups=mesh['dp'=16,'mp'=2] {'dp'}, dimensions={0}, use_global_device_ids=true | all-gather | bytes 4352 | tf_op jit(solution)/shard_map/all_gather | solution.py:95
  441.2 138.1 %all-gather.20.cloned.1.call-done = bf16[2048,4096]{1,0:T(8,128)(2,1)} async-done(((bf16[128,4096]{1,0:T(8,128)(2,1)}), bf16[2048,4096]{1,0:T(8,128)(2,1)}) %all-gather.20.cloned.1.call-update) | async-done | bytes 16777232 | tf_op jit(solution)/shard_map/all_gather | solution.py:97
  579.3 14.3 fusion.61
  593.6 179.2 %all-gather.18.cloned.1.call-done = bf16[2048,4096]{1,0:T(8,128)(2,1)} async-done(((bf16[128,4096]{1,0:T(8,128)(2,1)}), bf16[2048,4096]{1,0:T(8,128)(2,1)}) %all-gather.18.cloned.1.call-update) | async-done | bytes 16777232 | tf_op jit(solution)/shard_map/all_gather | solution.py:96
  772.9 14.9 fusion.60
  787.8 236.6 %all-gather.22.cloned.1.call-done = bf16[4096,2048]{1,0:T(8,128)(2,1)} async-done(((bf16[4096,128]{1,0:T(8,128)(2,1)}), bf16[4096,2048]{1,0:T(8,128)(2,1)}) %all-gather.22.cloned.1.call-update) | async-done | bytes 16777232 | tf_op jit(solution)/shard_map/all_gather | solution.py:98
  1024.4 21.1 multiply_convert_fusion
  1045.5 16.5 fusion.63
  1062.0 14.5 convolution_add_fusion
  1076.5 15.7 fusion.62
  1092.3 11.0 all-reduce.10.cloned.1.call-done
  1103.3 4.6 multiply_reduce_fusion
  1115.5 3.9 fusion.28
  1151.5 6.6 fusion.49
  1159.4 7.8 fusion.31
  1169.1 19.0 fusion.66
  1188.4 17.6 fusion.67
  1207.6 17.6 fusion.68
  1225.9 4.1 add_convert_fusion
  1233.4 7.1 all-to-all-start.1
  1240.5 4.1 fusion.11
  1245.3 4.7 fusion.10
  1249.9 7.1 gather_fusion.7
  1257.0 34.8 all-to-all-done.1
  1293.1 24.6 all-to-all-start.3
  1317.8 3.8 sort.62
  1322.8 119.9 %all-reduce.2 = (f32[2048]{0:T(1024)S(1)}, f32[2048]{0:T(1024)S(1)}) all-reduce(f32[2048]{0:T(1024)S(1)} %get-tuple-element.31, f32[2048]{0:T(1024)S(1)} %get-tuple-element.29), channel_id=2, replica_groups=mesh['dp'=16,'mp'=2] {'dp'}, use_global_device_ids=true, to_apply=%region_20.21.clone | all-reduce | flops 4096 | bytes 32768
  1448.7 7.1 gather_fusion.4
  1455.8 164.1 %reduce-scatter.8.cloned.1.call-done = f32[128,1024]{1,0:T(8,128)} async-done(((f32[2048,1024]{1,0:T(8,128)}), f32[128,1024]{1,0:T(8,128)}) %reduce-scatter.8.cloned.1.call-update) | async-done | bytes 524304 | tf_op jit(solution)/shard_map/reduce_scatter | solution.py:262
  1623.5 178.7 %reduce-scatter.14.cloned.1.call-done = f32[1024,128]{1,0:T(8,128)} async-done(((f32[1024,2048]{1,0:T(8,128)}), f32[1024,128]{1,0:T(8,128)}) %reduce-scatter.14.cloned.1.call-update) | async-done | bytes 524304 | tf_op jit(solution)/shard_map/reduce_scatter | solution.py:265
  1804.7 685.6 %reduce-scatter.16.cloned.1.call-done = f32[128,4096]{1,0:T(8,128)} async-done(((f32[2048,4096]{1,0:T(8,128)}), f32[128,4096]{1,0:T(8,128)}) %reduce-scatter.16.cloned.1.call-update) | async-done | bytes 2097168 | tf_op jit(solution)/shard_map/reduce_scatter | solution.py:267
  2493.7 687.9 %reduce-scatter.18.cloned.1.call-done = f32[128,4096]{1,0:T(8,128)} async-done(((f32[2048,4096]{1,0:T(8,128)}), f32[128,4096]{1,0:T(8,128)}) %reduce-scatter.18.cloned.1.call-update) | async-done | bytes 2097168 | tf_op jit(solution)/shard_map/reduce_scatter | solution.py:268
  3185.0 687.9 %reduce-scatter.20.cloned.1.call-done = f32[4096,128]{1,0:T(8,128)} async-done(((f32[4096,2048]{1,0:T(8,128)}), f32[4096,128]{1,0:T(8,128)}) %reduce-scatter.20.cloned.1.call-update) | async-done | bytes 2097168 | tf_op jit(solution)/shard_map/reduce_scatter | solution.py:269
  3879.7 44.7 %psum.39 = f32[]{:T(128)} all-reduce(f32[]{:T(128)S(6)} %add.240), channel_id=1, replica_groups=mesh['dp'=16,'mp'=2] {'dp','mp'}, use_global_device_ids=true, to_apply=%region_39.40 | all-reduce | flops 1 | bytes 8 | tf_op jit(solution)/shard_map/psum | solution.py:285
  3930.6 4.5 multiply_subtract_fusion
  3937.2 5.6 multiply_subtract_fusion.1
  (297 shorter events, 137.0 us)
Async XLA Ops:
  7.2 41.1 %copy-start = (bf16[512,2048]{1,0:T(8,128)(2,1)S(1)}, bf16[512,2048]{1,0:T(8,128)(2,1)}, u32[]{:S(2)}) copy-start(bf16[512,2048]{1,0:T(8,128)(2,1)} %param.23) | copy-start | bytes 6291460
  7.2 145.1 %all-gather.12.cloned.1.call-start = ((), (), s32[]{:S(2)}) async-start(), calls=%async_computation.12 | async-start | bytes 2228224 | tf_op jit(solution)/shard_map/all_gather | solution.py:87
  9.0 153.5 %all-gather.10.cloned.1.call-start = ((), (), s32[]{:S(2)}) async-start(), calls=%async_computation.11 | async-start | bytes 2228224 | tf_op jit(solution)/shard_map/all_gather | solution.py:88
  10.7 229.8 %all-gather.14.cloned.1.call-start = ((), (), s32[]{:S(2)}) async-start(), calls=%async_computation.13 | async-start | bytes 4456448 | tf_op jit(solution)/shard_map/all_gather | solution.py:86
  51.6 8.5 copy-start.36
  51.6 9.3 copy-start.75
  51.6 9.4 copy-start.2
  51.6 10.4 copy-start.68
  51.6 95.1 %all-to-all-start = ((bf16[16,32,2048]{2,1,0:T(8,128)(2,1)}), bf16[16,32,2048]{2,1,0:T(8,128)(2,1)S(1)}, u32[]{:S(2)}, u32[]{:S(2)}) async-start(bf16[16,32,2048]{2,1,0:T(8,128)(2,1)} %bitcast.125), calls=%async_computation | async-start | bytes 4194304 | tf_op jit(solution)/shard_map/all_to_all | solution.py:150
  60.1 271.4 %all-gather.16.cloned.1.call-start = ((), (), s32[]{:S(2)}) async-start(), calls=%async_computation.14 | async-start | bytes 4456448 | tf_op jit(solution)/shard_map/all_gather | solution.py:89
  60.9 374.4 %all-reduce.8.cloned.1.call-start = ((), (), s32[]{:S(2)}) async-start(), calls=%async_computation.15 | async-start | bytes 8388608 | tf_op jit(solution)/shard_map/psum | solution.py:80
  136.4 104.1 %copy-start.51 = (f32[16,1,128]{2,1,0:T(1,128)}, f32[16,1,128]{2,1,0:T(1,128)S(1)}, u32[]{:S(2)}) copy-start(f32[16,1,128]{2,1,0:T(1,128)S(1)} %convert_element_type.151) | copy-start | bytes 24580
  146.7 102.0 %copy-start.26 = (f32[512,128]{1,0:T(8,128)}, f32[512,128]{1,0:T(8,128)S(1)}, u32[]{:S(2)}) copy-start(f32[512,128]{1,0:T(8,128)S(1)} %get-tuple-element.74) | copy-start | bytes 786436
  146.7 102.0 %copy-start.28 = (f32[512,128]{1,0:T(8,128)}, f32[512,128]{1,0:T(8,128)S(1)}, u32[]{:S(2)}) copy-start(f32[512,128]{1,0:T(8,128)S(1)} %get-tuple-element.75) | copy-start | bytes 786436
  152.3 88.2 %copy-start.62 = (f32[512]{0:T(512)}, f32[512]{0:T(512)S(1)}, u32[]{:S(2)}) copy-start(f32[512]{0:T(512)S(1)} %add_rsqrt_fusion.1) | copy-start | bytes 6148
  162.2 87.2 %copy-start.43 = (bf16[512,2,128]{2,0,1:T(8,128)(2,1)}, bf16[512,2,128]{2,0,1:T(8,128)(2,1)S(1)}, u32[]{:S(2)}) copy-start(bf16[512,2,128]{2,0,1:T(8,128)(2,1)S(1)} %get-tuple-element.70) | copy-start | bytes 786436
  253.3 78.2 %copy-start.30 = (bf16[2,256,2,512]{3,1,2,0:T(8,128)(2,1)}, bf16[2,256,2,512]{3,1,2,0:T(8,128)(2,1)S(1)}, u32[]{:S(2)}) copy-start(bf16[2,256,2,512]{3,1,2,0:T(8,128)(2,1)S(1)} %fusion.22) | copy-start | bytes 3145732
  338.0 241.3 %all-gather.20.cloned.1.call-start = ((), (), s32[]{:S(2)}) async-start(), calls=%async_computation.17 | async-start | bytes 17825792 | tf_op jit(solution)/shard_map/all_gather | solution.py:97
  340.7 432.1 %all-gather.18.cloned.1.call-start = ((), (), s32[]{:S(2)}) async-start(), calls=%async_computation.16 | async-start | bytes 17825792 | tf_op jit(solution)/shard_map/all_gather | solution.py:96
  343.9 680.5 %all-gather.22.cloned.1.call-start = ((), (), s32[]{:S(2)}) async-start(), calls=%async_computation.18 | async-start | bytes 17825792 | tf_op jit(solution)/shard_map/all_gather | solution.py:98
  350.6 81.3 %all-to-all-start.2 = ((bf16[16,32,2048]{2,1,0:T(8,128)(2,1)}), bf16[16,32,2048]{2,1,0:T(8,128)(2,1)S(1)}, u32[]{:S(2)}, u32[]{:S(2)}) async-start(bf16[16,32,2048]{2,1,0:T(8,128)(2,1)} %bitcast.127), calls=%async_computation.2 | async-start | bytes 4194304 | tf_op jit(solution)/shard_map/all_to_all | solution.py:151
  354.5 748.8 %all-reduce.10.cloned.1.call-start = ((), (), s32[]{:S(2)}) async-start(), calls=%async_computation.19 | async-start | bytes 8388608 | tf_op jit(solution)/shard_map/psum | solution.py:80
  441.2 138.1 %copy-start.34 = (bf16[512,2048]{1,0:T(8,128)(2,1)}, bf16[512,2048]{1,0:T(8,128)(2,1)S(1)}, u32[]{:S(2)}) copy-start(bf16[512,2048]{1,0:T(8,128)(2,1)S(1)} %multiply_convert_fusion.3) | copy-start | bytes 6291460
  593.6 430.7 %copy-start.24 = (bf16[512,2048]{1,0:T(8,128)(2,1)S(1)}, bf16[512,2048]{1,0:T(8,128)(2,1)}, u32[]{:S(2)}) copy-start(bf16[512,2048]{1,0:T(8,128)(2,1)} %gather_fusion.6) | copy-start | bytes 6291460
  1045.5 16.5 copy-start.77
  1076.5 149.5 %all-reduce.12.cloned.1.call-start = ((), (), s32[]{:S(2)}) async-start(), calls=%async_computation.27 | async-start | bytes 16777216 | tf_op jit(solution)/shard_map/psum | solution.py:80
  1141.5 303.9 %reduce-scatter.12.cloned.1.call-start = ((), (), s32[]{:S(2)}) async-start(), calls=%async_computation.22 | async-start | bytes 4456448 | tf_op jit(solution)/shard_map/reduce_scatter | solution.py:264
  1146.6 300.4 %reduce-scatter.10.cloned.1.call-start = ((), (), s32[]{:S(2)}) async-start(), calls=%async_computation.21 | async-start | bytes 4456448 | tf_op jit(solution)/shard_map/reduce_scatter | solution.py:263
  1150.2 469.6 %reduce-scatter.8.cloned.1.call-start = ((), (), s32[]{:S(2)}) async-start(), calls=%async_computation.20 | async-start | bytes 8912896 | tf_op jit(solution)/shard_map/reduce_scatter | solution.py:262
  1158.1 644.1 %reduce-scatter.14.cloned.1.call-start = ((), (), s32[]{:S(2)}) async-start(), calls=%async_computation.23 | async-start | bytes 8912896 | tf_op jit(solution)/shard_map/reduce_scatter | solution.py:265
  1167.2 1323.1 %reduce-scatter.16.cloned.1.call-start = ((), (), s32[]{:S(2)}) async-start(), calls=%async_computation.24 | async-start | bytes 35651584 | tf_op jit(solution)/shard_map/reduce_scatter | solution.py:267
  1188.1 1993.5 %reduce-scatter.18.cloned.1.call-start = ((), (), s32[]{:S(2)}) async-start(), calls=%async_computation.25 | async-start | bytes 35651584 | tf_op jit(solution)/shard_map/reduce_scatter | solution.py:268
  1206.0 2666.9 %reduce-scatter.20.cloned.1.call-start = ((), (), s32[]{:S(2)}) async-start(), calls=%async_computation.26 | async-start | bytes 35651584 | tf_op jit(solution)/shard_map/reduce_scatter | solution.py:269
  1233.4 58.4 %all-to-all-start.1 = ((bf16[16,32,2048]{2,1,0:T(8,128)(2,1)}), bf16[16,32,2048]{2,1,0:T(8,128)(2,1)S(1)}, u32[]{:S(2)}, u32[]{:S(2)}) async-start(bf16[16,32,2048]{2,1,0:T(8,128)(2,1)} %bitcast.126), calls=%async_computation.1 | async-start | bytes 4194304 | tf_op jit(solution)/shard_map/all_to_all | solution.py:272
  1257.0 60.7 %copy-start.65 = (s32[512]{0:T(512)S(1)}, s32[512]{0:T(512)}, u32[]{:S(2)}) copy-start(s32[512]{0:T(512)} %copy-done.64) | copy-start | bytes 6148
  1257.0 64.5 %copy-start.76 = (u32[32]{0:T(128)S(1)}, u32[32]{0:T(128)}, u32[]{:S(2)}) copy-start(u32[32]{0:T(128)} %constant.88) | copy-start | bytes 388
  1293.1 2583.2 %all-to-all-start.3 = ((bf16[16,32,2048]{2,1,0:T(8,128)(2,1)}), bf16[16,32,2048]{2,1,0:T(8,128)(2,1)S(1)}, u32[]{:S(2)}, u32[]{:S(2)}) async-start(bf16[16,32,2048]{2,1,0:T(8,128)(2,1)} %bitcast.124), calls=%async_computation.3 | async-start | bytes 4194304 | tf_op jit(solution)/shard_map/all_to_all | solution.py:275
  3876.3 48.8 %copy-start.69 = (f32[128]{0:T(128)S(1)}, f32[128]{0:T(128)}, u32[]{:S(2)}) copy-start(f32[128]{0:T(128)} %param.28) | copy-start | bytes 1540
  3876.3 48.8 %copy-start.71 = (f32[128]{0:T(128)S(1)}, f32[128]{0:T(128)}, u32[]{:S(2)}) copy-start(f32[128]{0:T(128)} %param.33) | copy-start | bytes 1540
  3876.3 48.8 %copy-start.72 = (f32[128]{0:T(128)S(1)}, f32[128]{0:T(128)}, u32[]{:S(2)}) copy-start(f32[128]{0:T(128)} %param.42) | copy-start | bytes 1540
  3876.4 48.8 %copy-start.73 = (f32[128]{0:T(128)S(1)}, f32[128]{0:T(128)}, u32[]{:S(2)}) copy-start(f32[128]{0:T(128)} %param.37) | copy-start | bytes 1540
  3876.4 49.4 %copy-start.37 = (f32[1024,128]{1,0:T(8,128)S(1)}, f32[1024,128]{1,0:T(8,128)}, u32[]{:S(2)}) copy-start(f32[1024,128]{1,0:T(8,128)} %param.32) | copy-start | bytes 1572868
  3876.4 51.7 %copy-start.38 = (f32[128,1024]{1,0:T(8,128)S(1)}, f32[128,1024]{1,0:T(8,128)}, u32[]{:S(2)}) copy-start(f32[128,1024]{1,0:T(8,128)} %param.29) | copy-start | bytes 1572868
  3876.4 58.8 %copy-start.47 = (f32[128,512]{1,0:T(8,128)S(1)}, f32[128,512]{1,0:T(8,128)}, u32[]{:S(2)}) copy-start(f32[128,512]{1,0:T(8,128)} %param.30) | copy-start | bytes 786436
  3879.7 50.9 %copy-start.22 = (f32[4096,128]{1,0:T(8,128)S(1)}, f32[4096,128]{1,0:T(8,128)}, u32[]{:S(2)}) copy-start(f32[4096,128]{1,0:T(8,128)} %param.36) | copy-start | bytes 6291460
  3928.1 7.1 copy-start.49
  3928.1 7.1 copy-start.50
  3928.1 7.1 copy-start.60
  (51 other events, 162.9 us)
Sparse Core Ops, SparseCore 0:
  11.4 79.1 all-gather.11
  93.9 68.5 all-gather.9
  165.8 74.6 all-gather.13
  243.6 87.7 all-gather.15
  338.2 26.6 all-reduce.7
  368.4 210.8 all-gather.19
  583.0 189.7 all-gather.17
  776.5 247.8 all-gather.21
  1076.6 26.6 all-reduce.9
  1141.7 40.0 all-reduce.11
  1184.1 122.4 reduce-scatter.11
  1308.7 126.2 reduce-scatter.9
  1437.3 182.4 reduce-scatter.7
  1622.0 180.2 reduce-scatter.13
  1804.4 685.8 reduce-scatter.15
  2492.5 689.0 reduce-scatter.17
  3183.8 689.0 reduce-scatter.19
where the time goes:
time: 3960 us; the launch traced here: 3950 us
  waiting for transfers between devices  3160 us (80%)
  blocking collectives  316 us (8%)
  matrix products  211 us (5%)
  local copies, waits for them, and re-layouts  100 us (3%)
  other arithmetic  96.3 us (2%)
  starting transfers between devices  45.6 us (1%)
    reduce_scatter x1, waiting for transfers between devices, on_device(): lax.psum_scatter(owned_ffn[2], 'dp', scatter_dimension=0, tiled=True)  688 us
    reduce_scatter x1, waiting for transfers between devices, on_device(): lax.psum_scatter(owned_ffn[3], 'dp', scatter_dimension=1, tiled=True)  688 us
    reduce_scatter x1, waiting for transfers between devices, on_device(): lax.psum_scatter(owned_ffn[1], 'dp', scatter_dimension=0, tiled=True)  686 us
    all_gather x1, waiting for transfers between devices, fetch_ffn(): lax.all_gather(w_down.astype(jnp.bfloat16), 'dp', axis=1, tiled=True)  237 us
    all_gather x1, waiting for transfers between devices, fetch_ffn(): lax.all_gather(w_gate.astype(jnp.bfloat16), 'dp', axis=0, tiled=True)  179 us
    reduce_scatter x1, waiting for transfers between devices, on_device(): lax.psum_scatter(grad_wo, 'dp', scatter_dimension=1, tiled=True)  179 us
    reduce_scatter x1, waiting for transfers between devices, on_device(): lax.psum_scatter(grad_wq, 'dp', scatter_dimension=0, tiled=True)  164 us
    all_gather x1, waiting for transfers between devices, fetch_ffn(): lax.all_gather(w_up.astype(jnp.bfloat16), 'dp', axis=0, tiled=True)  138 us
  transfers between devices with their start and end apart: 21, of which 13 were waited for; matrix products, arithmetic and copies ran while one was open for 7% of the time, Pallas kernels for 0%

commit v1 on v0

--- a/solution.py
+++ b/solution.py
@@ -43,7 +43,8 @@
 
 
 def layout(block_len, row_count_local):
-    ends = jnp.cumsum(block_len)
+    rank = jnp.arange(block_len.shape[0], dtype=jnp.int32)
+    ends = jnp.sum(jnp.where(rank[None, :] <= rank[:, None], block_len[None, :], 0), axis=1)
     starts = ends - block_len
     index = jnp.arange(row_count_local, dtype=jnp.int32)
     inside = (index[:, None] >= starts[None, :]) & (index[:, None] < ends[None, :])

time: 3960 us -> 3960 us (level)
  no operation moved by 1% of the time
where the time goes in v1:
time: 3960 us; the launch traced here: 3950 us
  waiting for transfers between devices  3160 us (80%)
  blocking collectives  317 us (8%)
  matrix products  211 us (5%)
  local copies, waits for them, and re-layouts  100 us (3%)
  other arithmetic  96.2 us (2%)
  starting transfers between devices  45.6 us (1%)
    reduce_scatter x1, waiting for transfers between devices, on_device(): lax.psum_scatter(owned_ffn[2], 'dp', scatter_dimension=0, tiled=True)  688 us
    reduce_scatter x1, waiting for transfers between devices, on_device(): lax.psum_scatter(owned_ffn[3], 'dp', scatter_dimension=1, tiled=True)  688 us
    reduce_scatter x1, waiting for transfers between devices, on_device(): lax.psum_scatter(owned_ffn[1], 'dp', scatter_dimension=0, tiled=True)  686 us
    all_gather x1, waiting for transfers between devices, fetch_ffn(): lax.all_gather(w_down.astype(jnp.bfloat16), 'dp', axis=1, tiled=True)  237 us
    all_gather x1, waiting for transfers between devices, fetch_ffn(): lax.all_gather(w_gate.astype(jnp.bfloat16), 'dp', axis=0, tiled=True)  179 us
    reduce_scatter x1, waiting for transfers between devices, on_device(): lax.psum_scatter(grad_wo, 'dp', scatter_dimension=1, tiled=True)  179 us
    reduce_scatter x1, waiting for transfers between devices, on_device(): lax.psum_scatter(grad_wq, 'dp', scatter_dimension=0, tiled=True)  164 us
    all_gather x1, waiting for transfers between devices, fetch_ffn(): lax.all_gather(w_up.astype(jnp.bfloat16), 'dp', axis=0, tiled=True)  138 us
  transfers between devices with their start and end apart: 21, of which 13 were waited for; matrix products, arithmetic and copies ran while one was open for 7% of the time, Pallas kernels for 0%

profile of v1, /device:TPU:0, one launch (start us, length us, event | category | flops | bytes accessed | tf_op | source)
XLA Modules:
  0.0 3951.0 jit_solution(15310072413473392963)
XLA Ops:
  13.4 30.5 scatter_custom_fusion
  43.9 3.8 sort.59
  51.6 8.5 all-to-all-start
  61.9 74.5 %all-gather = bf16[16,1,128]{2,1,0:T(2,128)(2,1)S(1)} all-gather(bf16[1,1,128]{2,1,0:T(2,128)(2,1)S(1)} %convert_bitcast_fusion.1), channel_id=1, replica_groups=mesh['dp'=16,'mp'=2] {'dp'}, dimensions={0}, use_global_device_ids=true | all-gather | bytes 4352 | tf_op jit(solution)/shard_map/all_gather | solution.py:86
  137.2 3.8 sort.60
  141.0 3.8 sort.61
  162.5 3.8 convolution_convert_fusion.1
  166.3 74.2 %all-gather.14.cloned.1.call-done = bf16[2048,1024]{1,0:T(8,128)(2,1)} async-done(((bf16[128,1024]{1,0:T(8,128)(2,1)}), bf16[2048,1024]{1,0:T(8,128)(2,1)}) %all-gather.14.cloned.1.call-update) | async-done | bytes 4194320 | tf_op jit(solution)/shard_map/all_gather | solution.py:87
  240.5 5.9 fusion.51
  253.3 78.2 %all-gather.16.cloned.1.call-done = bf16[1024,2048]{1,0:T(8,128)(2,1)} async-done(((bf16[1024,128]{1,0:T(8,128)(2,1)}), bf16[1024,2048]{1,0:T(8,128)(2,1)}) %all-gather.16.cloned.1.call-update) | async-done | bytes 4194320 | tf_op jit(solution)/shard_map/all_gather | solution.py:90
  331.5 6.5 fusion.59
  350.6 3.9 all-to-all-start.2
  354.5 77.4 %all-gather.1 = bf16[16,1,128]{2,1,0:T(2,128)(2,1)S(1)} all-gather(bf16[1,1,128]{2,1,0:T(2,128)(2,1)S(1)} %convert_bitcast_fusion), channel_id=1, replica_groups=mesh['dp'=16,'mp'=2] {'dp'}, dimensions={0}, use_global_device_ids=true | all-gather | bytes 4352 | tf_op jit(solution)/shard_map/all_gather | solution.py:96
  441.2 138.1 %all-gather.20.cloned.1.call-done = bf16[2048,4096]{1,0:T(8,128)(2,1)} async-done(((bf16[128,4096]{1,0:T(8,128)(2,1)}), bf16[2048,4096]{1,0:T(8,128)(2,1)}) %all-gather.20.cloned.1.call-update) | async-done | bytes 16777232 | tf_op jit(solution)/shard_map/all_gather | solution.py:98
  579.3 14.3 fusion.61
  593.6 179.2 %all-gather.18.cloned.1.call-done = bf16[2048,4096]{1,0:T(8,128)(2,1)} async-done(((bf16[128,4096]{1,0:T(8,128)(2,1)}), bf16[2048,4096]{1,0:T(8,128)(2,1)}) %all-gather.18.cloned.1.call-update) | async-done | bytes 16777232 | tf_op jit(solution)/shard_map/all_gather | solution.py:97
  772.9 14.9 fusion.60
  787.8 236.6 %all-gather.22.cloned.1.call-done = bf16[4096,2048]{1,0:T(8,128)(2,1)} async-done(((bf16[4096,128]{1,0:T(8,128)(2,1)}), bf16[4096,2048]{1,0:T(8,128)(2,1)}) %all-gather.22.cloned.1.call-update) | async-done | bytes 16777232 | tf_op jit(solution)/shard_map/all_gather | solution.py:99
  1024.4 21.1 multiply_convert_fusion
  1045.5 16.5 fusion.63
  1062.0 14.5 convolution_add_fusion
  1076.5 15.7 fusion.62
  1092.3 11.0 all-reduce.10.cloned.1.call-done
  1103.3 4.6 multiply_reduce_fusion
  1115.5 3.9 fusion.28
  1151.5 6.6 fusion.49
  1159.4 7.8 fusion.31
  1169.1 19.0 fusion.66
  1188.4 17.6 fusion.67
  1207.6 17.6 fusion.68
  1225.9 4.1 add_convert_fusion
  1233.4 7.1 all-to-all-start.1
  1240.5 4.1 fusion.11
  1245.3 4.7 fusion.10
  1249.9 7.1 gather_fusion.7
  1257.0 34.8 all-to-all-done.1
  1293.1 24.6 all-to-all-start.3
  1317.8 3.8 sort.62
  1322.8 119.9 %all-reduce.2 = (f32[2048]{0:T(1024)S(1)}, f32[2048]{0:T(1024)S(1)}) all-reduce(f32[2048]{0:T(1024)S(1)} %get-tuple-element.31, f32[2048]{0:T(1024)S(1)} %get-tuple-element.29), channel_id=2, replica_groups=mesh['dp'=16,'mp'=2] {'dp'}, use_global_device_ids=true, to_apply=%region_20.21.clone | all-reduce | flops 4096 | bytes 32768
  1448.7 7.1 gather_fusion.4
  1455.8 164.1 %reduce-scatter.8.cloned.1.call-done = f32[128,1024]{1,0:T(8,128)} async-done(((f32[2048,1024]{1,0:T(8,128)}), f32[128,1024]{1,0:T(8,128)}) %reduce-scatter.8.cloned.1.call-update) | async-done | bytes 524304 | tf_op jit(solution)/shard_map/reduce_scatter | solution.py:263
  1623.5 178.7 %reduce-scatter.14.cloned.1.call-done = f32[1024,128]{1,0:T(8,128)} async-done(((f32[1024,2048]{1,0:T(8,128)}), f32[1024,128]{1,0:T(8,128)}) %reduce-scatter.14.cloned.1.call-update) | async-done | bytes 524304 | tf_op jit(solution)/shard_map/reduce_scatter | solution.py:266
  1804.7 685.6 %reduce-scatter.16.cloned.1.call-done = f32[128,4096]{1,0:T(8,128)} async-done(((f32[2048,4096]{1,0:T(8,128)}), f32[128,4096]{1,0:T(8,128)}) %reduce-scatter.16.cloned.1.call-update) | async-done | bytes 2097168 | tf_op jit(solution)/shard_map/reduce_scatter | solution.py:268
  2493.7 687.9 %reduce-scatter.18.cloned.1.call-done = f32[128,4096]{1,0:T(8,128)} async-done(((f32[2048,4096]{1,0:T(8,128)}), f32[128,4096]{1,0:T(8,128)}) %reduce-scatter.18.cloned.1.call-update) | async-done | bytes 2097168 | tf_op jit(solution)/shard_map/reduce_scatter | solution.py:269
  3185.0 687.9 %reduce-scatter.20.cloned.1.call-done = f32[4096,128]{1,0:T(8,128)} async-done(((f32[4096,2048]{1,0:T(8,128)}), f32[4096,128]{1,0:T(8,128)}) %reduce-scatter.20.cloned.1.call-update) | async-done | bytes 2097168 | tf_op jit(solution)/shard_map/reduce_scatter | solution.py:270
  3879.7 44.7 %psum.39 = f32[]{:T(128)} all-reduce(f32[]{:T(128)S(6)} %add.240), channel_id=1, replica_groups=mesh['dp'=16,'mp'=2] {'dp','mp'}, use_global_device_ids=true, to_apply=%region_39.40 | all-reduce | flops 1 | bytes 8 | tf_op jit(solution)/shard_map/psum | solution.py:286
  3930.6 4.5 multiply_subtract_fusion
  3937.2 5.6 multiply_subtract_fusion.1
  (297 shorter events, 136.9 us)
Async XLA Ops:
  7.2 41.1 %copy-start = (bf16[512,2048]{1,0:T(8,128)(2,1)S(1)}, bf16[512,2048]{1,0:T(8,128)(2,1)}, u32[]{:S(2)}) copy-start(bf16[512,2048]{1,0:T(8,128)(2,1)} %param.23) | copy-start | bytes 6291460
  7.2 145.1 %all-gather.12.cloned.1.call-start = ((), (), s32[]{:S(2)}) async-start(), calls=%async_computation.12 | async-start | bytes 2228224 | tf_op jit(solution)/shard_map/all_gather | solution.py:88
  9.0 153.5 %all-gather.10.cloned.1.call-start = ((), (), s32[]{:S(2)}) async-start(), calls=%async_computation.11 | async-start | bytes 2228224 | tf_op jit(solution)/shard_map/all_gather | solution.py:89
  10.7 229.8 %all-gather.14.cloned.1.call-start = ((), (), s32[]{:S(2)}) async-start(), calls=%async_computation.13 | async-start | bytes 4456448 | tf_op jit(solution)/shard_map/all_gather | solution.py:87
  51.6 8.5 copy-start.36
  51.6 9.3 copy-start.75
  51.6 9.4 copy-start.2
  51.6 10.3 copy-start.68
  51.6 95.1 %all-to-all-start = ((bf16[16,32,2048]{2,1,0:T(8,128)(2,1)}), bf16[16,32,2048]{2,1,0:T(8,128)(2,1)S(1)}, u32[]{:S(2)}, u32[]{:S(2)}) async-start(bf16[16,32,2048]{2,1,0:T(8,128)(2,1)} %bitcast.122), calls=%async_computation | async-start | bytes 4194304 | tf_op jit(solution)/shard_map/all_to_all | solution.py:151
  60.1 271.4 %all-gather.16.cloned.1.call-start = ((), (), s32[]{:S(2)}) async-start(), calls=%async_computation.14 | async-start | bytes 4456448 | tf_op jit(solution)/shard_map/all_gather | solution.py:90
  60.9 374.4 %all-reduce.8.cloned.1.call-start = ((), (), s32[]{:S(2)}) async-start(), calls=%async_computation.15 | async-start | bytes 8388608 | tf_op jit(solution)/shard_map/psum | solution.py:81
  136.4 104.1 %copy-start.51 = (f32[16,1,128]{2,1,0:T(1,128)}, f32[16,1,128]{2,1,0:T(1,128)S(1)}, u32[]{:S(2)}) copy-start(f32[16,1,128]{2,1,0:T(1,128)S(1)} %convert_element_type.151) | copy-start | bytes 24580
  146.7 102.0 %copy-start.26 = (f32[512,128]{1,0:T(8,128)}, f32[512,128]{1,0:T(8,128)S(1)}, u32[]{:S(2)}) copy-start(f32[512,128]{1,0:T(8,128)S(1)} %get-tuple-element.74) | copy-start | bytes 786436
  146.7 102.0 %copy-start.28 = (f32[512,128]{1,0:T(8,128)}, f32[512,128]{1,0:T(8,128)S(1)}, u32[]{:S(2)}) copy-start(f32[512,128]{1,0:T(8,128)S(1)} %get-tuple-element.75) | copy-start | bytes 786436
  152.3 88.2 %copy-start.62 = (f32[512]{0:T(512)}, f32[512]{0:T(512)S(1)}, u32[]{:S(2)}) copy-start(f32[512]{0:T(512)S(1)} %add_rsqrt_fusion.1) | copy-start | bytes 6148
  162.2 87.2 %copy-start.43 = (bf16[512,2,128]{2,0,1:T(8,128)(2,1)}, bf16[512,2,128]{2,0,1:T(8,128)(2,1)S(1)}, u32[]{:S(2)}) copy-start(bf16[512,2,128]{2,0,1:T(8,128)(2,1)S(1)} %get-tuple-element.70) | copy-start | bytes 786436
  253.3 78.2 %copy-start.30 = (bf16[2,256,2,512]{3,1,2,0:T(8,128)(2,1)}, bf16[2,256,2,512]{3,1,2,0:T(8,128)(2,1)S(1)}, u32[]{:S(2)}) copy-start(bf16[2,256,2,512]{3,1,2,0:T(8,128)(2,1)S(1)} %fusion.22) | copy-start | bytes 3145732
  338.0 241.3 %all-gather.20.cloned.1.call-start = ((), (), s32[]{:S(2)}) async-start(), calls=%async_computation.17 | async-start | bytes 17825792 | tf_op jit(solution)/shard_map/all_gather | solution.py:98
  340.7 432.1 %all-gather.18.cloned.1.call-start = ((), (), s32[]{:S(2)}) async-start(), calls=%async_computation.16 | async-start | bytes 17825792 | tf_op jit(solution)/shard_map/all_gather | solution.py:97
  343.9 680.5 %all-gather.22.cloned.1.call-start = ((), (), s32[]{:S(2)}) async-start(), calls=%async_computation.18 | async-start | bytes 17825792 | tf_op jit(solution)/shard_map/all_gather | solution.py:99
  350.6 81.3 %all-to-all-start.2 = ((bf16[16,32,2048]{2,1,0:T(8,128)(2,1)}), bf16[16,32,2048]{2,1,0:T(8,128)(2,1)S(1)}, u32[]{:S(2)}, u32[]{:S(2)}) async-start(bf16[16,32,2048]{2,1,0:T(8,128)(2,1)} %bitcast.124), calls=%async_computation.2 | async-start | bytes 4194304 | tf_op jit(solution)/shard_map/all_to_all | solution.py:152
  354.5 748.8 %all-reduce.10.cloned.1.call-start = ((), (), s32[]{:S(2)}) async-start(), calls=%async_computation.19 | async-start | bytes 8388608 | tf_op jit(solution)/shard_map/psum | solution.py:81
  441.2 138.1 %copy-start.34 = (bf16[512,2048]{1,0:T(8,128)(2,1)}, bf16[512,2048]{1,0:T(8,128)(2,1)S(1)}, u32[]{:S(2)}) copy-start(bf16[512,2048]{1,0:T(8,128)(2,1)S(1)} %multiply_convert_fusion.3) | copy-start | bytes 6291460
  593.6 430.7 %copy-start.24 = (bf16[512,2048]{1,0:T(8,128)(2,1)S(1)}, bf16[512,2048]{1,0:T(8,128)(2,1)}, u32[]{:S(2)}) copy-start(bf16[512,2048]{1,0:T(8,128)(2,1)} %gather_fusion.6) | copy-start | bytes 6291460
  1045.5 16.5 copy-start.77
  1076.5 149.5 %all-reduce.12.cloned.1.call-start = ((), (), s32[]{:S(2)}) async-start(), calls=%async_computation.27 | async-start | bytes 16777216 | tf_op jit(solution)/shard_map/psum | solution.py:81
  1141.5 303.9 %reduce-scatter.12.cloned.1.call-start = ((), (), s32[]{:S(2)}) async-start(), calls=%async_computation.22 | async-start | bytes 4456448 | tf_op jit(solution)/shard_map/reduce_scatter | solution.py:265
  1146.6 300.4 %reduce-scatter.10.cloned.1.call-start = ((), (), s32[]{:S(2)}) async-start(), calls=%async_computation.21 | async-start | bytes 4456448 | tf_op jit(solution)/shard_map/reduce_scatter | solution.py:264
  1150.2 469.6 %reduce-scatter.8.cloned.1.call-start = ((), (), s32[]{:S(2)}) async-start(), calls=%async_computation.20 | async-start | bytes 8912896 | tf_op jit(solution)/shard_map/reduce_scatter | solution.py:263
  1158.1 644.1 %reduce-scatter.14.cloned.1.call-start = ((), (), s32[]{:S(2)}) async-start(), calls=%async_computation.23 | async-start | bytes 8912896 | tf_op jit(solution)/shard_map/reduce_scatter | solution.py:266
  1167.2 1323.1 %reduce-scatter.16.cloned.1.call-start = ((), (), s32[]{:S(2)}) async-start(), calls=%async_computation.24 | async-start | bytes 35651584 | tf_op jit(solution)/shard_map/reduce_scatter | solution.py:268
  1188.1 1993.5 %reduce-scatter.18.cloned.1.call-start = ((), (), s32[]{:S(2)}) async-start(), calls=%async_computation.25 | async-start | bytes 35651584 | tf_op jit(solution)/shard_map/reduce_scatter | solution.py:269
  1206.0 2666.9 %reduce-scatter.20.cloned.1.call-start = ((), (), s32[]{:S(2)}) async-start(), calls=%async_computation.26 | async-start | bytes 35651584 | tf_op jit(solution)/shard_map/reduce_scatter | solution.py:270
  1233.4 58.4 %all-to-all-start.1 = ((bf16[16,32,2048]{2,1,0:T(8,128)(2,1)}), bf16[16,32,2048]{2,1,0:T(8,128)(2,1)S(1)}, u32[]{:S(2)}, u32[]{:S(2)}) async-start(bf16[16,32,2048]{2,1,0:T(8,128)(2,1)} %bitcast.123), calls=%async_computation.1 | async-start | bytes 4194304 | tf_op jit(solution)/shard_map/all_to_all | solution.py:273
  1257.0 60.7 %copy-start.65 = (s32[512]{0:T(512)S(1)}, s32[512]{0:T(512)}, u32[]{:S(2)}) copy-start(s32[512]{0:T(512)} %copy-done.64) | copy-start | bytes 6148
  1257.0 64.5 %copy-start.76 = (u32[32]{0:T(128)S(1)}, u32[32]{0:T(128)}, u32[]{:S(2)}) copy-start(u32[32]{0:T(128)} %constant.23) | copy-start | bytes 388
  1293.1 2583.2 %all-to-all-start.3 = ((bf16[16,32,2048]{2,1,0:T(8,128)(2,1)}), bf16[16,32,2048]{2,1,0:T(8,128)(2,1)S(1)}, u32[]{:S(2)}, u32[]{:S(2)}) async-start(bf16[16,32,2048]{2,1,0:T(8,128)(2,1)} %bitcast.121), calls=%async_computation.3 | async-start | bytes 4194304 | tf_op jit(solution)/shard_map/all_to_all | solution.py:276
  3876.3 48.8 %copy-start.69 = (f32[128]{0:T(128)S(1)}, f32[128]{0:T(128)}, u32[]{:S(2)}) copy-start(f32[128]{0:T(128)} %param.28) | copy-start | bytes 1540
  3876.3 48.8 %copy-start.71 = (f32[128]{0:T(128)S(1)}, f32[128]{0:T(128)}, u32[]{:S(2)}) copy-start(f32[128]{0:T(128)} %param.33) | copy-start | bytes 1540
  3876.3 48.8 %copy-start.72 = (f32[128]{0:T(128)S(1)}, f32[128]{0:T(128)}, u32[]{:S(2)}) copy-start(f32[128]{0:T(128)} %param.42) | copy-start | bytes 1540
  3876.4 48.8 %copy-start.73 = (f32[128]{0:T(128)S(1)}, f32[128]{0:T(128)}, u32[]{:S(2)}) copy-start(f32[128]{0:T(128)} %param.37) | copy-start | bytes 1540
  3876.4 49.4 %copy-start.37 = (f32[1024,128]{1,0:T(8,128)S(1)}, f32[1024,128]{1,0:T(8,128)}, u32[]{:S(2)}) copy-start(f32[1024,128]{1,0:T(8,128)} %param.32) | copy-start | bytes 1572868
  3876.4 51.7 %copy-start.38 = (f32[128,1024]{1,0:T(8,128)S(1)}, f32[128,1024]{1,0:T(8,128)}, u32[]{:S(2)}) copy-start(f32[128,1024]{1,0:T(8,128)} %param.29) | copy-start | bytes 1572868
  3876.4 58.8 %copy-start.47 = (f32[128,512]{1,0:T(8,128)S(1)}, f32[128,512]{1,0:T(8,128)}, u32[]{:S(2)}) copy-start(f32[128,512]{1,0:T(8,128)} %param.30) | copy-start | bytes 786436
  3879.7 50.9 %copy-start.22 = (f32[4096,128]{1,0:T(8,128)S(1)}, f32[4096,128]{1,0:T(8,128)}, u32[]{:S(2)}) copy-start(f32[4096,128]{1,0:T(8,128)} %param.36) | copy-start | bytes 6291460
  3928.1 7.1 copy-start.49
  3928.1 7.1 copy-start.50
  3928.1 7.1 copy-start.60
  (51 other events, 162.9 us)
Sparse Core Ops, SparseCore 0:
  11.4 79.1 all-gather.11
  93.9 68.5 all-gather.9
  165.8 74.6 all-gather.13
  243.6 87.7 all-gather.15
  338.2 26.6 all-reduce.7
  368.4 210.8 all-gather.19
  583.0 189.7 all-gather.17
  776.5 247.8 all-gather.21
  1076.6 26.6 all-reduce.9
  1141.7 40.0 all-reduce.11
  1184.1 122.4 reduce-scatter.11
  1308.7 126.2 reduce-scatter.9
  1437.3 182.4 reduce-scatter.7
  1622.0 180.2 reduce-scatter.13
  1804.4 685.8 reduce-scatter.15
  2492.5 689.0 reduce-scatter.17
  3183.8 689.0 reduce-scatter.19

commit v2 on v1

v2 whole, which is shorter than its diff:
```python
import math

import jax
import jax.numpy as jnp
from jax import lax
from jax.sharding import Mesh
from jax.sharding import PartitionSpec as P

HEAD_SIZE = 256
PARAMS = 62918656
EPS = 1e-06
THETA = 1000042.0
LEARN = 0.5
DECAY = 0.1
GROUP = 4
BF = jnp.bfloat16
F32 = jnp.float32


def angles(position, head):
    half = head // 2
    freq = THETA ** (-(2.0 * jnp.arange(half, dtype=F32)) / head)
    turned = position[:, None] * freq[None, :]
    return (jnp.cos(turned)[:, None, :], jnp.sin(turned)[:, None, :])


def apply_rotary(value, cosine, sine):
    half = value.shape[-1] // 2
    first, second = value[..., :half], value[..., half:]
    return jnp.concatenate(
        [first * cosine - second * sine, second * cosine + first * sine], axis=-1
    )


def unrotate(grads, cosine, sine):
    half = grads.shape[-1] // 2
    first, second = grads[..., :half], grads[..., half:]
    return jnp.concatenate(
        [first * cosine + second * sine, second * cosine - first * sine], axis=-1
    )


def layout(block_len, rows):
    rank = jnp.arange(block_len.shape[0], dtype=jnp.int32)
    ends = jnp.sum(jnp.where(rank[None, :] <= rank[:, None], block_len[None, :], 0), axis=1)
    starts = ends - block_len
    index = jnp.arange(rows, dtype=jnp.int32)
    inside = (index[:, None] >= starts[None, :]) & (index[:, None] < ends[None, :])
    segment = jnp.sum(jnp.where(inside, rank[None, :], 0), axis=1)
    position = jnp.sum(jnp.where(inside, index[:, None] - starts[None, :], 0), axis=1)
    mask = (segment[:, None] == segment[None, :]) & (index[None, :] <= index[:, None])
    return (position.astype(F32), mask)


def normalize(value):
    scale_inv = lax.rsqrt(jnp.mean(value * value, axis=-1, keepdims=True) + EPS)
    return (value * scale_inv, scale_inv)


def norm_back(grad_normed, normed, scale_inv, gain):
    scaled = grad_normed * gain
    return scale_inv * (scaled - normed * jnp.mean(scaled * normed, axis=-1, keepdims=True))


def mat_nn(left, right):
    return jnp.dot(left, right, preferred_element_type=F32)


def mat_nt(left, right):
    return lax.dot_general(left, right, (((1,), (1,)), ((), ())), preferred_element_type=F32)


def mat_tn(left, right):
    return lax.dot_general(left, right, (((0,), (0,)), ((), ())), preferred_element_type=F32)


def after(value, *others):
    return lax.optimization_barrier((value, *others))[0]


class Ways:
    def __init__(self):
        self.depth = lax.axis_size("line")
        self.n = self.depth * GROUP
        self.z = lax.axis_index("line")
        self.p = lax.axis_index("group")
        self.me = self.z * GROUP + self.p
        self.core = lax.axis_index("mp")

    def flip(self, value, k):
        return lax.ppermute(value, "group", [(i, i ^ k) for i in range(GROUP)])

    def swap(self, value):
        return lax.ppermute(value, "mp", [(0, 1), (1, 0)])

    def gather_line(self, value):
        return lax.all_gather(value, "line", axis=0, tiled=True)

    def scatter_line(self, whole):
        return lax.psum_scatter(
            whole.astype(BF), "line", scatter_dimension=0, tiled=True
        ).astype(F32)

    def gather_group(self, value):
        half = value.shape[0] // 2
        one, two = self.flip(value, 1), self.flip(value, 2)
        three = jnp.concatenate([self.flip(one[:half], 2), self.flip(two[half:], 1)])
        return [value, one, two, three]

    def scatter_group(self, parts):
        half = parts[0].shape[0] // 2
        first = self.flip(parts[3][:half].astype(BF), 2).astype(F32)
        second = self.flip(parts[3][half:].astype(BF), 1).astype(F32)
        one = jnp.concatenate([parts[1][:half] + first, parts[1][half:]]).astype(BF)
        two = jnp.concatenate([parts[2][:half], parts[2][half:] + second]).astype(BF)
        return parts[0] + self.flip(one, 1).astype(F32) + self.flip(two, 2).astype(F32)

    def spread_units(self, shards):
        rows, units = shards[0].shape[0], shards[0].shape[1] // GROUP
        send = jnp.stack(
            [
                jnp.concatenate([s[:, j * units : (j + 1) * units] for s in shards])
                for j in range(GROUP)
            ]
        )
        got = lax.all_to_all(send, "group", split_axis=0, concat_axis=0, tiled=True)
        return got.reshape(GROUP, len(shards), rows, units).swapaxes(0, 1).reshape(
            len(shards), GROUP * rows, units
        )

    def collect_units(self, whole):
        rows = whole.shape[0] // GROUP
        got = lax.all_to_all(
            whole.astype(BF), "group", split_axis=0, concat_axis=0, tiled=True
        ).astype(F32)
        return jnp.concatenate([got[j * rows : (j + 1) * rows] for j in range(GROUP)], axis=1)

    def exchange(self, value):
        return lax.all_to_all(value, ("line", "group"), split_axis=0, concat_axis=0, tiled=True)

    def own_half(self, value):
        half = value.shape[-1] // 2
        return jnp.where(self.core == 0, value[..., :half], value[..., half:])

    def other_half(self, value):
        half = value.shape[-1] // 2
        return jnp.where(self.core == 0, value[..., half:], value[..., :half])

    def join(self, mine, other):
        return jnp.where(
            self.core == 0,
            jnp.concatenate([mine, other], axis=-1),
            jnp.concatenate([other, mine], axis=-1),
        )


def deal_tables(token_order, me, rows):
    blocks = token_order.shape[0] // rows
    per = rows // blocks
    index = jnp.arange(rows, dtype=jnp.int32)
    wanted = lax.dynamic_slice_in_dim(token_order, me * rows, rows)
    source = wanted // rows
    same = (source[:, None] == source[None, :]) & (index[None, :] < index[:, None])
    slot = source * per + jnp.sum(same.astype(jnp.int32), axis=1)
    into = (slot[:, None] == index[None, :]).astype(BF)
    table = token_order.reshape(blocks, rows)
    taken = table // rows == me
    earlier = (index[:, None] < index[None, :]).astype(BF)
    rank = mat_nn(taken.astype(BF), earlier).astype(jnp.int32)
    hit = taken[:, None, :] & (rank[:, None, :] == jnp.arange(per, dtype=jnp.int32)[None, :, None])
    sent = jnp.sum(jnp.where(hit, (table - me * rows)[:, None, :], 0), axis=2).reshape(rows)
    out = (sent[:, None] == index[None, :]).astype(BF)
    return into, out


def on_device(
    tokens,
    cotangent,
    lengths,
    seq_deal,
    token_order,
    gain_attn,
    w_query,
    key_weight,
    value_weight,
    w_out,
    gain_ffn,
    w_gate,
    w_up,
    w_down,
    moment_gain_attn,
    moment_w_query,
    key_weight_momentum,
    value_weight_momentum,
    moment_w_out,
    moment_gain_ffn,
    moment_w_gate,
    moment_w_up,
    moment_w_down,
):
    ways = Ways()
    rows, width = tokens.shape
    me = ways.me
    shard_qkv = jnp.concatenate(
        [w_query.astype(BF), key_weight.astype(BF), value_weight.astype(BF)], axis=1
    )
    shard_out = w_out.astype(BF).T
    line_all = ways.gather_line(jnp.concatenate([shard_qkv, shard_out], axis=1))
    line_qkv = line_all[:, : shard_qkv.shape[1]]
    line_out = line_all[:, shard_qkv.shape[1] :]

    def natural(line):
        count, cols = ways.depth, line.shape[1]
        each = line.shape[0] // count
        whole = jnp.zeros((count, GROUP, each, cols), line.dtype)
        for k, part in enumerate(ways.gather_group(line)):
            whole = lax.dynamic_update_slice(
                whole, part.reshape(count, 1, each, cols), (0, ways.p ^ k, 0, 0)
            )
        return whole.reshape(count * GROUP * each, cols)

    into, out = deal_tables(token_order, me, rows)
    sent_tokens = mat_nn(out, ways.own_half(tokens)).astype(BF)
    sent_cot = mat_nn(out, ways.own_half(cotangent)).astype(BF)
    gains = jnp.stack([gain_attn, gain_ffn]).astype(BF)
    all_gains = ways.exchange(
        jnp.broadcast_to(gains[None], (ways.n, 2, gains.shape[1]))
    ).astype(F32)
    gain_a = all_gains[:, 0].reshape(width)
    gain_f = all_gains[:, 1].reshape(width)
    half_tokens = mat_nn(into, ways.exchange(sent_tokens)).astype(BF)
    dealt = ways.join(half_tokens, ways.swap(half_tokens))
    weight_qkv = natural(line_qkv)
    weight_out = natural(after(line_out, weight_qkv))
    half_cot = mat_nn(into, ways.exchange(after(sent_cot, weight_qkv))).astype(BF)
    wide_q = w_query.shape[1]
    wide_k = key_weight.shape[1]
    query_w = weight_qkv[:, :wide_q]
    key_w = weight_qkv[:, wide_q : wide_q + wide_k]
    value_w = weight_qkv[:, wide_q + wide_k :]

    units = ways.spread_units([w_down.astype(BF).T, w_gate.astype(BF), w_up.astype(BF)])
    line_units = lax.all_gather(units, "line", axis=1, tiled=False)
    down_t, gate_w, up_w = (line_units[i].reshape(width, -1) for i in range(3))

    cot_parts = jnp.concatenate(ways.gather_group(after(half_cot, weight_out)))
    group_cot = ways.join(cot_parts, ways.swap(cot_parts))
    dealt_cot = group_cot[:rows]

    seq_dev = seq_deal.shape[0] // ways.n
    mine = lax.dynamic_slice_in_dim(seq_deal, me * seq_dev, seq_dev)
    position, mask = layout(lengths[mine], rows)
    cosine, sine = angles(position, HEAD_SIZE)

    heads_q = query_w.shape[1] // HEAD_SIZE
    heads_kv = key_w.shape[1] // HEAD_SIZE
    head_group = heads_q // heads_kv
    root = HEAD_SIZE ** (-0.5)
    inputs = dealt.astype(F32)
    normed1, scale1 = normalize(inputs)
    hidden1 = (normed1 * gain_a).astype(BF)
    query = mat_nn(hidden1, query_w).reshape(rows, heads_q, HEAD_SIZE)
    key = mat_nn(hidden1, key_w).reshape(rows, heads_kv, HEAD_SIZE)
    value = mat_nn(hidden1, value_w).astype(BF).reshape(rows, heads_kv, HEAD_SIZE)
    query_rot = (
        apply_rotary(query, cosine, sine)
        .astype(BF)
        .reshape(rows, heads_kv, head_group, HEAD_SIZE)
    )
    key_rot = apply_rotary(key, cosine, sine).astype(BF)
    scores = jnp.einsum("rhgd,chd->hgrc", query_rot, key_rot, preferred_element_type=F32) * root
    scores = jnp.where(mask[None, None], scores, -1e30)
    top = jnp.max(scores, axis=-1, keepdims=True)
    expo = jnp.exp(scores - top)
    prob = expo / jnp.sum(expo, axis=-1, keepdims=True)
    prob_low = prob.astype(BF)
    mixed = (
        jnp.einsum("hgrc,chd->rhgd", prob_low, value, preferred_element_type=F32)
        .reshape(rows, heads_q * HEAD_SIZE)
        .astype(BF)
    )
    part = mat_nt(mixed, weight_out)
    middle = inputs + (part + ways.swap(part.astype(BF)).astype(F32))
    normed2, scale2 = normalize(middle)
    hidden2 = (normed2 * gain_f).astype(BF)

    parts = jnp.concatenate(ways.gather_group(ways.own_half(hidden2)))
    group_h2 = ways.join(parts, ways.swap(parts))
    grad_inner = mat_nn(group_cot, down_t)
    gate = mat_nn(group_h2, gate_w)
    upper = mat_nn(group_h2, up_w)
    sigma = jax.nn.sigmoid(gate)
    activ = gate * sigma
    inner = (activ * upper).astype(BF)
    grad_gate = (grad_inner * upper * (sigma * (1.0 + gate * (1.0 - sigma)))).astype(BF)
    grad_up = (grad_inner * activ).astype(BF)

    def token_sum(terms):
        other = ways.swap(ways.other_half(terms).astype(BF)).astype(F32)
        whole = ways.own_half(terms) + other
        return ways.scatter_group([whole[k * rows : (k + 1) * rows] for k in range(GROUP)])

    half_dh2 = token_sum(mat_nt(grad_gate, gate_w) + mat_nt(grad_up, up_w))
    sum_wd = ways.scatter_line(mat_tn(group_cot, inner))
    sum_wg = ways.scatter_line(mat_tn(group_h2, grad_gate))
    sum_wu = ways.scatter_line(mat_tn(group_h2, grad_up))
    half_result = ways.own_half(middle) + token_sum(mat_nt(inner, down_t))

    def give_back(half):
        slots = mat_tn(into, half.astype(BF)).astype(BF)
        back = mat_tn(out, ways.exchange(slots)).astype(BF)
        return ways.join(back, ways.swap(back))

    activations = give_back(half_result)

    grad_h2 = ways.join(half_dh2, ways.swap(half_dh2))
    grad_gf = jnp.sum(grad_h2 * normed2, axis=0)
    grad_mid = dealt_cot.astype(F32) + norm_back(grad_h2, normed2, scale2, gain_f)
    mid_low = grad_mid.astype(BF)

    grad_mixed = (
        mat_nn(mid_low, weight_out).astype(BF).reshape(rows, heads_kv, head_group, HEAD_SIZE)
    )
    grad_wo = mat_tn(mid_low, mixed)
    grad_prob = jnp.einsum("rhgd,chd->hgrc", grad_mixed, value, preferred_element_type=F32)
    delta = jnp.sum(prob * grad_prob, axis=-1, keepdims=True)
    grad_scores = (prob * (grad_prob - delta)).astype(BF)
    grad_qrot = (
        jnp.einsum("hgrc,chd->rhgd", grad_scores, key_rot, preferred_element_type=F32) * root
    )
    grad_krot = (
        jnp.einsum("hgrc,rhgd->chd", grad_scores, query_rot, preferred_element_type=F32) * root
    )
    grad_value = jnp.einsum("hgrc,rhgd->chd", prob_low, grad_mixed, preferred_element_type=F32)
    grad_q = (
        unrotate(grad_qrot.reshape(rows, heads_q, HEAD_SIZE), cosine, sine)
        .reshape(rows, heads_q * HEAD_SIZE)
        .astype(BF)
    )
    grad_k = unrotate(grad_krot, cosine, sine).reshape(rows, heads_kv * HEAD_SIZE).astype(BF)
    grad_v = grad_value.reshape(rows, heads_kv * HEAD_SIZE).astype(BF)

    def attention_sum(terms):
        count, cols = ways.depth, terms.shape[1]
        each = terms.shape[0] // (count * GROUP)
        view = terms.reshape(count, GROUP, each, cols)
        parts = [
            lax.dynamic_slice(
                view, (0, ways.p ^ k, 0, 0), (count, 1, each, cols)
            ).reshape(count * each, cols)
            for k in range(GROUP)
        ]
        return ways.scatter_line(ways.scatter_group(parts))

    sum_wo = attention_sum(grad_wo)
    grad_qkv = jnp.concatenate([grad_q, grad_k, grad_v], axis=1)
    sum_qkv = attention_sum(mat_tn(hidden1, grad_qkv))
    part = mat_nt(grad_qkv, weight_qkv)
    grad_h1 = part + ways.swap(part.astype(BF)).astype(F32)
    grad_ga = jnp.sum(grad_h1 * normed1, axis=0)
    grad_in = grad_mid + norm_back(grad_h1, normed1, scale1, gain_a)
    input_grad = give_back(ways.own_half(grad_in))

    gain_grads = jnp.sum(
        ways.exchange(jnp.stack([grad_ga, grad_gf]).reshape(2, ways.n, -1).swapaxes(0, 1)), axis=0
    )
    owned = (
        gain_grads[0],
        sum_qkv[:, :wide_q],
        sum_qkv[:, wide_q : wide_q + wide_k],
        sum_qkv[:, wide_q + wide_k :],
        sum_wo.T,
        gain_grads[1],
        ways.collect_units(sum_wg),
        ways.collect_units(sum_wu),
        ways.collect_units(sum_wd).T,
    )
    share = 0.5 * (jnp.sum(owned[0] * owned[0]) + jnp.sum(owned[5] * owned[5]))
    for k in (1, 2, 3, 4, 6, 7, 8):
        share = share + jnp.sum(owned[k] * owned[k])
    axes = ("line", "group", "mp")
    shares = jnp.broadcast_to(share, (2 * ways.n, 8, 128))
    shares = lax.all_to_all(shares, axes, split_axis=0, concat_axis=0, tiled=True)
    grad_norm = jnp.sqrt(jnp.sum(shares[:, 0, 0]))
    factor = jnp.minimum(1.0, math.sqrt(PARAMS) / grad_norm)
    weights = (gain_attn, w_query, key_weight, value_weight, w_out, gain_ffn, w_gate, w_up, w_down)
    moments = (
        moment_gain_attn,
        moment_w_query,
        key_weight_momentum,
        value_weight_momentum,
        moment_w_out,
        moment_gain_ffn,
        moment_w_gate,
        moment_w_up,
        moment_w_down,
    )
    new_moments = tuple(0.5 * m + 0.5 * factor * g for m, g in zip(moments, owned))
    new_weights = tuple(w - LEARN * (m + DECAY * w) for w, m in zip(weights, new_moments))
    return (activations, input_grad, grad_norm, *new_moments, *new_weights)


def solution(mesh):
    count, cores = mesh.devices.shape
    regrouped = Mesh(
        mesh.devices.reshape(count // GROUP, GROUP, cores), ("line", "group", "mp")
    )
    dp = ("line", "group")
    gain, tall, wide, row = P(dp), P(dp, "mp"), P("mp", dp), P(dp, None)
    leaves = (gain, tall, tall, tall, wide, gain, tall, tall, wide)
    return jax.shard_map(
        on_device,
        mesh=regrouped,
        in_specs=(row, row, P(), P(), P(), *leaves, *leaves),
        out_specs=(row, row, P(), *leaves, *leaves),
        check_vma=False,
    )
```

time: 3960 us -> 962 us (0.24)
  waiting for transfers between devices: 3160 us -> 287 us
  blocking collectives: 317 us -> 0 us
  local copies, waits for them, and re-layouts: 100 us -> 161 us
  other arithmetic: 96.2 us -> 149 us
  starting transfers between devices: 45.6 us -> 92 us
    reduce_scatter x7 -> x5, waiting for transfers between devices: 2400 us -> 0.03 us  [scatter_line(): lax.psum_scatter(whole.astype(BF), 'line', scatter_dimension=0, tiled=True)]
    all_gather x7 -> x2, waiting for transfers between devices: 707 us -> 28.3 us  [the longest x1 28.3 us: gather_line(): return lax.all_gather(value, 'line', axis=0, tiled=True)]
    ppermute x0 -> x42, waiting for transfers between devices: none -> 154 us  [the longest x32 154 us: flip(): return lax.ppermute(value, 'group', [(i, i ^ k) for i in range(GROUP)])]
    all_gather x2 -> x0, blocking collectives: 152 us -> none  [the longest x1 77.4 us: fetch_ffn(): lax.all_gather(gain_ffn.astype(jnp.bfloat16), 'dp', axis=0, tiled=True)]
    unnamed x1 -> x0, blocking collectives: 120 us -> none
    all_to_all x4 -> x11, waiting for transfers between devices: 34.8 us -> 105 us  [the longest x6 52 us: exchange(): lax.all_to_all(value, ('line', 'group'), split_axis=0, concat_axis=0, til...]
    psum x1 -> x0, blocking collectives: 44.7 us -> none  [on_device(): grad_norm = jnp.sqrt(lax.psum(share, ('dp', 'mp')))]
    dot_general x12 -> x17, matrix products: 72.2 us -> 98 us  [the longest x12 86.4 us: mat_nn(): return jnp.dot(left, right, preferred_element_type=F32)]
  transfers between devices with their start and end apart: 21 -> 60, of which waited for: 13 -> 23; matrix products, arithmetic and copies ran while one was open for 7% -> 45% of each run, Pallas kernels for 0% -> 0%
where the time goes in v2:
time: 962 us; the launch traced here: 951 us
  waiting for transfers between devices  287 us (30%)
  matrix products  238 us (25%)
  local copies, waits for them, and re-layouts  161 us (17%)
  other arithmetic  149 us (15%)
  starting transfers between devices  92 us (10%)
  between operations  24.1 us (3%)
    ppermute x32, waiting for transfers between devices, flip(): return lax.ppermute(value, 'group', [(i, i ^ k) for i in range(GROUP)])  154 us
    dot_general x12, matrix products, mat_nn(): return jnp.dot(left, right, preferred_element_type=F32)  86.4 us
    dot_general x9, matrix products, mat_tn(): lax.dot_general(left, right, (((0,), (0,)), ((), ())), preferred_element_...  75.5 us
    dot_general x5, matrix products, mat_nt(): lax.dot_general(left, right, (((1,), (1,)), ((), ())), preferred_element_...  62.3 us
    unnamed x224, local copies, waits for them, and re-layouts  52.5 us
    all_to_all x6, waiting for transfers between devices, exchange(): lax.all_to_all(value, ('line', 'group'), split_axis=0, concat_axis=0, til...  52 us
    ppermute x32, starting transfers between devices, flip(): return lax.ppermute(value, 'group', [(i, i ^ k) for i in range(GROUP)])  38.2 us
    another operation x12, other arithmetic  33.3 us
  transfers between devices with their start and end apart: 60, of which 23 were waited for; matrix products, arithmetic and copies ran while one was open for 45% of the time, Pallas kernels for 0%

profile of v2, /device:TPU:0, one launch (start us, length us, event | category | flops | bytes accessed | tf_op | source)
XLA Modules:
  0.0 950.9 jit_solution(9178930570178711843)
XLA Ops:
  18.7 5.3 all-to-all-start.2
  28.0 32.1 %all-to-all-done.2 = bf16[4,384,1024]{2,1,0:T(8,128)(2,1)S(1)} async-done(((bf16[4,384,1024]{2,1,0:T(8,128)(2,1)}), bf16[4,384,1024]{2,1,0:T(8,128)(2,1)S(1)}, u32[]{:S(2)}, u32[]{:S(2)}) %all-to-all-start.2) | async-done | bytes 3145760 | tf_op jit(solution)/shard_map/all_to_all | solution.py:126
  60.2 6.2 all-to-all-start
  69.7 28.3 %all-gather.3.cloned.1.call-done = bf16[512,3072]{0,1:T(8,128)(2,1)} async-done(((bf16[128,3072]{0,1:T(8,128)(2,1)}), bf16[512,3072]{0,1:T(8,128)(2,1)}) %all-gather.3.cloned.1.call-update) | async-done | bytes 3145744 | tf_op jit(solution)/shard_map/all_gather | solution.py:97
  116.2 34.6 %all-to-all-done.1 = bf16[16,2,128]{2,1,0:T(2,128)(2,1)S(1)} async-done(((bf16[16,2,128]{2,1,0:T(2,128)(2,1)}), bf16[16,2,128]{2,1,0:T(2,128)(2,1)S(1)}, u32[]{:S(2)}, u32[]{:S(2)}) %all-to-all-start.1) | async-done | bytes 8224 | tf_op jit(solution)/shard_map/all_to_all | solution.py:139
  207.2 6.0 fusion.13
  253.4 7.6 fusion.115
  264.2 24.6 %collective-permute-done.21 = bf16[512,1024]{1,0:T(8,128)(2,1)S(1)} collective-permute-done((bf16[512,1024]{1,0:T(8,128)(2,1)S(1)}, bf16[512,1024]{1,0:T(8,128)(2,1)S(1)}, u32[]{:S(2)}, u32[]{:S(2)}) %collective-permute-start.21) | collective-permute-done | bytes 1048608 | tf_op jit(solution)/shard_map/ppermute | solution.py:91
  298.6 5.2 collective-permute-done.23
  304.6 20.9 %collective-permute-done.10 = bf16[512,1024]{1,0:T(8,128)(2,1)S(1)} collective-permute-done((bf16[512,1024]{1,0:T(8,128)(2,1)S(1)}, bf16[512,1024]{1,0:T(8,128)(2,1)S(1)}, u32[]{:S(2)}, u32[]{:S(2)}) %collective-permute-start.10) | collective-permute-done | bytes 1048608 | tf_op jit(solution)/shard_map/ppermute | solution.py:91
  329.8 8.3 collective-permute-done.12
  340.2 5.2 maximum_select_fusion.1
  345.4 6.7 fusion.103
  352.1 17.6 %fusion.98 = f32[2048,1024]{1,0:T(8,128)} fusion(bf16[2048,1024]{1,0:T(8,128)(2,1)S(1)} %bitcast.249, bf16[2048,1024]{1,0:T(8,128)(2,1)} %collective-permute-done.14, bf16[2048,1024]{1,0:T(8,128)(2,1)} %constant_dynamic-update-slice_fusion, pred[]{:T(512)S(6)} %eq.42), kind=kOutput, calls=%fused_computation.296 | convolution fusion | flops 8627683328 | bytes 20971520 | tf_op jit(solution)/shard_map/dot_general | solution.py:66
  369.7 17.4 %fusion.99 = f32[2048,1024]{1,0:T(8,128)} fusion(bf16[2048,1024]{1,0:T(8,128)(2,1)} %bitcast.251, bf16[2048,1024]{1,0:T(8,128)(2,1)} %collective-permute-done.14, bf16[2048,1024]{1,0:T(8,128)(2,1)} %constant_dynamic-update-slice_fusion, pred[]{:T(512)S(6)} %eq.42), kind=kOutput, calls=%fused_computation.297 | convolution fusion | flops 8627683328 | bytes 20971520 | tf_op jit(solution)/shard_map/dot_general | solution.py:66
  387.1 21.6 %multiply_convert_fusion = (bf16[2048,1024]{1,0:T(8,128)(2,1)}, bf16[2048,1024]{1,0:T(8,128)(2,1)}, bf16[2048,1024]{1,0:T(8,128)(2,1)}) fusion(f32[2048,1024]{1,0:T(8,128)} %fusion.99, f32[2048,1024]{1,0:T(8,128)} %fusion.98, bf16[2048,2048]{1,0:T(8,128)(2,1)} %maximum_select_fusion.1, bf16[2048,1024]{1,0:T(8,128)(2,1)S(1)} %bitcast.247), kind=kOutput, calls=%fused_computation.6 | convolution fusion | flops 8621391872 | bytes 41943040 | tf_op jit(solution)/shard_map/dot_general | solution.py:66
  408.7 14.0 %convolution_convert_fusion = bf16[2048,1024]{1,0:T(8,128)(2,1)} fusion(bf16[2048,2048]{1,0:T(8,128)(2,1)} %maximum_select_fusion.1, bf16[2048,1024]{1,0:T(8,128)(2,1)} %get-tuple-element.176), kind=kOutput, calls=%fused_computation.48 | convolution fusion | flops 8592031744 | bytes 16777216 | tf_op jit(solution)/shard_map/dot_general | solution.py:74
  422.8 15.9 %fusion.118 = f32[2048,2048]{1,0:T(8,128)} fusion(bf16[2048,1024]{1,0:T(8,128)(2,1)} %get-tuple-element.175, bf16[2048,1024]{1,0:T(8,128)(2,1)} %bitcast.252), kind=kOutput, calls=%fused_computation.315 | convolution fusion | flops 8589934592 | bytes 25165824 | tf_op jit(solution)/shard_map/dot_general | solution.py:70
  438.7 17.1 %convolution_add_fusion = f32[2048,2048]{1,0:T(8,128)} fusion(f32[2048,2048]{1,0:T(8,128)} %fusion.118, bf16[2048,1024]{1,0:T(8,128)(2,1)S(1)} %copy-done.97, bf16[2048,1024]{1,0:T(8,128)(2,1)S(1)} %bitcast.250), kind=kOutput, calls=%fused_computation.13 | convolution fusion | flops 8594128896 | bytes 41943040 | tf_op jit(solution)/shard_map/dot_general | solution.py:70
  455.8 8.5 select_convert_fusion
  464.9 10.7 %fusion.117 = f32[2048,2048]{1,0:T(8,128)S(1)} fusion(bf16[2048,1024]{1,0:T(8,128)(2,1)} %get-tuple-element.176, bf16[2048,1024]{1,0:T(8,128)(2,1)S(1)} %bitcast.248), kind=kOutput, calls=%fused_computation.314 | convolution fusion | flops 8589934592 | bytes 25165824 | tf_op jit(solution)/shard_map/dot_general | solution.py:70
  475.6 5.8 copy-done.4
  484.1 17.7 %convolution_convert_fusion.1 = bf16[2048,1024]{1,0:T(8,128)(2,1)} fusion(bf16[2048,1024]{1,0:T(8,128)(2,1)S(1)} %copy-done.97, bf16[2048,1024]{1,0:T(8,128)(2,1)} %collective-permute-done.14, bf16[2048,1024]{1,0:T(8,128)(2,1)} %constant_dynamic-update-slice_fusion, pred[]{:T(512)S(6)} %eq.42), kind=kOutput, calls=%fused_computation.49 | convolution fusion | flops 8629780480 | bytes 16777216 | tf_op jit(solution)/shard_map/dot_general | solution.py:74
  501.9 9.1 fusion.101
  512.0 13.8 %fusion.102 = (bf16[2048,1024]{1,0:T(8,128)(2,1)S(1)}, f32[2048,1024]{1,0:T(8,128)}) fusion(bf16[2048,1024]{1,0:T(8,128)(2,1)} %collective-permute-done.15, f32[2048,2048]{1,0:T(8,128)} %copy-done.4, pred[]{:T(512)S(6)} %eq.42), kind=kLoop, calls=%fused_computation.299 | loop fusion | flops 8388608 | bytes 33554432 | tf_op jit(solution)/shard_map/convert.39
  531.7 10.3 %collective-permute-done.16 = bf16[256,1024]{1,0:T(8,128)(2,1)} collective-permute-done((bf16[256,1024]{1,0:T(8,128)(2,1)}, bf16[256,1024]{1,0:T(8,128)(2,1)}, u32[]{:S(2)}, u32[]{:S(2)}) %collective-permute-start.16) | collective-permute-done | bytes 524320 | tf_op jit(solution)/shard_map/ppermute | solution.py:91
  548.4 16.3 %collective-permute-done.28 = bf16[512,1024]{1,0:T(8,128)(2,1)} collective-permute-done((bf16[512,1024]{1,0:T(8,128)(2,1)S(1)}, bf16[512,1024]{1,0:T(8,128)(2,1)}, u32[]{:S(2)}, u32[]{:S(2)}) %collective-permute-start.28) | collective-permute-done | bytes 1048608 | tf_op jit(solution)/shard_map/ppermute | solution.py:91
  567.4 18.8 %convolution_convert_fusion.2 = bf16[2048,1024]{1,0:T(8,128)(2,1)} fusion(bf16[2048,1024]{1,0:T(8,128)(2,1)} %get-tuple-element.175, bf16[2048,1024]{1,0:T(8,128)(2,1)} %collective-permute-done.14, bf16[2048,1024]{1,0:T(8,128)(2,1)} %constant_dynamic-update-slice_fusion, pred[]{:T(512)S(6)} %eq.42), kind=kOutput, calls=%fused_computation.50 | convolution fusion | flops 8629780480 | bytes 16777216 | tf_op jit(solution)/shard_map/dot_general | solution.py:74
  586.8 5.8 convolution_convert_fusion.9
  592.6 5.6 all-to-all-start.3
  598.3 4.9 multiply_reduce_fusion
  603.2 4.9 convert_bitcast_fusion
  647.7 6.5 fusion.67
  662.6 11.1 %fusion.116 = (bf16[512,2048]{1,0:T(8,128)(2,1)}, f32[512,2048]{1,0:T(8,128)}) fusion(bf16[2048,2048]{1,0:T(8,128)(2,1)} %bitcast.10, bf16[512,512]{1,0:T(8,128)(2,1)} %copy-done.69, bf16[512,512]{1,0:T(8,128)(2,1)S(1)} %copy-done.68, bf16[512,1024]{1,0:T(8,128)(2,1)S(1)} %bitcast.270), kind=kOutput, calls=%fused_computation.313 | convolution fusion | flops 4302307328 | bytes 16777216 | tf_op jit(solution)/shard_map/dot_general | solution.py:70
  685.3 7.7 collective-permute-done.40
  699.9 15.6 %collective-permute-done.36 = bf16[256,2048]{1,0:T(8,128)(2,1)S(1)} collective-permute-done((bf16[256,2048]{1,0:T(8,128)(2,1)S(1)}, bf16[256,2048]{1,0:T(8,128)(2,1)S(1)}, u32[]{:S(2)}, u32[]{:S(2)}) %collective-permute-start.36) | collective-permute-done | bytes 1048608 | tf_op jit(solution)/shard_map/ppermute | solution.py:91
  720.9 17.0 %collective-permute-done.39 = bf16[512,1024]{1,0:T(8,128)(2,1)S(1)} collective-permute-done((bf16[512,1024]{1,0:T(8,128)(2,1)S(1)}, bf16[512,1024]{1,0:T(8,128)(2,1)S(1)}, u32[]{:S(2)}, u32[]{:S(2)}) %collective-permute-start.39) | collective-permute-done | bytes 1048608 | tf_op jit(solution)/shard_map/ppermute | solution.py:91
  756.7 26.3 %collective-permute-done.35 = bf16[512,2048]{1,0:T(8,128)(2,1)} collective-permute-done((bf16[512,2048]{1,0:T(8,128)(2,1)}, bf16[512,2048]{1,0:T(8,128)(2,1)}, u32[]{:S(2)}, u32[]{:S(2)}) %collective-permute-start.35) | collective-permute-done | bytes 2097184 | tf_op jit(solution)/shard_map/ppermute | solution.py:91
  782.9 5.9 fusion.16
  797.5 5.3 fusion.10
  804.7 6.6 all-to-all-done.8
  811.3 5.9 all-to-all-start.5
  842.2 11.2 %all-to-all-done.5 = bf16[16,32,1024]{2,1,0:T(8,128)(2,1)} async-done(((bf16[16,32,1024]{2,1,0:T(8,128)(2,1)}), bf16[16,32,1024]{2,1,0:T(8,128)(2,1)}, u32[]{:S(2)}, u32[]{:S(2)}) %all-to-all-start.5) | async-done | bytes 1048608 | tf_op jit(solution)/shard_map/all_to_all | solution.py:139
  865.1 6.0 all-to-all-done.7
  873.4 6.3 all-to-all-start.6
  880.9 6.2 all-to-all-done.6
  910.8 5.1 multiply_subtract_fusion
  924.3 5.0 multiply_subtract_fusion.2
  (495 shorter events, 352.4 us)
Async XLA Ops:
  7.2 90.7 %all-gather.3.cloned.1.call-start = ((), (), s32[]{:S(2)}) async-start(), calls=%async_computation.16 | async-start | bytes 3932160 | tf_op jit(solution)/shard_map/all_gather | solution.py:97
  18.7 41.4 %all-to-all-start.2 = ((bf16[4,384,1024]{2,1,0:T(8,128)(2,1)}), bf16[4,384,1024]{2,1,0:T(8,128)(2,1)S(1)}, u32[]{:S(2)}, u32[]{:S(2)}) async-start(bf16[4,384,1024]{2,1,0:T(8,128)(2,1)} %pad_maximum_fusion), calls=%async_computation.2 | async-start | bytes 6291456 | tf_op jit(solution)/shard_map/all_to_all | solution.py:126
  60.2 44.8 %all-to-all-start = ((bf16[16,32,1024]{2,1,0:T(8,128)(2,1)}), bf16[16,32,1024]{2,1,0:T(8,128)(2,1)}, u32[]{:S(2)}, u32[]{:S(2)}) async-start(bf16[16,32,1024]{2,1,0:T(8,128)(2,1)} %bitcast.265), calls=%async_computation | async-start | bytes 2097152 | tf_op jit(solution)/shard_map/all_to_all | solution.py:139
  66.4 279.0 %all-gather.5.cloned.1.call-start = ((), (), s32[]{:S(2)}) async-start(), calls=%async_computation.17 | async-start | bytes 15728640 | tf_op jit(solution)/shard_map/all_gather | solution.py:243
  101.0 50.5 %collective-permute-start.1 = (bf16[512,2048]{0,1:T(8,128)(2,1)}, bf16[512,2048]{0,1:T(8,128)(2,1)}, u32[]{:S(2)}, u32[]{:S(2)}) collective-permute-start(bf16[512,2048]{0,1:T(8,128)(2,1)} %slice.513), channel_id=1, source_target_pairs={{0,2},{2,0},{4,6},{6,4},{1,3},{3,1},{5,7},{7,5},{8,10},{10,8},{12,... | collective-permute-start | bytes 6291464 | tf_op jit(solution)/shard_map/ppermute | solution.py:91
  103.1 52.2 %collective-permute-start.2 = (bf16[512,2048]{0,1:T(8,128)(2,1)}, bf16[512,2048]{0,1:T(8,128)(2,1)}, u32[]{:S(2)}, u32[]{:S(2)}) collective-permute-start(bf16[512,2048]{0,1:T(8,128)(2,1)} %slice.513), channel_id=1, source_target_pairs={{0,4},{2,6},{4,0},{6,2},{1,5},{3,7},{5,1},{7,3},{8,12},{10,14},{12... | collective-permute-start | bytes 6291464 | tf_op jit(solution)/shard_map/ppermute | solution.py:91
  105.6 45.2 %all-to-all-start.1 = ((bf16[16,2,128]{2,1,0:T(2,128)(2,1)}), bf16[16,2,128]{2,1,0:T(2,128)(2,1)S(1)}, u32[]{:S(2)}, u32[]{:S(2)}) async-start(bf16[16,2,128]{2,1,0:T(2,128)(2,1)} %broadcast_in_dim.58), calls=%async_computation.1 | async-start | bytes 16384 | tf_op jit(solution)/shard_map/all_to_all | solution.py:139
  111.2 39.6 %collective-permute-start = (bf16[512,1024]{1,0:T(8,128)(2,1)S(1)}, bf16[512,1024]{1,0:T(8,128)(2,1)S(1)}, u32[]{:S(2)}, u32[]{:S(2)}) collective-permute-start(bf16[512,1024]{1,0:T(8,128)(2,1)S(1)} %convolution_convert_fusion.10), channel_id=1, source_target_pairs={{0,1},{1,0},{2,3},{3,2},{4,5},{5,4},{6,7},{7,6},{8,9},{9,8},{10,11... | collective-permute-start | bytes 3145736 | tf_op jit(solution)/shard_map/ppermute | solution.py:94
  153.7 29.1 %collective-permute-start.3 = (bf16[256,2048]{0,1:T(8,128)(2,1)}, bf16[256,2048]{0,1:T(8,128)(2,1)}, u32[]{:S(2)}, u32[]{:S(2)}) collective-permute-start(bf16[256,2048]{0,1:T(8,128)(2,1)} %slice.514), channel_id=1, source_target_pairs={{0,4},{2,6},{4,0},{6,2},{1,5},{3,7},{5,1},{7,3},{8,12},{10,14},{12... | collective-permute-start | bytes 3145736 | tf_op jit(solution)/shard_map/ppermute | solution.py:91
  157.5 25.3 %collective-permute-start.4 = (bf16[256,2048]{0,1:T(8,128)(2,1)}, bf16[256,2048]{0,1:T(8,128)(2,1)}, u32[]{:S(2)}, u32[]{:S(2)}) collective-permute-start(bf16[256,2048]{0,1:T(8,128)(2,1)} %slice.515), channel_id=1, source_target_pairs={{0,2},{2,0},{4,6},{6,4},{1,3},{3,1},{5,7},{7,5},{8,10},{10,8},{12,... | collective-permute-start | bytes 3145736 | tf_op jit(solution)/shard_map/ppermute | solution.py:91
  192.9 34.5 %collective-permute-start.5 = (bf16[512,1024]{0,1:T(8,128)(2,1)}, bf16[512,1024]{0,1:T(8,128)(2,1)}, u32[]{:S(2)}, u32[]{:S(2)}) collective-permute-start(bf16[512,1024]{0,1:T(8,128)(2,1)} %slice.523), channel_id=1, source_target_pairs={{0,2},{2,0},{4,6},{6,4},{1,3},{3,1},{5,7},{7,5},{8,10},{10,8},{12,... | collective-permute-start | bytes 3145736 | tf_op jit(solution)/shard_map/ppermute | solution.py:91
  194.4 36.8 %collective-permute-start.6 = (bf16[512,1024]{0,1:T(8,128)(2,1)}, bf16[512,1024]{0,1:T(8,128)(2,1)}, u32[]{:S(2)}, u32[]{:S(2)}) collective-permute-start(bf16[512,1024]{0,1:T(8,128)(2,1)} %slice.523), channel_id=1, source_target_pairs={{0,4},{2,6},{4,0},{6,2},{1,5},{3,7},{5,1},{7,3},{8,12},{10,14},{12... | collective-permute-start | bytes 3145736 | tf_op jit(solution)/shard_map/ppermute | solution.py:91
  194.9 66.1 %all-to-all-start.4 = ((bf16[16,32,1024]{2,1,0:T(8,128)(2,1)}), bf16[16,32,1024]{2,1,0:T(8,128)(2,1)}, u32[]{:S(2)}, u32[]{:S(2)}) async-start(bf16[16,32,1024]{2,1,0:T(8,128)(2,1)} %bitcast.264), calls=%async_computation.4 | async-start | bytes 2097152 | tf_op jit(solution)/shard_map/all_to_all | solution.py:139
  199.2 545.0 %reduce-scatter.14.cloned.1.call-start = ((), (), s32[]{:S(2)}) async-start(), calls=%async_computation.22 | async-start | bytes 5242880 | tf_op jit(solution)/shard_map/reduce_scatter | solution.py:100
  229.4 19.2 %collective-permute-start.7 = (bf16[256,1024]{0,1:T(8,128)(2,1)}, bf16[256,1024]{0,1:T(8,128)(2,1)}, u32[]{:S(2)}, u32[]{:S(2)}) collective-permute-start(bf16[256,1024]{0,1:T(8,128)(2,1)} %slice.524), channel_id=1, source_target_pairs={{0,4},{2,6},{4,0},{6,2},{1,5},{3,7},{5,1},{7,3},{8,12},{10,14},{12... | collective-permute-start | bytes 1572872 | tf_op jit(solution)/shard_map/ppermute | solution.py:91
  261.0 29.7 %collective-permute-start.9 = (bf16[512,2048]{1,0:T(8,128)(2,1)}, bf16[512,2048]{1,0:T(8,128)(2,1)}, u32[]{:S(2)}, u32[]{:S(2)}) collective-permute-start(bf16[512,2048]{1,0:T(8,128)(2,1)} %get-tuple-element.246), channel_id=1, source_target_pairs={{0,1},{1,0},{2,3},{3,2},{4,5},{5,4},{6,7},{7,6},{8,9},{9,8},{10,11... | collective-permute-start | bytes 6291464 | tf_op jit(solution)/shard_map/ppermute | solution.py:94
  263.2 25.6 %collective-permute-start.21 = (bf16[512,1024]{1,0:T(8,128)(2,1)S(1)}, bf16[512,1024]{1,0:T(8,128)(2,1)S(1)}, u32[]{:S(2)}, u32[]{:S(2)}) collective-permute-start(bf16[512,1024]{1,0:T(8,128)(2,1)S(1)} %convolution_convert_fusion.6), channel_id=1, source_target_pairs={{0,2},{2,0},{4,6},{6,4},{1,3},{3,1},{5,7},{7,5},{8,10},{10,8},{12,... | collective-permute-start | bytes 3145736 | tf_op jit(solution)/shard_map/ppermute | solution.py:91
  263.8 25.7 %collective-permute-start.22 = (bf16[512,1024]{1,0:T(8,128)(2,1)S(1)}, bf16[512,1024]{1,0:T(8,128)(2,1)S(1)}, u32[]{:S(2)}, u32[]{:S(2)}) collective-permute-start(bf16[512,1024]{1,0:T(8,128)(2,1)S(1)} %convolution_convert_fusion.6), channel_id=1, source_target_pairs={{0,4},{2,6},{4,0},{6,2},{1,5},{3,7},{5,1},{7,3},{8,12},{10,14},{12... | collective-permute-start | bytes 3145736 | tf_op jit(solution)/shard_map/ppermute | solution.py:91
  296.0 29.4 %collective-permute-start.10 = (bf16[512,1024]{1,0:T(8,128)(2,1)S(1)}, bf16[512,1024]{1,0:T(8,128)(2,1)S(1)}, u32[]{:S(2)}, u32[]{:S(2)}) collective-permute-start(bf16[512,1024]{1,0:T(8,128)(2,1)S(1)} %get-tuple-element.167), channel_id=1, source_target_pairs={{0,2},{2,0},{4,6},{6,4},{1,3},{3,1},{5,7},{7,5},{8,10},{10,8},{12,... | collective-permute-start | bytes 3145736 | tf_op jit(solution)/shard_map/ppermute | solution.py:91
  297.0 29.9 %collective-permute-start.11 = (bf16[512,1024]{1,0:T(8,128)(2,1)S(1)}, bf16[512,1024]{1,0:T(8,128)(2,1)S(1)}, u32[]{:S(2)}, u32[]{:S(2)}) collective-permute-start(bf16[512,1024]{1,0:T(8,128)(2,1)S(1)} %get-tuple-element.167), channel_id=1, source_target_pairs={{0,4},{2,6},{4,0},{6,2},{1,5},{3,7},{5,1},{7,3},{8,12},{10,14},{12... | collective-permute-start | bytes 3145736 | tf_op jit(solution)/shard_map/ppermute | solution.py:91
  304.5 35.7 %collective-permute-start.25 = (bf16[2048,1024]{1,0:T(8,128)(2,1)S(1)}, bf16[2048,1024]{1,0:T(8,128)(2,1)S(1)}, u32[]{:S(2)}, u32[]{:S(2)}) collective-permute-start(bf16[2048,1024]{1,0:T(8,128)(2,1)S(1)} %constant_dynamic-update-slice_fusion.5), channel_id=1, source_target_pairs={{0,1},{1,0},{2,3},{3,2},{4,5},{5,4},{6,7},{7,6},{8,9},{9,8},{10,11... | collective-permute-start | bytes 12582920 | tf_op jit(solution)/shard_map/ppermute | solution.py:94
  422.8 323.7 %reduce-scatter.12.cloned.1.call-start = ((), (), s32[]{:S(2)}) async-start(), calls=%async_computation.21 | async-start | bytes 5242880 | tf_op jit(solution)/shard_map/reduce_scatter | solution.py:100
  464.3 37.6 %collective-permute-start.26 = (bf16[2048,1024]{1,0:T(8,128)(2,1)}, bf16[2048,1024]{1,0:T(8,128)(2,1)}, u32[]{:S(2)}, u32[]{:S(2)}) collective-permute-start(bf16[2048,1024]{1,0:T(8,128)(2,1)} %select_convert_fusion), channel_id=1, source_target_pairs={{0,1},{1,0},{2,3},{3,2},{4,5},{5,4},{6,7},{7,6},{8,9},{9,8},{10,11... | collective-permute-start | bytes 12582920 | tf_op jit(solution)/shard_map/ppermute | solution.py:94
  484.0 28.0 %collective-permute-start.15 = (bf16[2048,1024]{1,0:T(8,128)(2,1)}, bf16[2048,1024]{1,0:T(8,128)(2,1)}, u32[]{:S(2)}, u32[]{:S(2)}) collective-permute-start(bf16[2048,1024]{1,0:T(8,128)(2,1)} %select_convert_fusion.1), channel_id=1, source_target_pairs={{0,1},{1,0},{2,3},{3,2},{4,5},{5,4},{6,7},{7,6},{8,9},{9,8},{10,11... | collective-permute-start | bytes 12582920 | tf_op jit(solution)/shard_map/ppermute | solution.py:94
  501.9 331.0 %reduce-scatter.10.cloned.1.call-start = ((), (), s32[]{:S(2)}) async-start(), calls=%async_computation.20 | async-start | bytes 5242880 | tf_op jit(solution)/shard_map/reduce_scatter | solution.py:100
  511.2 17.2 %collective-permute-start.27 = (bf16[256,1024]{1,0:T(8,128)(2,1)S(1)}, bf16[256,1024]{1,0:T(8,128)(2,1)S(1)}, u32[]{:S(2)}, u32[]{:S(2)}) collective-permute-start(bf16[256,1024]{1,0:T(8,128)(2,1)S(1)} %get-tuple-element.188), channel_id=1, source_target_pairs={{0,4},{2,6},{4,0},{6,2},{1,5},{3,7},{5,1},{7,3},{8,12},{10,14},{12... | collective-permute-start | bytes 1572872 | tf_op jit(solution)/shard_map/ppermute | solution.py:91
  511.4 17.0 %collective-permute-start.29 = (bf16[256,1024]{1,0:T(8,128)(2,1)S(1)}, bf16[256,1024]{1,0:T(8,128)(2,1)S(1)}, u32[]{:S(2)}, u32[]{:S(2)}) collective-permute-start(bf16[256,1024]{1,0:T(8,128)(2,1)S(1)} %get-tuple-element.189), channel_id=1, source_target_pairs={{0,2},{2,0},{4,6},{6,4},{1,3},{3,1},{5,7},{7,5},{8,10},{10,8},{12,... | collective-permute-start | bytes 1572872 | tf_op jit(solution)/shard_map/ppermute | solution.py:91
  528.8 35.9 %collective-permute-start.28 = (bf16[512,1024]{1,0:T(8,128)(2,1)S(1)}, bf16[512,1024]{1,0:T(8,128)(2,1)}, u32[]{:S(2)}, u32[]{:S(2)}) collective-permute-start(bf16[512,1024]{1,0:T(8,128)(2,1)S(1)} %pad_maximum_fusion.12), channel_id=1, source_target_pairs={{0,2},{2,0},{4,6},{6,4},{1,3},{3,1},{5,7},{7,5},{8,10},{10,8},{12,... | collective-permute-start | bytes 3145736 | tf_op jit(solution)/shard_map/ppermute | solution.py:91
  529.7 34.9 %collective-permute-start.30 = (bf16[512,1024]{1,0:T(8,128)(2,1)S(1)}, bf16[512,1024]{1,0:T(8,128)(2,1)}, u32[]{:S(2)}, u32[]{:S(2)}) collective-permute-start(bf16[512,1024]{1,0:T(8,128)(2,1)S(1)} %pad_maximum_fusion.13), channel_id=1, source_target_pairs={{0,4},{2,6},{4,0},{6,2},{1,5},{3,7},{5,1},{7,3},{8,12},{10,14},{12... | collective-permute-start | bytes 3145736 | tf_op jit(solution)/shard_map/ppermute | solution.py:91
  545.5 41.2 %collective-permute-start.17 = (bf16[512,1024]{1,0:T(8,128)(2,1)}, bf16[512,1024]{1,0:T(8,128)(2,1)}, u32[]{:S(2)}, u32[]{:S(2)}) collective-permute-start(bf16[512,1024]{1,0:T(8,128)(2,1)} %pad_maximum_fusion.10), channel_id=1, source_target_pairs={{0,2},{2,0},{4,6},{6,4},{1,3},{3,1},{5,7},{7,5},{8,10},{10,8},{12,... | collective-permute-start | bytes 3145736 | tf_op jit(solution)/shard_map/ppermute | solution.py:91
  547.8 38.8 %collective-permute-start.19 = (bf16[512,1024]{1,0:T(8,128)(2,1)}, bf16[512,1024]{1,0:T(8,128)(2,1)}, u32[]{:S(2)}, u32[]{:S(2)}) collective-permute-start(bf16[512,1024]{1,0:T(8,128)(2,1)} %pad_maximum_fusion.11), channel_id=1, source_target_pairs={{0,4},{2,6},{4,0},{6,2},{1,5},{3,7},{5,1},{7,3},{8,12},{10,14},{12... | collective-permute-start | bytes 3145736 | tf_op jit(solution)/shard_map/ppermute | solution.py:91
  567.3 31.0 %collective-permute-start.31 = (f32[512,1024]{1,0:T(8,128)S(1)}, f32[512,1024]{1,0:T(8,128)}, u32[]{:S(2)}, u32[]{:S(2)}) collective-permute-start(f32[512,1024]{1,0:T(8,128)S(1)} %fusion.22), channel_id=1, source_target_pairs={{0,1},{1,0},{2,3},{3,2},{4,5},{5,4},{6,7},{7,6},{8,9},{9,8},{10,11... | collective-permute-start | bytes 6291464 | tf_op jit(solution)/shard_map/ppermute | solution.py:94
  592.6 159.9 %all-to-all-start.3 = ((bf16[16,32,1024]{2,1,0:T(8,128)(2,1)}), bf16[16,32,1024]{2,1,0:T(8,128)(2,1)}, u32[]{:S(2)}, u32[]{:S(2)}) async-start(bf16[16,32,1024]{2,1,0:T(8,128)(2,1)} %bitcast.39), calls=%async_computation.3 | async-start | bytes 2097152 | tf_op jit(solution)/shard_map/all_to_all | solution.py:139
  598.2 290.8 %reduce-scatter.8.cloned.1.call-start = ((), (), s32[]{:S(2)}) async-start(), calls=%async_computation.19 | async-start | bytes 1310720 | tf_op jit(solution)/shard_map/reduce_scatter | solution.py:100
  632.1 49.8 %collective-permute-start.38 = (bf16[256,1024]{1,0:T(8,128)(2,1)}, bf16[256,1024]{1,0:T(8,128)(2,1)}, u32[]{:S(2)}, u32[]{:S(2)}) collective-permute-start(bf16[256,1024]{1,0:T(8,128)(2,1)} %bitcast.75), channel_id=1, source_target_pairs={{0,4},{2,6},{4,0},{6,2},{1,5},{3,7},{5,1},{7,3},{8,12},{10,14},{12... | collective-permute-start | bytes 1572872 | tf_op jit(solution)/shard_map/ppermute | solution.py:91
  656.1 39.0 %collective-permute-start.34 = (bf16[256,2048]{1,0:T(8,128)(2,1)}, bf16[256,2048]{1,0:T(8,128)(2,1)}, u32[]{:S(2)}, u32[]{:S(2)}) collective-permute-start(bf16[256,2048]{1,0:T(8,128)(2,1)} %bitcast.64), channel_id=1, source_target_pairs={{0,4},{2,6},{4,0},{6,2},{1,5},{3,7},{5,1},{7,3},{8,12},{10,14},{12... | collective-permute-start | bytes 3145736 | tf_op jit(solution)/shard_map/ppermute | solution.py:91
  680.0 35.4 %collective-permute-start.36 = (bf16[256,2048]{1,0:T(8,128)(2,1)S(1)}, bf16[256,2048]{1,0:T(8,128)(2,1)S(1)}, u32[]{:S(2)}, u32[]{:S(2)}) collective-permute-start(bf16[256,2048]{1,0:T(8,128)(2,1)S(1)} %bitcast.272), channel_id=1, source_target_pairs={{0,2},{2,0},{4,6},{6,4},{1,3},{3,1},{5,7},{7,5},{8,10},{10,8},{12,... | collective-permute-start | bytes 3145736 | tf_op jit(solution)/shard_map/ppermute | solution.py:91
  680.2 68.5 %collective-permute-start.32 = (bf16[512,2048]{1,0:T(8,128)(2,1)}, bf16[512,2048]{1,0:T(8,128)(2,1)}, u32[]{:S(2)}, u32[]{:S(2)}) collective-permute-start(bf16[512,2048]{1,0:T(8,128)(2,1)} %get-tuple-element.250), channel_id=1, source_target_pairs={{0,1},{1,0},{2,3},{3,2},{4,5},{5,4},{6,7},{7,6},{8,9},{9,8},{10,11... | collective-permute-start | bytes 6291464 | tf_op jit(solution)/shard_map/ppermute | solution.py:94
  683.4 54.5 %collective-permute-start.39 = (bf16[512,1024]{1,0:T(8,128)(2,1)S(1)}, bf16[512,1024]{1,0:T(8,128)(2,1)S(1)}, u32[]{:S(2)}, u32[]{:S(2)}) collective-permute-start(bf16[512,1024]{1,0:T(8,128)(2,1)S(1)} %pad_maximum_fusion.15), channel_id=1, source_target_pairs={{0,2},{2,0},{4,6},{6,4},{1,3},{3,1},{5,7},{7,5},{8,10},{10,8},{12,... | collective-permute-start | bytes 3145736 | tf_op jit(solution)/shard_map/ppermute | solution.py:91
  693.2 44.7 %collective-permute-start.41 = (bf16[512,1024]{1,0:T(8,128)(2,1)S(1)}, bf16[512,1024]{1,0:T(8,128)(2,1)S(1)}, u32[]{:S(2)}, u32[]{:S(2)}) collective-permute-start(bf16[512,1024]{1,0:T(8,128)(2,1)S(1)} %pad_maximum_fusion.16), channel_id=1, source_target_pairs={{0,4},{2,6},{4,0},{6,2},{1,5},{3,7},{5,1},{7,3},{8,12},{10,14},{12... | collective-permute-start | bytes 3145736 | tf_op jit(solution)/shard_map/ppermute | solution.py:91
  698.4 84.6 %collective-permute-start.35 = (bf16[512,2048]{1,0:T(8,128)(2,1)}, bf16[512,2048]{1,0:T(8,128)(2,1)}, u32[]{:S(2)}, u32[]{:S(2)}) collective-permute-start(bf16[512,2048]{1,0:T(8,128)(2,1)} %pad_maximum_fusion.3), channel_id=1, source_target_pairs={{0,2},{2,0},{4,6},{6,4},{1,3},{3,1},{5,7},{7,5},{8,10},{10,8},{12,... | collective-permute-start | bytes 6291464 | tf_op jit(solution)/shard_map/ppermute | solution.py:91
  717.3 65.6 %collective-permute-start.37 = (bf16[512,2048]{1,0:T(8,128)(2,1)}, bf16[512,2048]{1,0:T(8,128)(2,1)}, u32[]{:S(2)}, u32[]{:S(2)}) collective-permute-start(bf16[512,2048]{1,0:T(8,128)(2,1)} %pad_maximum_fusion.4), channel_id=1, source_target_pairs={{0,4},{2,6},{4,0},{6,2},{1,5},{3,7},{5,1},{7,3},{8,12},{10,14},{12... | collective-permute-start | bytes 6291464 | tf_op jit(solution)/shard_map/ppermute | solution.py:91
  752.6 40.7 %all-to-all-start.9 = ((bf16[4,128,1024]{1,2,0:T(8,128)(2,1)}), bf16[4,128,1024]{1,2,0:T(8,128)(2,1)S(1)}, u32[]{:S(2)}, u32[]{:S(2)}) async-start(bf16[4,128,1024]{1,2,0:T(8,128)(2,1)} %copy.301), calls=%async_computation.14 | async-start | bytes 2097152 | tf_op jit(solution)/shard_map/all_to_all | solution.py:133
  756.7 134.1 %reduce-scatter.6.cloned.1.call-start = ((), (), s32[]{:S(2)}) async-start(), calls=%async_computation.18 | async-start | bytes 2621440 | tf_op jit(solution)/shard_map/reduce_scatter | solution.py:100
  793.2 18.0 %all-to-all-start.8 = ((bf16[4,128,1024]{1,2,0:T(8,128)(2,1)}), bf16[4,128,1024]{1,2,0:T(8,128)(2,1)}, u32[]{:S(2)}, u32[]{:S(2)}) async-start(bf16[4,128,1024]{1,2,0:T(8,128)(2,1)} %copy.300), calls=%async_computation.12 | async-start | bytes 2097152 | tf_op jit(solution)/shard_map/all_to_all | solution.py:133
  811.3 42.1 %all-to-all-start.5 = ((bf16[16,32,1024]{2,1,0:T(8,128)(2,1)}), bf16[16,32,1024]{2,1,0:T(8,128)(2,1)}, u32[]{:S(2)}, u32[]{:S(2)}) async-start(bf16[16,32,1024]{2,1,0:T(8,128)(2,1)} %bitcast.268), calls=%async_computation.5 | async-start | bytes 2097152 | tf_op jit(solution)/shard_map/all_to_all | solution.py:139
  853.4 17.8 %all-to-all-start.7 = ((bf16[4,128,1024]{1,2,0:T(8,128)(2,1)}), bf16[4,128,1024]{1,2,0:T(8,128)(2,1)}, u32[]{:S(2)}, u32[]{:S(2)}) async-start(bf16[4,128,1024]{1,2,0:T(8,128)(2,1)} %copy.299), calls=%async_computation.10 | async-start | bytes 2097152 | tf_op jit(solution)/shard_map/all_to_all | solution.py:133
  864.0 37.1 %collective-permute-start.33 = (bf16[512,1024]{1,0:T(8,128)(2,1)}, bf16[512,1024]{1,0:T(8,128)(2,1)}, u32[]{:S(2)}, u32[]{:S(2)}) collective-permute-start(bf16[512,1024]{1,0:T(8,128)(2,1)} %convolution_convert_fusion.4), channel_id=1, source_target_pairs={{0,1},{1,0},{2,3},{3,2},{4,5},{5,4},{6,7},{7,6},{8,9},{9,8},{10,11... | collective-permute-start | bytes 3145736 | tf_op jit(solution)/shard_map/ppermute | solution.py:94
  (110 other events, 1948.2 us)
Sparse Core Ops, SparseCore 0:
  12.8 85.0 all-gather.2
  99.5 239.4 all-gather.4
  422.9 76.4 reduce-scatter.13
  502.0 76.8 reduce-scatter.11
  586.3 93.6 reduce-scatter.9
  739.6 28.3 reduce-scatter.7
  789.0 57.9 reduce-scatter.5

commit v3 on v2

--- a/solution.py
+++ b/solution.py
@@ -1,8 +1,11 @@
+import functools
 import math
 
 import jax
 import jax.numpy as jnp
 from jax import lax
+from jax.experimental import pallas as pl
+from jax.experimental.pallas import tpu as pltpu
 from jax.sharding import Mesh
 from jax.sharding import PartitionSpec as P
 
@@ -78,6 +81,744 @@
     return lax.optimization_barrier((value, *others))[0]
 
 
+MESH = pl.DeviceIdType.MESH
+ANY = pl.BlockSpec(memory_space=pl.ANY)
+WHOLE = pl.BlockSpec(memory_space=pltpu.VMEM)
+
+
+def places():
+    z, p, core = lax.axis_index("line"), lax.axis_index("group"), lax.axis_index("mp")
+    one = p + 1 - 2 * lax.rem(p, 2)
+    two = p + 2 - 4 * (p // 2)
+    three = GROUP - 1 - p
+    return z, p, core, one, two, three
+
+
+def meet(partners):
+    barrier = pltpu.get_barrier_semaphore()
+    for partner in partners:
+        pl.semaphore_signal(barrier, inc=1, device_id=partner, device_id_type=MESH)
+    pl.semaphore_wait(barrier, len(partners))
+
+
+def to(src, dst, send, recv, partner):
+    return pltpu.make_async_remote_copy(
+        src_ref=src, dst_ref=dst, send_sem=send, recv_sem=recv,
+        device_id=partner, device_id_type=MESH,
+    )
+
+
+def share_rows_kernel(h, out, send, recv, local):
+    z, p, core, one, two, _ = places()
+    rows, width = h.shape
+    half, wide = rows // 2, width // 2
+    cols = pl.ds(pl.multiple_of(core * wide, wide), wide)
+    x, y, twin = (z, one, core), (z, two, core), (z, p, 1 - core)
+    meet([x, y, twin])
+    own = pltpu.make_async_copy(h, out.at[pl.ds(0, rows)], local)
+    own.start()
+    first, second = pl.ds(0, half), pl.ds(half, half)
+
+    def part(k, b):
+        return out.at[pl.ds(k * rows + b * half, half), cols]
+
+    copies = {}
+
+    def go(name, i, src, dst, partner):
+        copies[name] = to(src, dst, send.at[i], recv.at[i], partner)
+        copies[name].start()
+
+    go("1a", 0, h.at[first, cols], part(1, 0), x)
+    go("2b", 3, h.at[second, cols], part(2, 1), y)
+    go("1b", 1, h.at[second, cols], part(1, 1), x)
+    go("2a", 2, h.at[first, cols], part(2, 0), y)
+    copies["1a"].wait_recv()
+    go("3a", 4, part(1, 0), part(3, 0), y)
+    copies["2b"].wait_recv()
+    go("3b", 5, part(2, 1), part(3, 1), x)
+    go("t0", 6, part(1, 0), part(1, 0), twin)
+    go("t3", 9, part(2, 1), part(2, 1), twin)
+    copies["1b"].wait_recv()
+    go("t1", 7, part(1, 1), part(1, 1), twin)
+    copies["2a"].wait_recv()
+    go("t2", 8, part(2, 0), part(2, 0), twin)
+    copies["3a"].wait_recv()
+    go("t4", 10, part(3, 0), part(3, 0), twin)
+    copies["3b"].wait_recv()
+    go("t5", 11, part(3, 1), part(3, 1), twin)
+    for i in range(6):
+        copies["t%d" % i].wait_recv()
+    for c in copies.values():
+        c.wait_send()
+    own.wait()
+
+
+def share_rows(h, ident):
+    rows, width = h.shape
+    return pl.pallas_call(
+        share_rows_kernel,
+        out_shape=jax.ShapeDtypeStruct((GROUP * rows, width), h.dtype),
+        in_specs=[WHOLE],
+        out_specs=ANY,
+        scratch_shapes=[
+            pltpu.SemaphoreType.DMA((12,)),
+            pltpu.SemaphoreType.DMA((12,)),
+            pltpu.SemaphoreType.DMA,
+        ],
+        compiler_params=pltpu.CompilerParams(collective_id=ident, has_side_effects=True),
+        name="share_rows",
+    )(h)
+
+
+def share_weights_kernel(n, *refs):
+    owns, outs, helds, (send, recv, local) = refs[:n], refs[n : 2 * n], refs[2 * n : 3 * n], refs[3 * n :]
+    z, p, core, one, two, _ = places()
+    x, y = (z, one, core), (z, two, core)
+    half = owns[0].shape[0] // 2
+    low, high = pl.ds(0, half), pl.ds(half, half)
+    loads = [pltpu.make_async_copy(owns[i], helds[i], local.at[0, i]) for i in range(n)]
+    stores = [pltpu.make_async_copy(helds[i], outs[i].at[:, p], local.at[1, i]) for i in range(n)]
+    for load in loads:
+        load.start()
+    meet([x, y])
+    copies = {}
+
+    def go(i, c, src, dst, partner):
+        copies[i, c] = to(src, dst, send.at[i, c], recv.at[i, c], partner)
+        copies[i, c].start()
+
+    for i in range(n):
+        own, out = owns[i], outs[i]
+        go(i, 0, own.at[low], out.at[low, p], x)
+        go(i, 1, own.at[high], out.at[high, p], y)
+        go(i, 2, own.at[high], out.at[high, p], x)
+        go(i, 3, own.at[low], out.at[low, p], y)
+    for i in range(n):
+        loads[i].wait()
+        stores[i].start()
+    for i in range(n):
+        copies[i, 0].wait_recv()
+        go(i, 4, outs[i].at[low, one], outs[i].at[low, one], y)
+        copies[i, 1].wait_recv()
+        go(i, 5, outs[i].at[high, two], outs[i].at[high, two], x)
+    for (_, c), copy in copies.items():
+        if c > 1:
+            copy.wait_recv()
+    for copy in copies.values():
+        copy.wait_send()
+    for store in stores:
+        store.wait()
+
+
+def share_weights(lines, ident):
+    depth = lax.axis_size("line")
+    n = len(lines)
+    each = lines[0].shape[0] // depth
+    outs = pl.pallas_call(
+        functools.partial(share_weights_kernel, n),
+        out_shape=[
+            jax.ShapeDtypeStruct((depth, GROUP, each, v.shape[1]), v.dtype) for v in lines
+        ],
+        in_specs=[ANY] * n,
+        out_specs=[ANY] * n,
+        scratch_shapes=[pltpu.VMEM((depth, each, v.shape[1]), v.dtype) for v in lines]
+        + [
+            pltpu.SemaphoreType.DMA((n, 6)),
+            pltpu.SemaphoreType.DMA((n, 6)),
+            pltpu.SemaphoreType.DMA((2, n)),
+        ],
+        compiler_params=pltpu.CompilerParams(collective_id=ident, has_side_effects=True),
+        name="share_weights",
+    )(*[v.reshape(depth, each, v.shape[1]) for v in lines])
+    return [v.reshape(depth * GROUP * each, v.shape[3]) for v in outs]
+
+
+TILE = 256
+
+
+def sum_rows_kernel(sizes, *refs):
+    pairs = sum(sizes)
+    ins, outs = refs[: 2 * pairs], refs[2 * pairs : 2 * pairs + len(sizes)]
+    refs = refs[2 * pairs + len(sizes) :]
+    mines, others, refs = refs[:pairs], refs[pairs : 2 * pairs], refs[2 * pairs :]
+    left, total, give, take, packed, from_x, from_y, diag_x, diag_y, send, recv, local = refs
+    z, p, core, one, two, _ = places()
+    rows, wide = outs[0].shape
+    half = rows // 2
+    x, y, twin = (z, one, core), (z, two, core), (z, p, 1 - core)
+    firsts = [sum(sizes[:j]) for j in range(len(sizes))]
+    steps = [(j, k) for j in range(len(sizes)) for k in (3, 1, 2, 0)]
+    mine = pl.ds(pl.multiple_of(core * wide, wide), wide)
+    other = pl.ds(pl.multiple_of((1 - core) * wide, wide), wide)
+    loads, copies = {}, {}
+
+    def load(name, i, src, dst):
+        loads[name] = pltpu.make_async_copy(src, dst, local.at[i])
+        loads[name].start()
+
+    def load_left(t):
+        j, k = steps[t]
+        for i in range(sizes[j]):
+            load(
+                ("l", t, i),
+                2 * pairs + t * max(sizes) + i,
+                ins[2 * (firsts[j] + i)].at[pl.ds(k * rows, rows)],
+                left.at[t % 2, i],
+            )
+
+    def load_right(kind, j, where, buffers):
+        for i in range(firsts[j], firsts[j] + sizes[j]):
+            load((kind, i), i + (pairs if kind == "m" else 0), ins[2 * i + 1].at[where], buffers[i])
+
+    load_right("o", 0, other, others)
+    load_left(0)
+    load_right("m", 0, mine, mines)
+    load_left(1)
+    for j in range(1, len(sizes)):
+        load_right("o", j, other, others)
+        load_right("m", j, mine, mines)
+    meet([x, y, twin])
+
+    def go(name, j, i, src, dst, partner):
+        copies[name, j] = to(src, dst, send.at[j, i], recv.at[j, i], partner)
+        copies[name, j].start()
+
+    def product(t, rights, store):
+        j, _ = steps[t]
+
+        def step(i, carry):
+            at = pl.ds(pl.multiple_of(i * TILE, TILE), TILE)
+            value = mat_nt(left[t % 2, 0], rights[firsts[j]][at, :])
+            for n in range(1, sizes[j]):
+                value = value + mat_nt(left[t % 2, n], rights[firsts[j] + n][at, :])
+            store(at, value)
+            return carry
+
+        lax.fori_loop(0, wide // TILE, step, 0)
+
+    def slot(t):
+        j, k = steps[t]
+        return t % 2 if k else 2 + j
+
+    def away(t):
+        j, k = steps[t]
+        if t >= 2:
+            copies[("t", steps[t - 2][1]), steps[t - 2][0]].wait_send()
+
+        def store(at, value):
+            give[t % 2, :, at] = value.astype(BF)
+
+        product(t, others, store)
+        go(("t", k), j, k, give.at[t % 2], take.at[j, k], twin)
+
+    def here(t):
+        def store(at, value):
+            total[slot(t), :, at] = value
+
+        product(t, mines, store)
+
+    low, high = pl.ds(0, half), pl.ds(half, half)
+
+    def term(t, at):
+        j, k = steps[t]
+        return total[slot(t), at, :] + take[j, k, at, :].astype(F32)
+
+    def finish(t):
+        j, k = steps[t]
+        copies[("t", k), j].wait_recv()
+        if k == 3:
+            packed[j, 0] = term(t, pl.ds(0, rows)).astype(BF)
+            go("3a", j, 4, packed.at[j, 0, low], diag_y.at[j], y)
+            go("3b", j, 5, packed.at[j, 0, high], diag_x.at[j], x)
+        elif k == 1:
+            packed[j, 1, high, :] = term(t, high).astype(BF)
+            go("1b", j, 6, packed.at[j, 1, high], from_x.at[j, high], x)
+            value = term(t, low)
+            packed[j, 1, low, :] = value.astype(BF)
+        elif k == 2:
+            packed[j, 2, low, :] = term(t, low).astype(BF)
+            go("2a", j, 8, packed.at[j, 2, low], from_y.at[j, low], y)
+            packed[j, 2, high, :] = term(t, high).astype(BF)
+
+    def relay_x(j):
+        copies["3a", j].wait_recv()
+        packed[j, 1, low, :] = (packed[j, 1, low, :].astype(F32) + diag_y[j].astype(F32)).astype(BF)
+        go("1a", j, 7, packed.at[j, 1, low], from_x.at[j, low], x)
+
+    def relay_y(j):
+        copies["3b", j].wait_recv()
+        packed[j, 2, high, :] = (packed[j, 2, high, :].astype(F32) + diag_x[j].astype(F32)).astype(BF)
+        go("2b", j, 9, packed.at[j, 2, high], from_y.at[j, high], y)
+
+    def wait(kind, j):
+        for i in range(firsts[j], firsts[j] + sizes[j]):
+            loads[kind, i].wait()
+
+    for t, (j, k) in enumerate(steps):
+        for i in range(sizes[j]):
+            loads["l", t, i].wait()
+        if k == 3:
+            wait("o", j)
+        away(t)
+        if k == 3:
+            wait("m", j)
+        if k in (1, 2, 0):
+            finish(t - 1)
+        if k == 0:
+            relay_x(j)
+        if k == 3 and j:
+            relay_y(j - 1)
+        here(t)
+        if t + 2 < len(steps):
+            load_left(t + 2)
+    relay_y(len(sizes) - 1)
+    for j in range(len(sizes)):
+        copies[("t", 0), j].wait_recv()
+        for name in ("1a", "1b", "2a", "2b"):
+            copies[name, j].wait_recv()
+        outs[j][...] = (
+            term(4 * j + 3, pl.ds(0, rows)) + from_x[j].astype(F32) + from_y[j].astype(F32)
+        )
+    waited = {(("t", steps[t][1]), steps[t][0]) for t in range(len(steps) - 2)}
+    for name, copy in copies.items():
+        if name not in waited:
+            copy.wait_send()
+
+
+def sum_rows(sums, ident):
+    sizes = tuple(len(pairs) for pairs in sums)
+    flat = [v for pairs in sums for pair in pairs for v in pair]
+    rows = flat[0].shape[0] // GROUP
+    units = flat[0].shape[1]
+    wide = flat[1].shape[0] // 2
+    n, m = sum(sizes), len(sizes)
+    return pl.pallas_call(
+        functools.partial(sum_rows_kernel, sizes),
+        out_shape=[jax.ShapeDtypeStruct((rows, wide), F32)] * m,
+        in_specs=[ANY] * (2 * n),
+        out_specs=[WHOLE] * m,
+        scratch_shapes=[pltpu.VMEM((wide, units), BF)] * (2 * n)
+        + [
+            pltpu.VMEM((2, max(sizes), rows, units), BF),
+            pltpu.VMEM((2 + m, rows, wide), F32),
+            pltpu.VMEM((2, rows, wide), BF),
+            pltpu.VMEM((m, GROUP, rows, wide), BF),
+            pltpu.VMEM((m, 3, rows, wide), BF),
+            pltpu.VMEM((m, rows, wide), BF),
+            pltpu.VMEM((m, rows, wide), BF),
+            pltpu.VMEM((m, rows // 2, wide), BF),
+            pltpu.VMEM((m, rows // 2, wide), BF),
+            pltpu.SemaphoreType.DMA((m, 10)),
+            pltpu.SemaphoreType.DMA((m, 10)),
+            pltpu.SemaphoreType.DMA((2 * n + 4 * m * max(sizes),)),
+        ],
+        compiler_params=pltpu.CompilerParams(
+            collective_id=ident, has_side_effects=True, vmem_limit_bytes=58 << 20
+        ),
+        name="sum_rows",
+    )(*flat)
+
+
+WIDTH = 512
+
+
+def finish_kernel(
+    g_out, g_qkv, sum_0, sum_1, sum_d, slots, gain_terms,
+    new_qkv, new_out, new_gate, new_up, new_down, new_gain, norm, back,
+    own, to_x, to_y, diag_x, diag_y, from_x, from_y, add_x, add_y, sums, packed, line,
+    ffn, gain_got, shares,
+    send, recv, local, row_send, row_recv, ends, keeps, unit_send, unit_recv, unit_local, all_send, all_recv,
+):
+    z, p, core, one, two, three = places()
+    depth, _, each, _ = g_out.shape
+    count = slots.shape[0]
+    wide = slots.shape[2] // 2
+    units = sum_d.shape[1]
+    span = units // 2
+    me = z * GROUP + p
+    half = depth // 2
+    low, high = pl.ds(0, half), pl.ds(half, half)
+    x, y, twin = (z, one, core), (z, two, core), (z, p, 1 - core)
+    column = [(lax.rem(z + s, depth), p, core) for s in range(1, depth)]
+    columns = pl.ds(pl.multiple_of(core * wide, wide), wide)
+    places_of = [(g, c) for g in (g_out, g_qkv) for c in range(g.shape[3] // WIDTH)]
+    chunks = len(places_of)
+
+    def source(rows, q, c):
+        g, at = places_of[c]
+        return g.at[rows, q, :, pl.ds(at * WIDTH, WIDTH)]
+
+    loads = []
+    for c in range(chunks):
+        loads.append(pltpu.make_async_copy(source(pl.ds(0, depth), p, c), own.at[c], local.at[0, c]))
+        loads.append(pltpu.make_async_copy(source(low, one, c), to_x.at[c], local.at[1, c]))
+        loads.append(pltpu.make_async_copy(source(high, two, c), to_y.at[c], local.at[2, c]))
+    for load in loads:
+        load.start()
+
+    def partner(s):
+        t = lax.rem(me + s, count)
+        return t, (t // GROUP, lax.rem(t, GROUP), core)
+
+    def anyone(s):
+        t = lax.rem(me * 2 + core + s, 2 * count)
+        return (t // (2 * GROUP), lax.rem(t // 2, GROUP), lax.rem(t, 2))
+
+    barrier = pltpu.get_barrier_semaphore()
+
+    def greet(s, carry):
+        pl.semaphore_signal(barrier, inc=1, device_id=anyone(s), device_id_type=MESH)
+        return carry
+
+    lax.fori_loop(1, 2 * count, greet, 0)
+    keep = [
+        pltpu.make_async_copy(
+            slots.at[me, :, pl.ds(i * wide, wide)], back.at[i, me, :, columns], keeps.at[i]
+        )
+        for i in range(2)
+    ] + [pltpu.make_async_copy(gain_terms.at[me], gain_got.at[me], keeps.at[2])]
+    for copy in keep:
+        copy.start()
+
+    def unit_parts(q, of):
+        rows = pl.ds(pl.multiple_of(q * each, each), each)
+
+        def place(i, shift, size):
+            return ffn.at[i, :, pl.ds(pl.multiple_of(of * units + shift, span), size)]
+
+        return [
+            (sum_0.at[rows, pl.ds(0, span)], place(0, 0, span)),
+            (sum_0.at[rows, pl.ds(span, span)], place(1, 0, span)),
+            (sum_1.at[rows, pl.ds(0, span)], place(0, span, span)),
+            (sum_1.at[rows, pl.ds(span, span)], place(1, span, span)),
+            (sum_d.at[rows], place(2, 0, units)),
+        ]
+
+    stay = [
+        pltpu.make_async_copy(src, dst, unit_local.at[i])
+        for i, (src, dst) in enumerate(unit_parts(p, p))
+    ]
+    for copy in stay:
+        copy.start()
+    pl.semaphore_wait(barrier, 2 * count - 1)
+    copies = {}
+
+    def rows(s, kinds):
+        t, who = partner(s)
+        made = []
+        for i in kinds:
+            if i < 2:
+                src, dst = slots.at[t, :, pl.ds(i * wide, wide)], back.at[i, me, :, columns]
+            else:
+                src, dst = gain_terms.at[t], gain_got.at[me]
+            made.append(to(src, dst, row_send.at[i, s], row_recv.at[i, s], who))
+        return made
+
+    def each_row(act):
+        def step(s, carry):
+            for copy in rows(s, (0, 1, 2)):
+                act(copy)
+            return carry
+
+        lax.fori_loop(1, count, step, 0)
+
+    def go(name, c, i, src, dst, who):
+        copies[name, c] = to(src, dst, send.at[c, i], recv.at[c, i], who)
+        copies[name, c].start()
+
+    def first(c):
+        go("3a", c, 0, source(low, three, c), diag_y.at[c], y)
+        go("3b", c, 1, source(high, three, c), diag_x.at[c], x)
+        go("1b", c, 2, source(high, one, c), from_x.at[c, high], x)
+        go("2a", c, 3, source(low, two, c), from_y.at[c, low], y)
+
+    def relay(c):
+        copies["3a", c].wait_recv()
+        add_x[c] = (to_x[c].astype(F32) + diag_y[c].astype(F32)).astype(BF)
+        go("1a", c, 4, add_x.at[c], from_x.at[c, low], x)
+        copies["3b", c].wait_recv()
+        add_y[c] = (to_y[c].astype(F32) + diag_x[c].astype(F32)).astype(BF)
+        go("2b", c, 5, add_y.at[c], from_y.at[c, high], y)
+
+    def along(c):
+        for name in ("1a", "1b", "2a", "2b"):
+            copies[name, c].wait_recv()
+        sums[c] = own[c].astype(F32) + from_x[c].astype(F32) + from_y[c].astype(F32)
+        packed[c] = sums[c].astype(BF)
+        for s, who in enumerate(column, 1):
+            go(s, c, 5 + s, packed.at[c, who[0]], line.at[c, s - 1], who)
+
+    first(0)
+    each_row(lambda copy: copy.start())
+    first(1)
+    shared = []
+    for k, q in ((3, three), (1, one), (2, two)):
+        for i, (src, dst) in enumerate(unit_parts(q, p)):
+            copy = to(src, dst, unit_send.at[k, i], unit_recv.at[k, i], (z, q, core))
+            copy.start()
+            shared.append(copy)
+    for load in loads:
+        load.wait()
+    for c in range(chunks):
+        relay(c)
+        if c + 2 < chunks:
+            first(c + 2)
+        if c:
+            along(c - 1)
+    for copy in keep:
+        copy.wait()
+    each_row(lambda copy: copy.wait_recv())
+    pass_on = to(
+        back.at[:, :, :, columns], back.at[:, :, :, columns], ends.at[0], ends.at[1], twin
+    )
+    pass_on.start()
+    along(chunks - 1)
+
+    def squares(value):
+        return jnp.sum(jnp.sum(value * value, axis=0, keepdims=True), axis=1, keepdims=True)
+
+    for copy in stay:
+        copy.wait()
+    for copy in shared:
+        copy.wait_recv()
+    total = jnp.zeros((1, 1), F32)
+    for i, ref in ((0, new_gate), (1, new_up)):
+        for at in range(0, ref.shape[1], WIDTH):
+            value = ffn[i, :, at : at + WIDTH].astype(F32)
+            total = total + squares(value)
+            ref[:, at : at + WIDTH] = value
+    for at in range(0, new_down.shape[0], 128):
+        value = ffn[2, :, at : at + 128].astype(F32)
+        total = total + squares(value)
+        new_down[at : at + 128, :] = value.T
+    gain = gain_got[0]
+    for t in range(1, count):
+        gain = gain + gain_got[t]
+    new_gain[...] = gain
+    total = total + 0.5 * squares(gain[:2])
+    for c in range(chunks):
+        value = sums[c, z]
+        for s in range(1, depth):
+            copies[s, c].wait_recv()
+            value = value + line[c, s - 1].astype(F32)
+        total = total + squares(value)
+        g, at = places_of[c]
+        if g is g_qkv:
+            new_qkv[:, pl.ds(at * WIDTH, WIDTH)] = value
+        else:
+            for i in range(0, WIDTH, 128):
+                new_out[pl.ds(at * WIDTH + i, 128), :] = value[:, i : i + 128].T
+    shares[0] = jnp.broadcast_to(total, (8, 128))
+
+    def tell(s):
+        return to(shares.at[0], shares.at[s], all_send.at[s], all_recv.at[s], anyone(s))
+
+    def tell_start(s, carry):
+        tell(s).start()
+        return carry
+
+    def tell_end(s, carry):
+        tell(s).wait_recv()
+        return carry
+
+    def tell_left(s, carry):
+        tell(s).wait_send()
+        return carry
+
+    lax.fori_loop(1, 2 * count, tell_start, 0)
+    lax.fori_loop(1, 2 * count, tell_end, 0)
+    everyone = jnp.sum(shares[...], axis=0)
+    norm[...] = jnp.sqrt(everyone)
+    lax.fori_loop(1, 2 * count, tell_left, 0)
+    pass_on.wait_recv()
+    for copy in [*copies.values(), *shared]:
+        copy.wait_send()
+    each_row(lambda copy: copy.wait_send())
+    pass_on.wait_send()
+
+
+def finish(g_out, g_qkv, sum_0, sum_1, sum_d, slots, gain_terms, ident):
+    depth = lax.axis_size("line")
+    each = g_qkv.shape[0] // (depth * GROUP)
+    units = sum_d.shape[1]
+    chunks = (g_out.shape[1] + g_qkv.shape[1]) // WIDTH
+    count, per, both = slots.shape
+
+    def buffer(rows, dtype=BF):
+        return pltpu.VMEM((chunks, rows, each, WIDTH), dtype)
+
+    return pl.pallas_call(
+        finish_kernel,
+        out_shape=[
+            jax.ShapeDtypeStruct((each, g_qkv.shape[1]), F32),
+            jax.ShapeDtypeStruct((g_out.shape[1], each), F32),
+            jax.ShapeDtypeStruct((each, GROUP * units), F32),
+            jax.ShapeDtypeStruct((each, GROUP * units), F32),
+            jax.ShapeDtypeStruct((GROUP * units, each), F32),
+            jax.ShapeDtypeStruct(gain_terms.shape[1:], F32),
+            jax.ShapeDtypeStruct((8, 128), F32),
+            jax.ShapeDtypeStruct((2, count, per, both), BF),
+        ],
+        in_specs=[ANY] * 5 + [WHOLE] * 2,
+        out_specs=[WHOLE] * 7 + [ANY],
+        scratch_shapes=[
+            buffer(depth),
+            buffer(depth // 2),
+            buffer(depth // 2),
+            buffer(depth // 2),
+            buffer(depth // 2),
+            buffer(depth),
+            buffer(depth),
+            buffer(depth // 2),
+            buffer(depth // 2),
+            buffer(depth, F32),
+            buffer(depth),
+            buffer(depth - 1),
+            pltpu.VMEM((3, each, GROUP * units), BF),
+            pltpu.VMEM(gain_terms.shape, F32),
+            pltpu.VMEM((2 * count, 8, 128), F32),
+            pltpu.SemaphoreType.DMA((chunks, 5 + depth)),
+            pltpu.SemaphoreType.DMA((chunks, 5 + depth)),
+            pltpu.SemaphoreType.DMA((3, chunks)),
+            pltpu.SemaphoreType.DMA((3, count)),
+            pltpu.SemaphoreType.DMA((3, count)),
+            pltpu.SemaphoreType.DMA((2,)),
+            pltpu.SemaphoreType.DMA((3,)),
+            pltpu.SemaphoreType.DMA((4, 5)),
+            pltpu.SemaphoreType.DMA((4, 5)),
+            pltpu.SemaphoreType.DMA((5,)),
+            pltpu.SemaphoreType.DMA((2 * count,)),
+            pltpu.SemaphoreType.DMA((2 * count,)),
+        ],
+        compiler_params=pltpu.CompilerParams(
+            collective_id=ident, has_side_effects=True, vmem_limit_bytes=58 << 20
+        ),
+        name="finish",
+    )(
+        g_out.reshape(depth, GROUP, each, -1),
+        g_qkv.reshape(depth, GROUP, each, -1),
+        sum_0,
+        sum_1,
+        sum_d,
+        slots,
+        gain_terms,
+    )
+
+
+def deal_kernel(sent, pieces, gains, tokens, cots, units, all_gains, held, send, recv, ends, local):
+    z, p, core, one, two, three = places()
+    count, per, both = sent.shape
+    wide = both // 2
+    me = z * GROUP + p
+    cols = pl.ds(pl.multiple_of(core * wide, wide), wide)
+    twin = (z, p, 1 - core)
+
+    def partner(s):
+        t = lax.rem(me + s, count)
+        return t, (t // GROUP, lax.rem(t, GROUP), core)
+
+    barrier = pltpu.get_barrier_semaphore()
+
+    def greet(s, carry):
+        pl.semaphore_signal(barrier, inc=1, device_id=partner(s)[1], device_id_type=MESH)
+        return carry
+
+    lax.fori_loop(1, count, greet, 0)
+    pl.semaphore_signal(barrier, inc=1, device_id=twin, device_id_type=MESH)
+    mine = pltpu.make_async_copy(pieces.at[p], held, local.at[0])
+    mine.start()
+    keep = [
+        pltpu.make_async_copy(sent.at[me, :, pl.ds(0, wide)], tokens.at[me, :, cols], local.at[1]),
+        pltpu.make_async_copy(sent.at[me, :, pl.ds(wide, wide)], cots.at[me], local.at[2]),
+        pltpu.make_async_copy(gains, all_gains.at[me], local.at[3]),
+    ]
+    for copy in keep:
+        copy.start()
+    pl.semaphore_wait(barrier, count)
+
+    def rows(s):
+        t, who = partner(s)
+        return (
+            to(sent.at[t, :, pl.ds(0, wide)], tokens.at[me, :, cols], send.at[0, s], recv.at[0, s], who),
+            to(sent.at[t, :, pl.ds(wide, wide)], cots.at[me], send.at[1, s], recv.at[1, s], who),
+            to(gains, all_gains.at[me], send.at[2, s], recv.at[2, s], who),
+        )
+
+    def start(i):
+        def step(s, carry):
+            rows(s)[i].start()
+            return carry
+
+        lax.fori_loop(1, count, step, 0)
+
+    start(0)
+    start(2)
+    shares = [
+        to(pieces.at[q], units.at[:, p], ends.at[0, k], ends.at[1, k], (z, q, core))
+        for k, q in ((1, one), (2, two), (3, three))
+    ]
+    for copy in shares:
+        copy.start()
+    start(1)
+    mine.wait()
+    store = pltpu.make_async_copy(held, units.at[:, p], local.at[4])
+    store.start()
+    keep[0].wait()
+
+    def arrived(i):
+        def step(s, carry):
+            rows(s)[i].wait_recv()
+            return carry
+
+        lax.fori_loop(1, count, step, 0)
+
+    arrived(0)
+    pass_on = to(tokens.at[:, :, cols], tokens.at[:, :, cols], ends.at[0, 0], ends.at[1, 0], twin)
+    pass_on.start()
+    arrived(2)
+    for copy in shares:
+        copy.wait_recv()
+    arrived(1)
+    pass_on.wait_recv()
+
+    def leave(s, carry):
+        for copy in rows(s):
+            copy.wait_send()
+        return carry
+
+    lax.fori_loop(1, count, leave, 0)
+    for copy in [*shares, pass_on]:
+        copy.wait_send()
+    keep[1].wait()
+    keep[2].wait()
+    store.wait()
+
+
+def deal(sent, pieces, gains, ident):
+    count, per, both = sent.shape
+    _, three, rows, units = pieces.shape
+    return pl.pallas_call(
+        deal_kernel,
+        out_shape=[
+            jax.ShapeDtypeStruct((count, per, both), BF),
+            jax.ShapeDtypeStruct((count, per, both // 2), BF),
+            jax.ShapeDtypeStruct((three, GROUP, rows, units), BF),
+            jax.ShapeDtypeStruct((count, *gains.shape), F32),
+        ],
+        in_specs=[WHOLE, ANY, WHOLE],
+        out_specs=[ANY] * 4,
+        scratch_shapes=[
+            pltpu.VMEM((three, rows, units), BF),
+            pltpu.SemaphoreType.DMA((3, count)),
+            pltpu.SemaphoreType.DMA((3, count)),
+            pltpu.SemaphoreType.DMA((2, 4)),
+            pltpu.SemaphoreType.DMA((5,)),
+        ],
+        compiler_params=pltpu.CompilerParams(collective_id=ident, has_side_effects=True),
+        name="deal",
+    )(sent, pieces, gains)
+
+
 class Ways:
     def __init__(self):
         self.depth = lax.axis_size("line")
@@ -97,9 +838,7 @@
         return lax.all_gather(value, "line", axis=0, tiled=True)
 
     def scatter_line(self, whole):
-        return lax.psum_scatter(
-            whole.astype(BF), "line", scatter_dimension=0, tiled=True
-        ).astype(F32)
+        return lax.psum_scatter(whole, "line", scatter_dimension=0, tiled=True)
 
     def gather_group(self, value):
         half = value.shape[0] // 2
@@ -115,26 +854,6 @@
         two = jnp.concatenate([parts[2][:half], parts[2][half:] + second]).astype(BF)
         return parts[0] + self.flip(one, 1).astype(F32) + self.flip(two, 2).astype(F32)
 
-    def spread_units(self, shards):
-        rows, units = shards[0].shape[0], shards[0].shape[1] // GROUP
-        send = jnp.stack(
-            [
-                jnp.concatenate([s[:, j * units : (j + 1) * units] for s in shards])
-                for j in range(GROUP)
-            ]
-        )
-        got = lax.all_to_all(send, "group", split_axis=0, concat_axis=0, tiled=True)
-        return got.reshape(GROUP, len(shards), rows, units).swapaxes(0, 1).reshape(
-            len(shards), GROUP * rows, units
-        )
-
-    def collect_units(self, whole):
-        rows = whole.shape[0] // GROUP
-        got = lax.all_to_all(
-            whole.astype(BF), "group", split_axis=0, concat_axis=0, tiled=True
-        ).astype(F32)
-        return jnp.concatenate([got[j * rows : (j + 1) * rows] for j in range(GROUP)], axis=1)
-
     def exchange(self, value):
         return lax.all_to_all(value, ("line", "group"), split_axis=0, concat_axis=0, tiled=True)
 
@@ -152,6 +871,22 @@
             jnp.concatenate([mine, other], axis=-1),
             jnp.concatenate([other, mine], axis=-1),
         )
+
+
+def unit_pieces(down, gate, upper):
+    units = down.shape[1] // GROUP
+    half = units // 2
+
+    def cut(j, c):
+        at = slice(j * units + c * half, j * units + (c + 1) * half)
+        return jnp.concatenate([gate[:, at], upper[:, at]], axis=1)
+
+    return jnp.stack(
+        [
+            jnp.stack([down[:, j * units : (j + 1) * units], cut(j, 0), cut(j, 1)])
+            for j in range(GROUP)
+        ]
+    )
 
 
 def deal_tables(token_order, me, rows):
@@ -209,39 +944,33 @@
     line_qkv = line_all[:, : shard_qkv.shape[1]]
     line_out = line_all[:, shard_qkv.shape[1] :]
 
-    def natural(line):
-        count, cols = ways.depth, line.shape[1]
-        each = line.shape[0] // count
-        whole = jnp.zeros((count, GROUP, each, cols), line.dtype)
-        for k, part in enumerate(ways.gather_group(line)):
-            whole = lax.dynamic_update_slice(
-                whole, part.reshape(count, 1, each, cols), (0, ways.p ^ k, 0, 0)
-            )
-        return whole.reshape(count * GROUP * each, cols)
-
     into, out = deal_tables(token_order, me, rows)
-    sent_tokens = mat_nn(out, ways.own_half(tokens)).astype(BF)
-    sent_cot = mat_nn(out, ways.own_half(cotangent)).astype(BF)
-    gains = jnp.stack([gain_attn, gain_ffn]).astype(BF)
-    all_gains = ways.exchange(
-        jnp.broadcast_to(gains[None], (ways.n, 2, gains.shape[1]))
-    ).astype(F32)
+    sent = mat_nn(
+        out, jnp.concatenate([ways.own_half(tokens), ways.own_half(cotangent)], axis=1)
+    ).astype(BF)
+    pieces = unit_pieces(w_down.astype(BF).T, w_gate.astype(BF), w_up.astype(BF))
+    gains = jnp.pad(
+        jnp.stack([gain_attn, gain_ffn]).astype(BF).astype(F32), ((0, 6), (0, 0))
+    )
+    got_tokens, got_cot, units, all_gains = deal(
+        sent.reshape(ways.n, rows // ways.n, width), pieces, gains, 5
+    )
     gain_a = all_gains[:, 0].reshape(width)
     gain_f = all_gains[:, 1].reshape(width)
-    half_tokens = mat_nn(into, ways.exchange(sent_tokens)).astype(BF)
-    dealt = ways.join(half_tokens, ways.swap(half_tokens))
-    weight_qkv = natural(line_qkv)
-    weight_out = natural(after(line_out, weight_qkv))
-    half_cot = mat_nn(into, ways.exchange(after(sent_cot, weight_qkv))).astype(BF)
+    dealt = mat_nn(into, got_tokens.reshape(rows, width)).astype(BF)
+    half_cot = mat_nn(into, got_cot.reshape(rows, width // 2)).astype(BF)
+
+    weight_qkv, weight_out = share_weights([line_qkv, line_out], 4)
     wide_q = w_query.shape[1]
     wide_k = key_weight.shape[1]
     query_w = weight_qkv[:, :wide_q]
     key_w = weight_qkv[:, wide_q : wide_q + wide_k]
     value_w = weight_qkv[:, wide_q + wide_k :]
 
-    units = ways.spread_units([w_down.astype(BF).T, w_gate.astype(BF), w_up.astype(BF)])
-    line_units = lax.all_gather(units, "line", axis=1, tiled=False)
-    down_t, gate_w, up_w = (line_units[i].reshape(width, -1) for i in range(3))
+    line_units = lax.all_gather(
+        units.reshape(3, -1, units.shape[-1]), "line", axis=1, tiled=False
+    )
+    down_t, first_w, second_w = (line_units[i].reshape(width, -1) for i in range(3))
 
     cot_parts = jnp.concatenate(ways.gather_group(after(half_cot, weight_out)))
     group_cot = ways.join(cot_parts, ways.swap(cot_parts))
@@ -284,36 +1013,36 @@
     normed2, scale2 = normalize(middle)
     hidden2 = (normed2 * gain_f).astype(BF)
 
-    parts = jnp.concatenate(ways.gather_group(ways.own_half(hidden2)))
-    group_h2 = ways.join(parts, ways.swap(parts))
+    group_h2 = share_rows(hidden2, 1)
     grad_inner = mat_nn(group_cot, down_t)
-    gate = mat_nn(group_h2, gate_w)
-    upper = mat_nn(group_h2, up_w)
-    sigma = jax.nn.sigmoid(gate)
-    activ = gate * sigma
-    inner = (activ * upper).astype(BF)
-    grad_gate = (grad_inner * upper * (sigma * (1.0 + gate * (1.0 - sigma)))).astype(BF)
-    grad_up = (grad_inner * activ).astype(BF)
-
-    def token_sum(terms):
-        other = ways.swap(ways.other_half(terms).astype(BF)).astype(F32)
-        whole = ways.own_half(terms) + other
-        return ways.scatter_group([whole[k * rows : (k + 1) * rows] for k in range(GROUP)])
-
-    half_dh2 = token_sum(mat_nt(grad_gate, gate_w) + mat_nt(grad_up, up_w))
-    sum_wd = ways.scatter_line(mat_tn(group_cot, inner))
-    sum_wg = ways.scatter_line(mat_tn(group_h2, grad_gate))
-    sum_wu = ways.scatter_line(mat_tn(group_h2, grad_up))
-    half_result = ways.own_half(middle) + token_sum(mat_nt(inner, down_t))
-
-    def give_back(half):
-        slots = mat_tn(into, half.astype(BF)).astype(BF)
-        back = mat_tn(out, ways.exchange(slots)).astype(BF)
-        return ways.join(back, ways.swap(back))
-
-    activations = give_back(half_result)
-
-    grad_h2 = ways.join(half_dh2, ways.swap(half_dh2))
+    span = grad_inner.shape[1] // 2
+
+    def units_half(group_rows, weight, grad_inner):
+        both = mat_nn(group_rows, weight)
+        gate, upper = both[:, :span], both[:, span:]
+        sigma = jax.nn.sigmoid(gate)
+        activ = gate * sigma
+        inner = (activ * upper).astype(BF)
+        slope = sigma * (1.0 + gate * (1.0 - sigma))
+        grads = jnp.concatenate([grad_inner * upper * slope, grad_inner * activ], axis=1)
+        return inner, grads.astype(BF)
+
+    inner_0, grads_0 = units_half(group_h2, first_w, grad_inner[:, :span])
+    terms_0 = mat_tn(group_h2, grads_0).astype(BF)
+    sum_0 = ways.scatter_line(terms_0)
+    inner_1, grads_1 = units_half(after(group_h2, terms_0), second_w, grad_inner[:, span:])
+    inner = jnp.concatenate([inner_0, inner_1], axis=1)
+    terms_d = mat_tn(group_cot, inner).astype(BF)
+    sum_d = ways.scatter_line(terms_d)
+    half_dh2, half_ffn = sum_rows(
+        [[(grads_0, first_w), (after(grads_1, terms_d), second_w)], [(inner, down_t)]], 2
+    )
+    terms_1 = mat_tn(after(group_h2, half_dh2), grads_1).astype(BF)
+    sum_1 = ways.scatter_line(terms_1)
+    half_dh2 = after(half_dh2, terms_1)
+    half_result = ways.own_half(middle) + half_ffn
+
+    grad_h2 = ways.join(half_dh2, ways.swap(half_dh2)) + 0.0 * sum_0[0, 0].astype(F32)
     grad_gf = jnp.sum(grad_h2 * normed2, axis=0)
     grad_mid = dealt_cot.astype(F32) + norm_back(grad_h2, normed2, scale2, gain_f)
     mid_low = grad_mid.astype(BF)
@@ -340,48 +1069,37 @@
     grad_k = unrotate(grad_krot, cosine, sine).reshape(rows, heads_kv * HEAD_SIZE).astype(BF)
     grad_v = grad_value.reshape(rows, heads_kv * HEAD_SIZE).astype(BF)
 
-    def attention_sum(terms):
-        count, cols = ways.depth, terms.shape[1]
-        each = terms.shape[0] // (count * GROUP)
-        view = terms.reshape(count, GROUP, each, cols)
-        parts = [
-            lax.dynamic_slice(
-                view, (0, ways.p ^ k, 0, 0), (count, 1, each, cols)
-            ).reshape(count * each, cols)
-            for k in range(GROUP)
-        ]
-        return ways.scatter_line(ways.scatter_group(parts))
-
-    sum_wo = attention_sum(grad_wo)
     grad_qkv = jnp.concatenate([grad_q, grad_k, grad_v], axis=1)
-    sum_qkv = attention_sum(mat_tn(hidden1, grad_qkv))
     part = mat_nt(grad_qkv, weight_qkv)
-    grad_h1 = part + ways.swap(part.astype(BF)).astype(F32)
+    other = ways.swap(part.astype(BF)).astype(F32)
+    terms_qkv = mat_tn(hidden1, grad_qkv).astype(BF)
+    grad_h1 = part + other
     grad_ga = jnp.sum(grad_h1 * normed1, axis=0)
     grad_in = grad_mid + norm_back(grad_h1, normed1, scale1, gain_a)
-    input_grad = give_back(ways.own_half(grad_in))
-
-    gain_grads = jnp.sum(
-        ways.exchange(jnp.stack([grad_ga, grad_gf]).reshape(2, ways.n, -1).swapaxes(0, 1)), axis=0
-    )
+    slots = mat_tn(
+        into, jnp.concatenate([half_result, ways.own_half(grad_in)], axis=1).astype(BF)
+    ).astype(BF)
+    gain_terms = jnp.pad(
+        jnp.stack([grad_ga, grad_gf]).reshape(2, ways.n, -1).swapaxes(0, 1), ((0, 0), (0, 6), (0, 0))
+    )
+    new_qkv, new_out, new_gate, new_up, new_down, new_gain, norm, back = finish(
+        grad_wo.astype(BF), terms_qkv, sum_0, sum_1, sum_d,
+        slots.reshape(ways.n, -1, width), gain_terms, 3,
+    )
+    activations = mat_tn(out, back[0].reshape(rows, width)).astype(BF)
+    input_grad = mat_tn(out, back[1].reshape(rows, width)).astype(BF)
     owned = (
-        gain_grads[0],
-        sum_qkv[:, :wide_q],
-        sum_qkv[:, wide_q : wide_q + wide_k],
-        sum_qkv[:, wide_q + wide_k :],
-        sum_wo.T,
-        gain_grads[1],
-        ways.collect_units(sum_wg),
-        ways.collect_units(sum_wu),
-        ways.collect_units(sum_wd).T,
-    )
-    share = 0.5 * (jnp.sum(owned[0] * owned[0]) + jnp.sum(owned[5] * owned[5]))
-    for k in (1, 2, 3, 4, 6, 7, 8):
-        share = share + jnp.sum(owned[k] * owned[k])
-    axes = ("line", "group", "mp")
-    shares = jnp.broadcast_to(share, (2 * ways.n, 8, 128))
-    shares = lax.all_to_all(shares, axes, split_axis=0, concat_axis=0, tiled=True)
-    grad_norm = jnp.sqrt(jnp.sum(shares[:, 0, 0]))
+        new_gain[0],
+        new_qkv[:, :wide_q],
+        new_qkv[:, wide_q : wide_q + wide_k],
+        new_qkv[:, wide_q + wide_k :],
+        new_out,
+        new_gain[1],
+        new_gate,
+        new_up,
+        new_down,
+    )
+    grad_norm = norm[0, 0]
     factor = jnp.minimum(1.0, math.sqrt(PARAMS) / grad_norm)
     weights = (gain_attn, w_query, key_weight, value_weight, w_out, gain_ffn, w_gate, w_up, w_down)
     moments = (

time: 962 us -> 892 us (0.927)
  Pallas kernels: 0 us -> 513 us
  waiting for transfers between devices: 287 us -> 47.6 us
  matrix products: 238 us -> 133 us
  starting transfers between devices: 92 us -> 5.22 us
  local copies, waits for them, and re-layouts: 161 us -> 81.1 us
  other arithmetic: 149 us -> 90.1 us
    pallas_call x0 -> x5, Pallas kernels: none -> 513 us  [the longest x1 202 us: finish(): pl.pallas_call(finish_kernel, out_shape=[jax.ShapeDtypeStruct((each, g_qk...]
    ppermute x32 -> x4, waiting for transfers between devices: 154 us -> 4.34 us  [flip(): return lax.ppermute(value, 'group', [(i, i ^ k) for i in range(GROUP)])]
    all_to_all x11 -> x0, waiting for transfers between devices: 105 us -> none  [the longest x6 52 us: exchange(): lax.all_to_all(value, ('line', 'group'), split_axis=0, concat_axis=0, til...]
    all_to_all x11 -> x0, starting transfers between devices: 52.3 us -> none  [the longest x6 31.8 us: exchange(): lax.all_to_all(value, ('line', 'group'), split_axis=0, concat_axis=0, til...]
    dot_general x5 -> x2, matrix products: 62.3 us -> 11.9 us  [mat_nt(): lax.dot_general(left, right, (((1,), (1,)), ((), ())), preferred_element_...]
    ppermute x32 -> x4, starting transfers between devices: 38.2 us -> 4.26 us  [flip(): return lax.ppermute(value, 'group', [(i, i ^ k) for i in range(GROUP)])]
    dot_general x12 -> x11, matrix products: 86.4 us -> 54.9 us  [mat_nn(): return jnp.dot(left, right, preferred_element_type=F32)]
    reduce_scatter x5 -> x3, waiting for transfers between devices: 0.03 us -> 26.1 us  [scatter_line(): return lax.psum_scatter(whole, 'line', scatter_dimension=0, tiled=True)]
  transfers between devices with their start and end apart: 60 -> 13, of which waited for: 23 -> 6; matrix products, arithmetic and copies ran while one was open for 45% -> 24% of each run, Pallas kernels for 0% -> 35%
where the time goes in v3:
time: 892 us; the launch traced here: 887 us
  Pallas kernels  513 us (58%)
  matrix products  133 us (15%)
  other arithmetic  90.1 us (10%)
  local copies, waits for them, and re-layouts  81.1 us (9%)
  waiting for transfers between devices  47.6 us (5%)
  between operations  16.7 us (2%)
    pallas_call x1, Pallas kernels, finish(): pl.pallas_call(finish_kernel, out_shape=[jax.ShapeDtypeStruct((each, g_qk...  202 us
    pallas_call x1, Pallas kernels, share_weights(): pl.pallas_call(functools.partial(share_weights_kernel, n), out_shape=[jax...  105 us
    pallas_call x1, Pallas kernels, sum_rows(): pl.pallas_call(functools.partial(sum_rows_kernel, sizes), out_shape=[jax....  86.6 us
    pallas_call x1, Pallas kernels, deal(): pl.pallas_call(deal_kernel, out_shape=[jax.ShapeDtypeStruct((count, per,...  78.3 us
    dot_general x8, matrix products, mat_tn(): lax.dot_general(left, right, (((0,), (0,)), ((), ())), preferred_element_...  57.4 us
    dot_general x11, matrix products, mat_nn(): return jnp.dot(left, right, preferred_element_type=F32)  54.9 us
    pallas_call x1, Pallas kernels, share_rows(): pl.pallas_call(share_rows_kernel, out_shape=jax.ShapeDtypeStruct((GROUP *...  41 us
    unnamed x175, local copies, waits for them, and re-layouts  36.7 us
  transfers between devices with their start and end apart: 13, of which 6 were waited for; matrix products, arithmetic and copies ran while one was open for 24% of the time, Pallas kernels for 35%

profile of v3, /device:TPU:0, one launch (start us, length us, event | category | flops | bytes accessed | tf_op | source)
XLA Modules:
  0.0 886.7 jit_solution(1316462016989589491)
XLA Ops:
  13.6 2.7 convert_element_type.164
  23.2 2.6 convolution_convert_fusion.9
  27.8 78.3 %deal.1 = (bf16[16,32,2048]{2,1,0:T(8,128)(2,1)}, bf16[16,32,1024]{2,1,0:T(8,128)(2,1)}, bf16[3,4,128,1024]{3,2,1,0:T(8,128)(2,1)}, f32[16,8,128]{2,1,0:T(8,128)}) custom-call(bf16[16,32,2048]{2,1,0:T(8,128)(2,1)} %bitcast.181, bf16[4,3,128,1024]{3,2,1,0:T(8,128)(2,1)} %pad_maximum_fusion.3.pieces, f32[8,128]{1,0:T(8,128)} %fusion.66.gains), custom_call_target="tpu_custom_call" | custom-call | tf_op jit(solution)/shard_map/deal/pallas_call | solution.py:800
  107.8 3.1 fusion.11
  114.9 10.0 %all-gather.3.cloned.1.call-done = bf16[512,3072]{0,1:T(8,128)(2,1)} async-done(((bf16[128,3072]{0,1:T(8,128)(2,1)}), bf16[512,3072]{0,1:T(8,128)(2,1)}) %all-gather.3.cloned.1.call-update) | async-done | bytes 3145744 | tf_op jit(solution)/shard_map/all_gather | solution.py:838
  124.9 3.0 slice.278
  128.0 3.9 copy.110
  136.7 105.1 %share_weights.1 = (bf16[4,4,128,2048]{3,2,1,0:T(8,128)(2,1)}, bf16[4,4,128,1024]{3,2,1,0:T(8,128)(2,1)}) custom-call(bf16[4,128,2048]{2,1,0:T(8,128)(2,1)} %bitcast.173, bf16[4,128,1024]{2,1,0:T(8,128)(2,1)} %bitcast.177), custom_call_target="tpu_custom_call" | custom-call | tf_op jit(solution)/shard_map/share_weights/pallas_call | solution.py:217
  243.9 6.0 fusion.12
  249.8 3.2 reshape.298
  253.0 2.9 subtract_convert_fusion.1
  256.0 3.0 fusion.24
  268.6 2.5 fusion.88
  273.6 3.0 fusion.39
  285.8 4.2 collective-permute-done.3
  296.4 4.6 collective-permute-done.5
  306.0 41.0 %share_rows.1 = bf16[2048,2048]{1,0:T(8,128)(2,1)} custom-call(bf16[512,2048]{1,0:T(8,128)(2,1)} %multiply_convert_fusion.6.h), custom_call_target="tpu_custom_call" | custom-call | tf_op jit(solution)/shard_map/share_rows/pallas_call | solution.py:158
  347.0 11.4 %maximum_select_fusion = bf16[2048,2048]{1,0:T(8,128)(2,1)} fusion(bf16[2048,1024]{1,0:T(8,128)(2,1)} %collective-permute-done.4, bf16[2048,1024]{1,0:T(8,128)(2,1)} %constant_dynamic-update-slice_fusion, pred[]{:T(512)S(6)} %eq.93), kind=kLoop, calls=%fused_computation.2 | loop fusion | flops 37748736 | bytes 16777216 | tf_op jit(solution)/shard_map/jit(_where)/select_n | solution.py:869
  358.4 7.4 fusion.81
  367.1 11.2 %fusion.91 = f32[2048,1024]{1,0:T(8,128)} fusion(bf16[2048,2048]{1,0:T(8,128)(2,1)S(1)} %copy-done.11, bf16[2048,1024]{1,0:T(8,128)(2,1)S(1)} %bitcast.168), kind=kOutput, calls=%fused_computation.229 | convolution fusion | flops 8589934592 | bytes 20971520 | tf_op jit(solution)/shard_map/dot_general | solution.py:69
  378.4 9.1 %fusion.92 = f32[2048,1024]{1,0:T(8,128)S(1)} fusion(bf16[2048,2048]{1,0:T(8,128)(2,1)S(1)} %bitcast.171, bf16[2048,1024]{1,0:T(8,128)(2,1)S(1)} %bitcast.166), kind=kOutput, calls=%fused_computation.230 | convolution fusion | flops 8589934592 | bytes 20971520 | tf_op jit(solution)/shard_map/dot_general | solution.py:69
  387.4 4.6 multiply_convert_fusion.5
  394.1 11.1 %convolution_convert_fusion.4 = bf16[2048,1024]{1,0:T(8,128)(2,1)} fusion(bf16[2048,2048]{1,0:T(8,128)(2,1)S(1)} %bitcast.171, bf16[2048,512]{1,0:T(8,128)(2,1)S(1)} %get-tuple-element.92, bf16[2048,512]{1,0:T(8,128)(2,1)S(1)} %get-tuple-element.91), kind=kOutput, calls=%fused_computation.51 | convolution fusion | flops 8600420352 | bytes 16777216 | tf_op jit(solution)/shard_map/dot_general | solution.py:77
  405.2 12.7 %fusion.93 = f32[2048,1024]{1,0:T(8,128)S(1)} fusion(bf16[2048,2048]{1,0:T(8,128)(2,1)} %share_rows.1, bf16[2048,1024]{1,0:T(8,128)(2,1)} %bitcast.164), kind=kOutput, calls=%fused_computation.231 | convolution fusion | flops 8589934592 | bytes 20971520 | tf_op jit(solution)/shard_map/dot_general | solution.py:69
  417.9 5.7 multiply_convert_fusion.3
  424.9 13.0 %convolution_convert_fusion.3 = bf16[2048,1024]{1,0:T(8,128)(2,1)} fusion(bf16[2048,2048]{1,0:T(8,128)(2,1)} %maximum_select_fusion, bf16[2048,512]{1,0:T(8,128)(2,1)S(1)} %get-tuple-element.97, bf16[2048,512]{1,0:T(8,128)(2,1)S(1)} %get-tuple-element.96), kind=kOutput, calls=%fused_computation.50 | convolution fusion | flops 8600420352 | bytes 16777216 | tf_op jit(solution)/shard_map/dot_general | solution.py:77
  438.0 5.0 pad_maximum_fusion.1.refs_2_
  443.1 2.7 pad_maximum_fusion.refs_0_
  445.7 2.7 pad_maximum_fusion.2.refs_4_
  448.4 86.6 %sum_rows.1 = (f32[512,1024]{1,0:T(8,128)}, f32[512,1024]{1,0:T(8,128)}) custom-call(bf16[2048,1024]{1,0:T(8,128)(2,1)} %pad_maximum_fusion.refs_0_, bf16[2048,1024]{1,0:T(8,128)(2,1)} %bitcast.167, bf16[2048,1024]{1,0:T(8,128)(2,1)} %pad_maximum_fusion.1.refs_2_, bf16[2048,1024]{1,0:T(8,128)(2,1)} %bitcast.165, ...), custom_call_target="tpu_custom_call" | custom-call | tf_op jit(solution)/shard_map/sum_rows/pallas_call | solution.py:395
  535.1 13.1 %convolution_convert_fusion.2 = bf16[2048,1024]{1,0:T(8,128)(2,1)} fusion(bf16[2048,2048]{1,0:T(8,128)(2,1)} %share_rows.1, bf16[2048,512]{1,0:T(8,128)(2,1)S(1)} %copy-done.17, bf16[2048,512]{1,0:T(8,128)(2,1)S(1)} %copy-done.16), kind=kOutput, calls=%fused_computation.49 | convolution fusion | flops 8600420352 | bytes 16777216 | tf_op jit(solution)/shard_map/dot_general | solution.py:77
  552.6 5.0 multiply_reduce_fusion
  557.7 4.3 multiply_add_fusion
  567.1 5.3 fusion.15
  574.2 5.3 fusion.17
  591.1 9.5 %fusion.90 = (bf16[512,2048]{1,0:T(8,128)(2,1)}, f32[512,2048]{1,0:T(8,128)S(1)}) fusion(bf16[2048,2048]{1,0:T(8,128)(2,1)} %bitcast.209, bf16[512,512]{1,0:T(8,128)(2,1)S(1)} %copy-done.52, bf16[512,512]{1,0:T(8,128)(2,1)S(1)} %copy-done.54, bf16[512,1024]{1,0:T(8,128)(2,1)S(1)} %bitcast.189), kind=kOutput, calls=%fused_computation.228 | convolution fusion | flops 4302307328 | bytes 16777216 | tf_op jit(solution)/shard_map/dot_general | solution.py:73
  603.1 4.8 convolution_convert_fusion.1
  607.9 7.3 convolution_convert_fusion
  619.0 2.7 convolution_convert_fusion.7
  621.7 26.1 %reduce-scatter.6.cloned.1.call-done.sum_1 = bf16[512,1024]{1,0:T(8,128)(2,1)} async-done(((bf16[2048,1024]{1,0:T(8,128)(2,1)}), bf16[512,1024]{1,0:T(8,128)(2,1)}) %reduce-scatter.6.cloned.1.call-update) | async-done | bytes 1048592 | tf_op jit(solution)/shard_map/reduce_scatter | solution.py:841
  647.8 201.8 %finish.1 = (f32[128,2048]{1,0:T(8,128)}, f32[1024,128]{1,0:T(8,128)}, f32[128,4096]{1,0:T(8,128)}, f32[128,4096]{1,0:T(8,128)}, f32[4096,128]{1,0:T(8,128)}, /*...) custom-call(bf16[4,4,128,1024]{3,2,1,0:T(8,128)(2,1)} %bitcast.175, ...), custom_call_target="tpu_custom_call" | custom-call | tf_op jit(solution)/shard_map/finish/pallas_call | solution.py:650
  850.9 2.7 fusion.82
  853.6 2.7 convolution_convert_fusion.5
  856.3 2.7 convolution_convert_fusion.6
  859.9 2.5 multiply_subtract_fusion.4
  867.2 2.8 multiply_subtract_fusion.1
  871.5 2.6 multiply_subtract_fusion
  875.9 2.8 multiply_subtract_fusion.2
  (284 shorter events, 103.6 us)
Async XLA Ops:
  7.2 99.2 %copy-start = (s32[64]{0:T(128)S(1)}, s32[64]{0:T(128)}, u32[]{:S(2)}) copy-start(s32[64]{0:T(128)} %param.25) | copy-start | bytes 772
  7.2 5.7 copy-start.58
  7.2 9.1 %copy-start.20 = (f32[128,4096]{1,0:T(8,128)S(1)}, f32[128,4096]{1,0:T(8,128)}, u32[]{:S(2)}) copy-start(f32[128,4096]{1,0:T(8,128)} %param.35) | copy-start | bytes 6291460
  7.2 117.7 %all-gather.3.cloned.1.call-start = ((), (), s32[]{:S(2)}) async-start(), calls=%async_computation.3 | async-start | bytes 3932160 | tf_op jit(solution)/shard_map/all_gather | solution.py:838
  12.8 345.5 %all-gather.5.cloned.1.call-start = ((), (), s32[]{:S(2)}) async-start(), calls=%async_computation.4 | async-start | bytes 15728640 | tf_op jit(solution)/shard_map/all_gather | solution.py:970
  13.6 9.6 %copy-start.61 = (s32[512]{0:T(512)}, s32[512]{0:T(512)S(1)}, u32[]{:S(2)}) copy-start(s32[512]{0:T(512)S(1)} %eq.90) | copy-start | bytes 6148
  27.8 78.6 %copy-start.74 = (s32[64]{0:T(128)S(1)}, s32[64]{0:T(128)}, u32[]{:S(2)}) copy-start(s32[64]{0:T(128)} %param.26) | copy-start | bytes 772
  106.1 442.1 %reduce-scatter.4.cloned.1.call-start = ((), (), s32[]{:S(2)}) async-start(), calls=%async_computation.5 | async-start | bytes 5242880 | tf_op jit(solution)/shard_map/reduce_scatter | solution.py:841
  107.8 5.4 copy-start.63
  107.8 5.4 copy-start.73
  110.8 190.1 %copy-start.5 = (bf16[512,2048]{1,0:T(8,128)(2,1)}, bf16[512,2048]{1,0:T(8,128)(2,1)S(1)}, u32[]{:S(2)}) copy-start(bf16[512,2048]{1,0:T(8,128)(2,1)S(1)} %get-tuple-element.141) | copy-start | bytes 6291460
  110.9 162.8 %copy-start.59 = (f32[512]{0:T(512)}, f32[512]{0:T(512)S(1)}, u32[]{:S(2)}) copy-start(f32[512]{0:T(512)S(1)} %add_rsqrt_fusion.1) | copy-start | bytes 6148
  111.9 161.7 %copy-start.56 = (f32[16,1,128]{2,1,0:T(1,128)}, f32[16,1,128]{2,1,0:T(1,128)S(1)}, u32[]{:S(2)}) copy-start(f32[16,1,128]{2,1,0:T(1,128)S(1)} %get-tuple-element.135) | copy-start | bytes 24580
  113.1 152.2 %copy-start.25 = (f32[512,128]{1,0:T(8,128)}, f32[512,128]{1,0:T(8,128)S(1)}, u32[]{:S(2)}) copy-start(f32[512,128]{1,0:T(8,128)S(1)} %get-tuple-element.138) | copy-start | bytes 786436
  113.1 152.2 %copy-start.27 = (f32[512,128]{1,0:T(8,128)}, f32[512,128]{1,0:T(8,128)S(1)}, u32[]{:S(2)}) copy-start(f32[512,128]{1,0:T(8,128)S(1)} %get-tuple-element.139) | copy-start | bytes 786436
  241.8 34.9 %collective-permute-start.1 = (bf16[512,1024]{1,0:T(8,128)(2,1)}, bf16[512,1024]{1,0:T(8,128)(2,1)}, u32[]{:S(2)}, u32[]{:S(2)}) collective-permute-start(bf16[512,1024]{1,0:T(8,128)(2,1)} %convolution_convert_fusion.11), channel_id=1, source_target_pairs={{0,4},{2,6},{4,0},{6,2},{1,5},{3,7},{5,1},{7,3},{8,12},{10,14},{12... | collective-permute-start | bytes 3145736 | tf_op jit(solution)/shard_map/ppermute | solution.py:832
  242.8 28.4 %collective-permute-start = (bf16[512,1024]{1,0:T(8,128)(2,1)}, bf16[512,1024]{1,0:T(8,128)(2,1)}, u32[]{:S(2)}, u32[]{:S(2)}) collective-permute-start(bf16[512,1024]{1,0:T(8,128)(2,1)} %convolution_convert_fusion.11), channel_id=1, source_target_pairs={{0,2},{2,0},{4,6},{6,4},{1,3},{3,1},{5,7},{7,5},{8,10},{10,8},{12,... | collective-permute-start | bytes 3145736 | tf_op jit(solution)/shard_map/ppermute | solution.py:832
  271.1 19.7 %copy-start.29 = (f32[2,2,512,512]{2,3,1,0:T(8,128)}, f32[2,2,512,512]{2,3,1,0:T(8,128)S(1)}, u32[]{:S(2)}) copy-start(f32[2,2,512,512]{2,3,1,0:T(8,128)S(1)} %get-tuple-element.143) | copy-start | bytes 12582916
  272.6 6.5 copy-start.50
  272.7 12.3 %collective-permute-start.2 = (bf16[256,1024]{1,0:T(8,128)(2,1)S(1)}, bf16[256,1024]{1,0:T(8,128)(2,1)S(1)}, u32[]{:S(2)}, u32[]{:S(2)}) collective-permute-start(bf16[256,1024]{1,0:T(8,128)(2,1)S(1)} %slice.280), channel_id=1, source_target_pairs={{0,4},{2,6},{4,0},{6,2},{1,5},{3,7},{5,1},{7,3},{8,12},{10,14},{12... | collective-permute-start | bytes 1572872 | tf_op jit(solution)/shard_map/ppermute | solution.py:832
  276.7 14.2 %copy-start.77 = (bf16[512,512]{0,1:T(8,128)(2,1)}, bf16[512,512]{0,1:T(8,128)(2,1)S(1)}, u32[]{:S(2)}) copy-start(bf16[512,512]{0,1:T(8,128)(2,1)S(1)} %fusion.39) | copy-start | bytes 1572868
  278.0 12.0 %collective-permute-start.3 = (bf16[256,1024]{1,0:T(8,128)(2,1)S(1)}, bf16[256,1024]{1,0:T(8,128)(2,1)S(1)}, u32[]{:S(2)}, u32[]{:S(2)}) collective-permute-start(bf16[256,1024]{1,0:T(8,128)(2,1)S(1)} %slice.281), channel_id=1, source_target_pairs={{0,2},{2,0},{4,6},{6,4},{1,3},{3,1},{5,7},{7,5},{8,10},{10,8},{12,... | collective-permute-start | bytes 1572872 | tf_op jit(solution)/shard_map/ppermute | solution.py:832
  290.8 56.2 %collective-permute-start.4 = (bf16[2048,1024]{1,0:T(8,128)(2,1)}, bf16[2048,1024]{1,0:T(8,128)(2,1)}, u32[]{:S(2)}, u32[]{:S(2)}) collective-permute-start(bf16[2048,1024]{1,0:T(8,128)(2,1)} %constant_dynamic-update-slice_fusion), channel_id=1, source_target_pairs={{0,1},{1,0},{2,3},{3,2},{4,5},{5,4},{6,7},{7,6},{8,9},{9,8},{10,11... | collective-permute-start | bytes 12582920 | tf_op jit(solution)/shard_map/ppermute | solution.py:835
  295.8 5.1 collective-permute-start.5
  358.4 8.8 copy-start.11
  358.4 20.0 %slice-start = ((s8[8388608]{0:T(1024)(128)(4,1)}), s8[4194304]{0:T(1024)(128)(4,1)S(1)}, s32[]{:S(2)}) async-start(s8[8388608]{0:T(1024)(128)(4,1)} %bitcast.170), calls=%async_computation.8 | async-start | bytes 8388608
  365.8 12.5 %copy-start.10 = (bf16[1,4,512,1024]{3,2,1,0:T(8,128)(2,1)}, bf16[1,4,512,1024]{3,2,1,0:T(8,128)(2,1)S(1)}, u32[]{:S(2)}) copy-start(bf16[1,4,512,1024]{3,2,1,0:T(8,128)(2,1)S(1)} %get-tuple-element.95) | copy-start | bytes 12582916
  365.8 12.5 %copy-start.9 = (bf16[1,4,512,1024]{3,2,1,0:T(8,128)(2,1)}, bf16[1,4,512,1024]{3,2,1,0:T(8,128)(2,1)S(1)}, u32[]{:S(2)}) copy-start(bf16[1,4,512,1024]{3,2,1,0:T(8,128)(2,1)S(1)} %get-tuple-element.94) | copy-start | bytes 12582916
  367.1 11.2 %slice-start.1 = ((s8[8388608]{0:T(1024)(128)(4,1)}), s8[4194304]{0:T(1024)(128)(4,1)S(1)}, s32[]{:S(2)}) async-start(s8[8388608]{0:T(1024)(128)(4,1)} %bitcast.170), calls=%async_computation.9 | async-start | bytes 8388608
  405.2 216.5 %reduce-scatter.8.cloned.1.call-start = ((), (), s32[]{:S(2)}) async-start(), calls=%async_computation.7 | async-start | bytes 5242880 | tf_op jit(solution)/shard_map/reduce_scatter | solution.py:841
  438.0 209.9 %reduce-scatter.6.cloned.1.call-start = ((), (), s32[]{:S(2)}) async-start(), calls=%async_computation.6 | async-start | bytes 5242880 | tf_op jit(solution)/shard_map/reduce_scatter | solution.py:841
  448.4 86.6 %copy-start.16 = (bf16[2048,512]{1,0:T(8,128)(2,1)S(1)}, bf16[2048,512]{1,0:T(8,128)(2,1)}, u32[]{:S(2)}) copy-start(bf16[2048,512]{1,0:T(8,128)(2,1)} %get-tuple-element.89) | copy-start | bytes 6291460
  448.4 86.6 %copy-start.17 = (bf16[2048,512]{1,0:T(8,128)(2,1)S(1)}, bf16[2048,512]{1,0:T(8,128)(2,1)}, u32[]{:S(2)}) copy-start(bf16[2048,512]{1,0:T(8,128)(2,1)} %get-tuple-element.90) | copy-start | bytes 6291460
  548.1 4.5 collective-permute-start.6
  557.7 6.3 copy-start.72
  574.2 5.3 copy-start.47
  574.2 5.3 copy-start.49
  579.6 6.1 copy-start.32
  579.6 6.1 copy-start.34
  591.0 9.5 %copy-start.4 = (f32[512,2048]{1,0:T(8,128)S(1)}, f32[512,2048]{1,0:T(8,128)}, u32[]{:S(2)}) copy-start(f32[512,2048]{1,0:T(8,128)} %copy-done.2) | copy-start | bytes 12582916
  591.0 9.5 %copy-start.42 = (f32[512,1024]{1,0:T(8,128)S(1)}, f32[512,1024]{1,0:T(8,128)}, u32[]{:S(2)}) copy-start(f32[512,1024]{1,0:T(8,128)} %get-tuple-element.54) | copy-start | bytes 6291460
  600.6 14.7 %collective-permute-start.7 = (bf16[512,2048]{1,0:T(8,128)(2,1)}, bf16[512,2048]{1,0:T(8,128)(2,1)S(1)}, u32[]{:S(2)}, u32[]{:S(2)}) collective-permute-start(bf16[512,2048]{1,0:T(8,128)(2,1)} %get-tuple-element.148), channel_id=1, source_target_pairs={{0,1},{1,0},{2,3},{3,2},{4,5},{5,4},{6,7},{7,6},{8,9},{9,8},{10,11... | collective-permute-start | bytes 6291464 | tf_op jit(solution)/shard_map/ppermute | solution.py:835
  856.3 6.1 copy-start.51
  856.3 8.4 copy-start.38
  859.0 8.1 copy-start.21
  859.9 7.2 copy-start.39
  859.9 7.2 copy-start.45
  874.1 5.9 copy-start.1
  (46 other events, 138.8 us)
Sparse Core Ops, SparseCore 0:
  12.9 111.9 all-gather.2
  126.5 216.6 all-gather.4
  405.3 83.5 reduce-scatter.3
  491.1 77.2 reduce-scatter.7
  570.5 77.2 reduce-scatter.5

commit v4 on v3

--- a/solution.py
+++ b/solution.py
@@ -32,14 +32,6 @@
     first, second = value[..., :half], value[..., half:]
     return jnp.concatenate(
         [first * cosine - second * sine, second * cosine + first * sine], axis=-1
-    )
-
-
-def unrotate(grads, cosine, sine):
-    half = grads.shape[-1] // 2
-    first, second = grads[..., :half], grads[..., half:]
-    return jnp.concatenate(
-        [first * cosine + second * sine, second * cosine - first * sine], axis=-1
     )
 
 
@@ -58,11 +50,6 @@
 def normalize(value):
     scale_inv = lax.rsqrt(jnp.mean(value * value, axis=-1, keepdims=True) + EPS)
     return (value * scale_inv, scale_inv)
-
-
-def norm_back(grad_normed, normed, scale_inv, gain):
-    scaled = grad_normed * gain
-    return scale_inv * (scaled - normed * jnp.mean(scaled * normed, axis=-1, keepdims=True))
 
 
 def mat_nn(left, right):
@@ -422,289 +409,6 @@
 WIDTH = 512
 
 
-def finish_kernel(
-    g_out, g_qkv, sum_0, sum_1, sum_d, slots, gain_terms,
-    new_qkv, new_out, new_gate, new_up, new_down, new_gain, norm, back,
-    own, to_x, to_y, diag_x, diag_y, from_x, from_y, add_x, add_y, sums, packed, line,
-    ffn, gain_got, shares,
-    send, recv, local, row_send, row_recv, ends, keeps, unit_send, unit_recv, unit_local, all_send, all_recv,
-):
-    z, p, core, one, two, three = places()
-    depth, _, each, _ = g_out.shape
-    count = slots.shape[0]
-    wide = slots.shape[2] // 2
-    units = sum_d.shape[1]
-    span = units // 2
-    me = z * GROUP + p
-    half = depth // 2
-    low, high = pl.ds(0, half), pl.ds(half, half)
-    x, y, twin = (z, one, core), (z, two, core), (z, p, 1 - core)
-    column = [(lax.rem(z + s, depth), p, core) for s in range(1, depth)]
-    columns = pl.ds(pl.multiple_of(core * wide, wide), wide)
-    places_of = [(g, c) for g in (g_out, g_qkv) for c in range(g.shape[3] // WIDTH)]
-    chunks = len(places_of)
-
-    def source(rows, q, c):
-        g, at = places_of[c]
-        return g.at[rows, q, :, pl.ds(at * WIDTH, WIDTH)]
-
-    loads = []
-    for c in range(chunks):
-        loads.append(pltpu.make_async_copy(source(pl.ds(0, depth), p, c), own.at[c], local.at[0, c]))
-        loads.append(pltpu.make_async_copy(source(low, one, c), to_x.at[c], local.at[1, c]))
-        loads.append(pltpu.make_async_copy(source(high, two, c), to_y.at[c], local.at[2, c]))
-    for load in loads:
-        load.start()
-
-    def partner(s):
-        t = lax.rem(me + s, count)
-        return t, (t // GROUP, lax.rem(t, GROUP), core)
-
-    def anyone(s):
-        t = lax.rem(me * 2 + core + s, 2 * count)
-        return (t // (2 * GROUP), lax.rem(t // 2, GROUP), lax.rem(t, 2))
-
-    barrier = pltpu.get_barrier_semaphore()
-
-    def greet(s, carry):
-        pl.semaphore_signal(barrier, inc=1, device_id=anyone(s), device_id_type=MESH)
-        return carry
-
-    lax.fori_loop(1, 2 * count, greet, 0)
-    keep = [
-        pltpu.make_async_copy(
-            slots.at[me, :, pl.ds(i * wide, wide)], back.at[i, me, :, columns], keeps.at[i]
-        )
-        for i in range(2)
-    ] + [pltpu.make_async_copy(gain_terms.at[me], gain_got.at[me], keeps.at[2])]
-    for copy in keep:
-        copy.start()
-
-    def unit_parts(q, of):
-        rows = pl.ds(pl.multiple_of(q * each, each), each)
-
-        def place(i, shift, size):
-            return ffn.at[i, :, pl.ds(pl.multiple_of(of * units + shift, span), size)]
-
-        return [
-            (sum_0.at[rows, pl.ds(0, span)], place(0, 0, span)),
-            (sum_0.at[rows, pl.ds(span, span)], place(1, 0, span)),
-            (sum_1.at[rows, pl.ds(0, span)], place(0, span, span)),
-            (sum_1.at[rows, pl.ds(span, span)], place(1, span, span)),
-            (sum_d.at[rows], place(2, 0, units)),
-        ]
-
-    stay = [
-        pltpu.make_async_copy(src, dst, unit_local.at[i])
-        for i, (src, dst) in enumerate(unit_parts(p, p))
-    ]
-    for copy in stay:
-        copy.start()
-    pl.semaphore_wait(barrier, 2 * count - 1)
-    copies = {}
-
-    def rows(s, kinds):
-        t, who = partner(s)
-        made = []
-        for i in kinds:
-            if i < 2:
-                src, dst = slots.at[t, :, pl.ds(i * wide, wide)], back.at[i, me, :, columns]
-            else:
-                src, dst = gain_terms.at[t], gain_got.at[me]
-            made.append(to(src, dst, row_send.at[i, s], row_recv.at[i, s], who))
-        return made
-
-    def each_row(act):
-        def step(s, carry):
-            for copy in rows(s, (0, 1, 2)):
-                act(copy)
-            return carry
-
-        lax.fori_loop(1, count, step, 0)
-
-    def go(name, c, i, src, dst, who):
-        copies[name, c] = to(src, dst, send.at[c, i], recv.at[c, i], who)
-        copies[name, c].start()
-
-    def first(c):
-        go("3a", c, 0, source(low, three, c), diag_y.at[c], y)
-        go("3b", c, 1, source(high, three, c), diag_x.at[c], x)
-        go("1b", c, 2, source(high, one, c), from_x.at[c, high], x)
-        go("2a", c, 3, source(low, two, c), from_y.at[c, low], y)
-
-    def relay(c):
-        copies["3a", c].wait_recv()
-        add_x[c] = (to_x[c].astype(F32) + diag_y[c].astype(F32)).astype(BF)
-        go("1a", c, 4, add_x.at[c], from_x.at[c, low], x)
-        copies["3b", c].wait_recv()
-        add_y[c] = (to_y[c].astype(F32) + diag_x[c].astype(F32)).astype(BF)
-        go("2b", c, 5, add_y.at[c], from_y.at[c, high], y)
-
-    def along(c):
-        for name in ("1a", "1b", "2a", "2b"):
-            copies[name, c].wait_recv()
-        sums[c] = own[c].astype(F32) + from_x[c].astype(F32) + from_y[c].astype(F32)
-        packed[c] = sums[c].astype(BF)
-        for s, who in enumerate(column, 1):
-            go(s, c, 5 + s, packed.at[c, who[0]], line.at[c, s - 1], who)
-
-    first(0)
-    each_row(lambda copy: copy.start())
-    first(1)
-    shared = []
-    for k, q in ((3, three), (1, one), (2, two)):
-        for i, (src, dst) in enumerate(unit_parts(q, p)):
-            copy = to(src, dst, unit_send.at[k, i], unit_recv.at[k, i], (z, q, core))
-            copy.start()
-            shared.append(copy)
-    for load in loads:
-        load.wait()
-    for c in range(chunks):
-        relay(c)
-        if c + 2 < chunks:
-            first(c + 2)
-        if c:
-            along(c - 1)
-    for copy in keep:
-        copy.wait()
-    each_row(lambda copy: copy.wait_recv())
-    pass_on = to(
-        back.at[:, :, :, columns], back.at[:, :, :, columns], ends.at[0], ends.at[1], twin
-    )
-    pass_on.start()
-    along(chunks - 1)
-
-    def squares(value):
-        return jnp.sum(jnp.sum(value * value, axis=0, keepdims=True), axis=1, keepdims=True)
-
-    for copy in stay:
-        copy.wait()
-    for copy in shared:
-        copy.wait_recv()
-    total = jnp.zeros((1, 1), F32)
-    for i, ref in ((0, new_gate), (1, new_up)):
-        for at in range(0, ref.shape[1], WIDTH):
-            value = ffn[i, :, at : at + WIDTH].astype(F32)
-            total = total + squares(value)
-            ref[:, at : at + WIDTH] = value
-    for at in range(0, new_down.shape[0], 128):
-        value = ffn[2, :, at : at + 128].astype(F32)
-        total = total + squares(value)
-        new_down[at : at + 128, :] = value.T
-    gain = gain_got[0]
-    for t in range(1, count):
-        gain = gain + gain_got[t]
-    new_gain[...] = gain
-    total = total + 0.5 * squares(gain[:2])
-    for c in range(chunks):
-        value = sums[c, z]
-        for s in range(1, depth):
-            copies[s, c].wait_recv()
-            value = value + line[c, s - 1].astype(F32)
-        total = total + squares(value)
-        g, at = places_of[c]
-        if g is g_qkv:
-            new_qkv[:, pl.ds(at * WIDTH, WIDTH)] = value
-        else:
-            for i in range(0, WIDTH, 128):
-                new_out[pl.ds(at * WIDTH + i, 128), :] = value[:, i : i + 128].T
-    shares[0] = jnp.broadcast_to(total, (8, 128))
-
-    def tell(s):
-        return to(shares.at[0], shares.at[s], all_send.at[s], all_recv.at[s], anyone(s))
-
-    def tell_start(s, carry):
-        tell(s).start()
-        return carry
-
-    def tell_end(s, carry):
-        tell(s).wait_recv()
-        return carry
-
-    def tell_left(s, carry):
-        tell(s).wait_send()
-        return carry
-
-    lax.fori_loop(1, 2 * count, tell_start, 0)
-    lax.fori_loop(1, 2 * count, tell_end, 0)
-    everyone = jnp.sum(shares[...], axis=0)
-    norm[...] = jnp.sqrt(everyone)
-    lax.fori_loop(1, 2 * count, tell_left, 0)
-    pass_on.wait_recv()
-    for copy in [*copies.values(), *shared]:
-        copy.wait_send()
-    each_row(lambda copy: copy.wait_send())
-    pass_on.wait_send()
-
-
-def finish(g_out, g_qkv, sum_0, sum_1, sum_d, slots, gain_terms, ident):
-    depth = lax.axis_size("line")
-    each = g_qkv.shape[0] // (depth * GROUP)
-    units = sum_d.shape[1]
-    chunks = (g_out.shape[1] + g_qkv.shape[1]) // WIDTH
-    count, per, both = slots.shape
-
-    def buffer(rows, dtype=BF):
-        return pltpu.VMEM((chunks, rows, each, WIDTH), dtype)
-
-    return pl.pallas_call(
-        finish_kernel,
-        out_shape=[
-            jax.ShapeDtypeStruct((each, g_qkv.shape[1]), F32),
-            jax.ShapeDtypeStruct((g_out.shape[1], each), F32),
-            jax.ShapeDtypeStruct((each, GROUP * units), F32),
-            jax.ShapeDtypeStruct((each, GROUP * units), F32),
-            jax.ShapeDtypeStruct((GROUP * units, each), F32),
-            jax.ShapeDtypeStruct(gain_terms.shape[1:], F32),
-            jax.ShapeDtypeStruct((8, 128), F32),
-            jax.ShapeDtypeStruct((2, count, per, both), BF),
-        ],
-        in_specs=[ANY] * 5 + [WHOLE] * 2,
-        out_specs=[WHOLE] * 7 + [ANY],
-        scratch_shapes=[
-            buffer(depth),
-            buffer(depth // 2),
-            buffer(depth // 2),
-            buffer(depth // 2),
-            buffer(depth // 2),
-            buffer(depth),
-            buffer(depth),
-            buffer(depth // 2),
-            buffer(depth // 2),
-            buffer(depth, F32),
-            buffer(depth),
-            buffer(depth - 1),
-            pltpu.VMEM((3, each, GROUP * units), BF),
-            pltpu.VMEM(gain_terms.shape, F32),
-            pltpu.VMEM((2 * count, 8, 128), F32),
-            pltpu.SemaphoreType.DMA((chunks, 5 + depth)),
-            pltpu.SemaphoreType.DMA((chunks, 5 + depth)),
-            pltpu.SemaphoreType.DMA((3, chunks)),
-            pltpu.SemaphoreType.DMA((3, count)),
-            pltpu.SemaphoreType.DMA((3, count)),
-            pltpu.SemaphoreType.DMA((2,)),
-            pltpu.SemaphoreType.DMA((3,)),
-            pltpu.SemaphoreType.DMA((4, 5)),
-            pltpu.SemaphoreType.DMA((4, 5)),
-            pltpu.SemaphoreType.DMA((5,)),
-            pltpu.SemaphoreType.DMA((2 * count,)),
-            pltpu.SemaphoreType.DMA((2 * count,)),
-        ],
-        compiler_params=pltpu.CompilerParams(
-            collective_id=ident, has_side_effects=True, vmem_limit_bytes=58 << 20
-        ),
-        name="finish",
-    )(
-        g_out.reshape(depth, GROUP, each, -1),
-        g_qkv.reshape(depth, GROUP, each, -1),
-        sum_0,
-        sum_1,
-        sum_d,
-        slots,
-        gain_terms,
-    )
-
-
 def deal_kernel(sent, pieces, gains, tokens, cots, units, all_gains, held, send, recv, ends, local):
     z, p, core, one, two, three = places()
     count, per, both = sent.shape
@@ -819,6 +523,560 @@
     )(sent, pieces, gains)
 
 
+STRIP = 16
+
+
+def attend_back_kernel(
+    dh2_half, middle, cot, w_out, w_qkv, mixed, q_rot, k_rot, value, prob, tokens, half_result,
+    scale1, scale2, gain_a, gain_f, cosine, sine, into,
+    new_qkv, new_out, new_gain, back,
+    dh2, mid, low_mid, xs, hidden, w_part, g, mix, d_mix, qs, ks, vs, pb, gq, got_part,
+    from_x, from_y, diag_x, diag_y, own, line, slots, half_rows, gain_terms, gain_got,
+    send, recv, loads, row_send, row_recv, ends, keeps,
+):
+    z, p, core, one, two, three = places()
+    chunks, depth, _, each, _ = g.shape
+    rows, width = mid.shape
+    wide = width // 2
+    query_cols, key_cols = qs.shape[1], ks.shape[1]
+    outs = query_cols // WIDTH
+    count, per, _ = slots.shape[1:]
+    me = z * GROUP + p
+    half = depth // 2
+    low, high = pl.ds(0, half), pl.ds(half, half)
+    x, y, twin = (z, one, core), (z, two, core), (z, p, 1 - core)
+    column = [(lax.rem(z + s, depth), p, core) for s in range(1, depth)]
+    columns = pl.ds(pl.multiple_of(core * wide, wide), wide)
+    root = HEAD_SIZE ** (-0.5)
+    pending = {}
+
+    def load(name, i, src, dst):
+        pending[name] = pltpu.make_async_copy(src, dst, loads.at[i])
+        pending[name].start()
+
+    load("half", 0, half_result, half_rows)
+    load("dh2", 1, dh2_half, dh2.at[:, columns])
+    load("mid", 2, middle, mid)
+    load("cot", 3, cot, low_mid)
+    load("x", 4, tokens, xs)
+    load("mix", 5, mixed, mix)
+    for i in range(outs):
+        load(("out", i), 6 + i, w_out.at[:, :, :, pl.ds(i * WIDTH, WIDTH)], g.at[chunks - outs + i])
+    at = 6 + outs
+    load("q", at, q_rot, qs)
+    load("k", at + 1, k_rot, ks)
+    load("v", at + 2, value, vs)
+    load(("p", 0), at + 3, prob.at[0], pb.at[0])
+    load(("p", 1), at + 4, prob.at[1], pb.at[1])
+    block = w_part.shape[1]
+
+    def load_part(i):
+        load(("w", i), at + 5 + i % 2, w_qkv.at[pl.ds(i * block, block)], w_part.at[i % 2])
+
+    load_part(0)
+    load_part(1)
+
+    def partner(s):
+        t = lax.rem(me + s, count)
+        return t, (t // GROUP, lax.rem(t, GROUP), core)
+
+    barrier = pltpu.get_barrier_semaphore()
+
+    def greet(s, carry):
+        pl.semaphore_signal(barrier, inc=1, device_id=partner(s)[1], device_id_type=MESH)
+        return carry
+
+    lax.fori_loop(1, count, greet, 0)
+    pl.semaphore_signal(barrier, inc=1, device_id=twin, device_id_type=MESH)
+    pl.semaphore_wait(barrier, count)
+    copies = {}
+
+    def go(name, c, i, src, dst, who):
+        copies[name, c] = to(src, dst, send.at[c, i], recv.at[c, i], who)
+        copies[name, c].start()
+
+    def row(i, s):
+        t, who = partner(s)
+        if i < 2:
+            return to(slots.at[i, t], back.at[i, me, :, columns], row_send.at[i, s], row_recv.at[i, s], who)
+        return to(gain_terms.at[t], gain_got.at[me], row_send.at[2, s], row_recv.at[2, s], who)
+
+    def each_row(kinds, act):
+        def step(s, carry):
+            for i in kinds:
+                act(row(i, s))
+            return carry
+
+        lax.fori_loop(1, count, step, 0)
+
+    kept = []
+
+    def give_rows(i):
+        slots[i] = mat_tn(into[...], half_rows[...]).reshape(count, per, wide).astype(BF)
+        kept.append(pltpu.make_async_copy(slots.at[i, me], back.at[i, me, :, columns], keeps.at[i]))
+        kept[-1].start()
+        each_row((i,), lambda copy: copy.start())
+
+    def first(c):
+        go("3a", c, 0, g.at[c, low, three], diag_y.at[c], y)
+        go("3b", c, 1, g.at[c, high, three], diag_x.at[c], x)
+        go("1b", c, 2, g.at[c, high, one], from_x.at[c, high], x)
+        go("2a", c, 3, g.at[c, low, two], from_y.at[c, low], y)
+
+    def relay(c):
+        copies["3a", c].wait_recv()
+        for j in range(half):
+            diag_y[c, j] = (g[c, j, one].astype(F32) + diag_y[c, j].astype(F32)).astype(BF)
+        go("1a", c, 4, diag_y.at[c], from_x.at[c, low], x)
+        copies["3b", c].wait_recv()
+        for j in range(half):
+            diag_x[c, j] = (g[c, half + j, two].astype(F32) + diag_x[c, j].astype(F32)).astype(BF)
+        go("2b", c, 5, diag_x.at[c], from_y.at[c, high], y)
+
+    def along(c):
+        for name in ("1a", "1b", "2a", "2b"):
+            copies[name, c].wait_recv()
+        own[c] = g[c, z, p].astype(F32) + from_x[c, z].astype(F32) + from_y[c, z].astype(F32)
+        for j in range(depth):
+            from_x[c, j] = (
+                g[c, j, p].astype(F32) + from_x[c, j].astype(F32) + from_y[c, j].astype(F32)
+            ).astype(BF)
+        for s, who in enumerate(column, 1):
+            go(s, c, 5 + s, from_x.at[c, who[0]], line.at[c, s - 1], who)
+
+    def terms(c, left, right):
+        span = GROUP * each
+        for j in range(depth):
+            part = mat_tn(left[:, j * span : (j + 1) * span], right)
+            g[c, j] = part.reshape(GROUP, each, WIDTH).astype(BF)
+        first(c)
+
+    pending["dh2"].wait()
+    swap = to(dh2.at[:, columns], dh2.at[:, columns], ends.at[0, 0], ends.at[1, 0], twin)
+    swap.start()
+    pending["half"].wait()
+    give_rows(0)
+    for name in ("mid", "cot", "x"):
+        pending[name].wait()
+    swap.wait_recv()
+
+    def norm_2(i, total):
+        strip = pl.ds(pl.multiple_of(i * STRIP, STRIP), STRIP)
+        r2 = scale2[strip, :]
+        n2 = mid[strip, :] * r2
+        d = dh2[strip, :]
+        s = d * gain_f[...]
+        mean = jnp.sum(s * n2, axis=1, keepdims=True) * (1.0 / width)
+        dm = low_mid[strip, :].astype(F32) + r2 * (s - n2 * mean)
+        mid[strip, :] = dm
+        low_mid[strip, :] = dm.astype(BF)
+        hidden[strip, :] = (xs[strip, :].astype(F32) * scale1[strip, :] * gain_a[...]).astype(BF)
+        return total + jnp.sum(d * n2, axis=0, keepdims=True)
+
+    grad_gf = lax.fori_loop(0, rows // STRIP, norm_2, jnp.zeros((1, width), F32))
+    pending["mix"].wait()
+    for i in range(outs):
+        pending["out", i].wait()
+        d_mix[:, i * WIDTH : (i + 1) * WIDTH] = mat_nn(
+            low_mid[...], g[chunks - outs + i].reshape(width, WIDTH)
+        ).astype(BF)
+    for i in range(outs):
+        terms(i, low_mid, mix[:, i * WIDTH : (i + 1) * WIDTH])
+    swap.wait_send()
+
+    def turned_back(grad):
+        a, b = grad[:, : HEAD_SIZE // 2], grad[:, HEAD_SIZE // 2 :]
+        c, s = cosine[...], sine[...]
+        return jnp.concatenate([a * c + b * s, b * c - a * s], axis=1).astype(BF)
+
+    for name in ("q", "k", "v"):
+        pending[name].wait()
+    heads, kv_heads = query_cols // HEAD_SIZE, key_cols // HEAD_SIZE
+    each_kv = heads // kv_heads
+    for h in range(kv_heads):
+        kk, vv = ks[:, h * HEAD_SIZE : (h + 1) * HEAD_SIZE], vs[:, h * HEAD_SIZE : (h + 1) * HEAD_SIZE]
+        dk = dv = None
+        for j in range(h * each_kv, (h + 1) * each_kv):
+            cols = slice(j * HEAD_SIZE, (j + 1) * HEAD_SIZE)
+            pending["p", j].wait()
+            pr = pb[j % 2]
+            do = d_mix[:, cols]
+            dp = mat_nt(do, vv)
+            delta = jnp.sum(pr * dp, axis=1, keepdims=True)
+            ds = (pr * (dp - delta)).astype(BF)
+            gq[:, cols] = turned_back(mat_nn(ds, kk) * root)
+            more_k, more_v = mat_tn(ds, qs[:, cols]), mat_tn(pr.astype(BF), do)
+            dk, dv = (more_k, more_v) if dk is None else (dk + more_k, dv + more_v)
+            if j + 2 < heads:
+                load(("p", j + 2), at + 3 + j % 2, prob.at[j + 2], pb.at[j % 2])
+        base = query_cols + h * HEAD_SIZE
+        gq[:, base : base + HEAD_SIZE] = turned_back(dk * root)
+        base += key_cols
+        gq[:, base : base + HEAD_SIZE] = dv.astype(BF)
+        done = (h + 1) * each_kv * HEAD_SIZE // WIDTH
+        for i in range(h * each_kv * HEAD_SIZE // WIDTH, done):
+            terms(outs + i, hidden, gq[:, i * WIDTH : (i + 1) * WIDTH])
+        if h < outs:
+            relay(h)
+    for i in range(kv_heads, outs):
+        relay(i)
+    for i in range(done, gq.shape[1] // WIDTH):
+        terms(outs + i, hidden, gq[:, i * WIDTH : (i + 1) * WIDTH])
+    for i in range(width // block):
+        pending["w", i].wait()
+        part = mat_nt(gq[...], w_part[i % 2])
+        dh2[:, i * block : (i + 1) * block] = part
+        low_mid[:, i * block : (i + 1) * block] = part.astype(BF)
+        if i + 2 < width // block:
+            load_part(i + 2)
+    pass_part = to(low_mid, got_part, ends.at[0, 1], ends.at[1, 1], twin)
+    pass_part.start()
+    for c in range(outs):
+        along(c)
+    relay(outs)
+    each_row((0,), lambda copy: copy.wait_send())
+    pass_part.wait_recv()
+
+    def norm_1(i, total):
+        strip = pl.ds(pl.multiple_of(i * STRIP, STRIP), STRIP)
+        r1 = scale1[strip, :]
+        n1 = xs[strip, :].astype(F32) * r1
+        d = dh2[strip, :] + got_part[strip, :].astype(F32)
+        s = d * gain_a[...]
+        mean = jnp.sum(s * n1, axis=1, keepdims=True) * (1.0 / width)
+        dx = mid[strip, :] + r1 * (s - n1 * mean)
+        half_rows[strip, :] = jnp.where(core == 0, dx[:, :wide], dx[:, wide:]).astype(BF)
+        return total + jnp.sum(d * n1, axis=0, keepdims=True)
+
+    grad_ga = lax.fori_loop(0, rows // STRIP, norm_1, jnp.zeros((1, width), F32))
+    give_rows(1)
+    for t in range(count):
+        gain_terms[t, 0:1, :] = grad_ga[:, t * each : (t + 1) * each]
+        gain_terms[t, 1:2, :] = grad_gf[:, t * each : (t + 1) * each]
+        gain_terms[t, 2:8, :] = jnp.zeros((6, each), F32)
+    kept.append(pltpu.make_async_copy(gain_terms.at[me], gain_got.at[me], keeps.at[2]))
+    kept[-1].start()
+    each_row((2,), lambda copy: copy.start())
+    for c in range(outs + 1, chunks):
+        relay(c)
+        along(c - 1)
+    for copy in kept:
+        copy.wait()
+    each_row((0, 1, 2), lambda copy: copy.wait_recv())
+    pass_on = to(
+        back.at[:, :, :, columns], back.at[:, :, :, columns], ends.at[0, 2], ends.at[1, 2], twin
+    )
+    pass_on.start()
+    along(chunks - 1)
+    gain = gain_got[0]
+    for t in range(1, count):
+        gain = gain + gain_got[t]
+    new_gain[...] = gain
+    for c in range(chunks):
+        total = own[c]
+        for s in range(1, depth):
+            copies[s, c].wait_recv()
+            total = total + line[c, s - 1].astype(F32)
+        if c < outs:
+            new_out[:, c * WIDTH : (c + 1) * WIDTH] = total
+        else:
+            new_qkv[:, (c - outs) * WIDTH : (c - outs + 1) * WIDTH] = total
+    pass_on.wait_recv()
+    for copy in copies.values():
+        copy.wait_send()
+    each_row((1, 2), lambda copy: copy.wait_send())
+    pass_part.wait_send()
+    pass_on.wait_send()
+
+
+def attend_back(
+    dh2_half, middle, cot, w_out, w_qkv, mixed, q_rot, k_rot, value, prob, tokens, half_result,
+    scale1, scale2, gain_a, gain_f, cosine, sine, into, ident,
+):
+    depth = lax.axis_size("line")
+    count = depth * GROUP
+    rows, width = middle.shape
+    wide = width // 2
+    each = width // count
+    query_cols, key_cols = q_rot.shape[1], k_rot.shape[1]
+    cols = query_cols + 2 * key_cols
+    chunks = (query_cols + cols) // WIDTH
+    block = min(512, width)
+
+    def vmem(*shape, dtype=BF):
+        return pltpu.VMEM(shape, dtype)
+
+    return pl.pallas_call(
+        attend_back_kernel,
+        out_shape=[
+            jax.ShapeDtypeStruct((each, cols), F32),
+            jax.ShapeDtypeStruct((each, query_cols), F32),
+            jax.ShapeDtypeStruct((8, each), F32),
+            jax.ShapeDtypeStruct((2, count, rows // count, width), BF),
+        ],
+        in_specs=[ANY] * 12 + [WHOLE] * 7,
+        out_specs=[WHOLE] * 3 + [ANY],
+        scratch_shapes=[
+            vmem(rows, width, dtype=F32),
+            vmem(rows, width, dtype=F32),
+            vmem(rows, width),
+            vmem(rows, width),
+            vmem(rows, width),
+            vmem(2, block, cols),
+            vmem(chunks, depth, GROUP, each, WIDTH),
+            vmem(rows, query_cols),
+            vmem(rows, query_cols),
+            vmem(rows, query_cols),
+            vmem(rows, key_cols),
+            vmem(rows, key_cols),
+            vmem(2, rows, rows, dtype=F32),
+            vmem(rows, cols),
+            vmem(rows, width),
+            vmem(chunks, depth, each, WIDTH),
+            vmem(chunks, depth, each, WIDTH),
+            vmem(chunks, depth // 2, each, WIDTH),
+            vmem(chunks, depth // 2, each, WIDTH),
+            vmem(chunks, each, WIDTH, dtype=F32),
+            vmem(chunks, depth - 1, each, WIDTH),
+            vmem(2, count, rows // count, wide),
+            vmem(rows, wide),
+            vmem(count, 8, each, dtype=F32),
+            vmem(count, 8, each, dtype=F32),
+            pltpu.SemaphoreType.DMA((chunks, 5 + depth)),
+            pltpu.SemaphoreType.DMA((chunks, 5 + depth)),
+            pltpu.SemaphoreType.DMA((16,)),
+            pltpu.SemaphoreType.DMA((3, count)),
+            pltpu.SemaphoreType.DMA((3, count)),
+            pltpu.SemaphoreType.DMA((2, 3)),
+            pltpu.SemaphoreType.DMA((3,)),
+        ],
+        compiler_params=pltpu.CompilerParams(
+            collective_id=ident, has_side_effects=True, vmem_limit_bytes=62 << 20
+        ),
+        name="attend_back",
+    )(
+        dh2_half, middle, cot, w_out.reshape(depth, GROUP, each, query_cols), w_qkv, mixed, q_rot, k_rot, value,
+        prob, tokens, half_result, scale1, scale2, gain_a, gain_f, cosine, sine, into,
+    )
+
+
+def settle_kernel(
+    sum_0, sum_1, sum_d, grad_qkv, grad_out, grad_gain, norm, new_ffn, new_down, new_out,
+    ffn, shares, store, unit_send, unit_recv, unit_local, all_send, all_recv,
+):
+    z, p, core, one, two, three = places()
+    count = shares.shape[0] // 2
+    me = z * GROUP + p
+    each, units = ffn.shape[1], sum_d.shape[1]
+    span = units // 2
+
+    def anyone(s):
+        t = lax.rem(me * 2 + core + s, 2 * count)
+        return (t // (2 * GROUP), lax.rem(t // 2, GROUP), lax.rem(t, 2))
+
+    barrier = pltpu.get_barrier_semaphore()
+
+    def greet(s, carry):
+        pl.semaphore_signal(barrier, inc=1, device_id=anyone(s), device_id_type=MESH)
+        return carry
+
+    lax.fori_loop(1, 2 * count, greet, 0)
+
+    def unit_parts(q, of):
+        rows = pl.ds(pl.multiple_of(q * each, each), each)
+
+        def place(i, shift, size):
+            return ffn.at[i, :, pl.ds(pl.multiple_of(of * units + shift, span), size)]
+
+        return [
+            (sum_d.at[rows], place(2, 0, units)),
+            (sum_0.at[rows, pl.ds(0, span)], place(0, 0, span)),
+            (sum_0.at[rows, pl.ds(span, span)], place(1, 0, span)),
+            (sum_1.at[rows, pl.ds(0, span)], place(0, span, span)),
+            (sum_1.at[rows, pl.ds(span, span)], place(1, span, span)),
+        ]
+
+    stay = [
+        pltpu.make_async_copy(src, dst, unit_local.at[i])
+        for i, (src, dst) in enumerate(unit_parts(p, p))
+    ]
+    for copy in stay:
+        copy.start()
+    pl.semaphore_wait(barrier, 2 * count - 1)
+    shared = []
+    for i in range(5):
+        for k, q in ((3, three), (1, one), (2, two)):
+            src, dst = unit_parts(q, p)[i]
+            copy = to(src, dst, unit_send.at[k, i], unit_recv.at[k, i], (z, q, core))
+            copy.start()
+            shared.append(copy)
+
+    def squares(value):
+        return jnp.sum(jnp.sum(value * value, axis=0, keepdims=True), axis=1, keepdims=True)
+
+    gain = grad_gain[...]
+    total = 0.5 * squares(gain[:2])
+    for at in range(0, grad_qkv.shape[1], WIDTH):
+        total = total + squares(grad_qkv[:, at : at + WIDTH])
+    for at in range(0, grad_out.shape[1], 128):
+        value = grad_out[:, at : at + 128]
+        total = total + squares(value)
+        new_out[at : at + 128, :] = value.T
+    for copy in stay:
+        copy.wait()
+    for copy in shared[:3]:
+        copy.wait_recv()
+    for at in range(0, new_down.shape[0], 128):
+        value = ffn[2, :, at : at + 128].astype(F32)
+        total = total + squares(value)
+        new_down[at : at + 128, :] = value.T
+    for copy in shared[3:]:
+        copy.wait_recv()
+    keep = pltpu.make_async_copy(ffn.at[pl.ds(0, 2)], new_ffn, store)
+    keep.start()
+    for i in range(2):
+        for at in range(0, GROUP * units, WIDTH):
+            total = total + squares(ffn[i, :, at : at + WIDTH].astype(F32))
+    shares[0] = jnp.broadcast_to(total, (8, 128))
+
+    def tell(s):
+        return to(shares.at[0], shares.at[s], all_send.at[s], all_recv.at[s], anyone(s))
+
+    def tell_start(s, carry):
+        tell(s).start()
+        return carry
+
+    def tell_end(s, carry):
+        tell(s).wait_recv()
+        return carry
+
+    def tell_left(s, carry):
+        tell(s).wait_send()
+        return carry
+
+    lax.fori_loop(1, 2 * count, tell_start, 0)
+    lax.fori_loop(1, 2 * count, tell_end, 0)
+    norm[...] = jnp.sqrt(jnp.sum(shares[...], axis=0))
+    lax.fori_loop(1, 2 * count, tell_left, 0)
+    for copy in shared:
+        copy.wait_send()
+    keep.wait()
+
+
+def settle(sum_0, sum_1, sum_d, grad_qkv, grad_out, grad_gain, ident):
+    count = lax.axis_size("line") * GROUP
+    each, units = grad_qkv.shape[0], sum_d.shape[1]
+    return pl.pallas_call(
+        settle_kernel,
+        out_shape=[
+            jax.ShapeDtypeStruct((8, 128), F32),
+            jax.ShapeDtypeStruct((2, each, GROUP * units), BF),
+            jax.ShapeDtypeStruct((GROUP * units, each), F32),
+            jax.ShapeDtypeStruct(grad_out.shape[::-1], F32),
+        ],
+        in_specs=[ANY] * 3 + [WHOLE] * 3,
+        out_specs=[WHOLE, ANY, WHOLE, WHOLE],
+        scratch_shapes=[
+            pltpu.VMEM((3, each, GROUP * units), BF),
+            pltpu.VMEM((2 * count, 8, 128), F32),
+            pltpu.SemaphoreType.DMA,
+            pltpu.SemaphoreType.DMA((4, 5)),
+            pltpu.SemaphoreType.DMA((4, 5)),
+            pltpu.SemaphoreType.DMA((5,)),
+            pltpu.SemaphoreType.DMA((2 * count,)),
+            pltpu.SemaphoreType.DMA((2 * count,)),
+        ],
+        compiler_params=pltpu.CompilerParams(
+            collective_id=ident, has_side_effects=True, vmem_limit_bytes=24 << 20
+        ),
+        name="settle",
+    )(sum_0, sum_1, sum_d, grad_qkv, grad_out, grad_gain)
+
+
+def update_kernel(limit, norm, gain, qkv, ffn, down, out, *refs):
+    weights, moments, new_moments, new_weights = refs[:9], refs[9:18], refs[18:27], refs[27:36]
+    w_buf, m_buf = refs[36:45], refs[45:54]
+    qkv_buf, ffn_buf, down_buf, out_buf, loads, stores, grads = refs[54:]
+    sources = {
+        6: pltpu.make_async_copy(ffn, ffn_buf, grads.at[0]),
+        8: pltpu.make_async_copy(down, down_buf, grads.at[1]),
+        1: pltpu.make_async_copy(qkv, qkv_buf, grads.at[2]),
+        4: pltpu.make_async_copy(out, out_buf, grads.at[3]),
+    }
+    order = (0, 5, 2, 3, 1, 4, 8, 6, 7)
+    pending = {}
+    for i in order:
+        if i in sources and i != 1:
+            sources[i].start()
+        if i == 2:
+            sources[1].start()
+        pending[i] = [
+            pltpu.make_async_copy(weights[i], w_buf[i], loads.at[0, i]),
+            pltpu.make_async_copy(moments[i], m_buf[i], loads.at[1, i]),
+        ]
+        for copy in pending[i]:
+            copy.start()
+    factor = 0.5 * jnp.minimum(1.0, limit / norm[:1, :1])
+    writes = []
+    everything = slice(None)
+    base = qkv_buf.shape[1] // 2
+
+    def update(i, at, grad):
+        m = 0.5 * m_buf[i][at] + factor * grad
+        w = w_buf[i][at]
+        m_buf[i][at] = m
+        w_buf[i][at] = w - LEARN * (m + DECAY * w)
+
+    for i in order:
+        if i in sources and i != 1:
+            sources[i].wait()
+        if i == 2:
+            sources[1].wait()
+        for copy in pending[i]:
+            copy.wait()
+        if i in (0, 5):
+            update(i, (everything, everything), gain[i // 5 : i // 5 + 1, :])
+        elif i in (1, 2, 3):
+            shift = 0 if i == 1 else base + (i - 2) * w_buf[2].shape[1]
+            for at in range(0, w_buf[i].shape[1], WIDTH):
+                update(i, (everything, slice(at, at + WIDTH)), qkv_buf[:, shift + at : shift + at + WIDTH])
+        elif i in (6, 7):
+            for at in range(0, w_buf[i].shape[1], WIDTH):
+                cols = (everything, slice(at, at + WIDTH))
+                update(i, cols, ffn_buf[(i - 6, *cols)].astype(F32))
+        else:
+            source = down_buf if i == 8 else out_buf
+            for at in range(0, w_buf[i].shape[0], WIDTH):
+                rows = (slice(at, at + WIDTH), everything)
+                update(i, rows, source[rows])
+        for buf, new, j in ((m_buf, new_moments, 0), (w_buf, new_weights, 1)):
+            writes.append(pltpu.make_async_copy(buf[i], new[i], stores.at[j, i]))
+            writes[-1].start()
+    for copy in writes:
+        copy.wait()
+
+
+def update(norm, gain, qkv, ffn, down, out, weights, moments, limit):
+    like = [jax.ShapeDtypeStruct(v.shape, F32) for v in weights]
+    size = sum(v.size for v in weights)
+    return pl.pallas_call(
+        functools.partial(update_kernel, limit),
+        out_shape=[*like, *like],
+        in_specs=[WHOLE] * 2 + [ANY] * 22,
+        out_specs=[ANY] * 18,
+        scratch_shapes=[pltpu.VMEM(v.shape, F32) for v in (*weights, *moments)]
+        + [pltpu.VMEM(v.shape, v.dtype) for v in (qkv, ffn, down, out)]
+        + [
+            pltpu.SemaphoreType.DMA((2, 9)),
+            pltpu.SemaphoreType.DMA((2, 9)),
+            pltpu.SemaphoreType.DMA((4,)),
+        ],
+        compiler_params=pltpu.CompilerParams(vmem_limit_bytes=40 << 20),
+        cost_estimate=pl.CostEstimate(flops=7 * size, bytes_accessed=20 * size, transcendentals=0),
+        name="update",
+    )(norm, gain, qkv, ffn, down, out, *weights, *moments)
+
+
 class Ways:
     def __init__(self):
         self.depth = lax.axis_size("line")
@@ -845,17 +1103,6 @@
         one, two = self.flip(value, 1), self.flip(value, 2)
         three = jnp.concatenate([self.flip(one[:half], 2), self.flip(two[half:], 1)])
         return [value, one, two, three]
-
-    def scatter_group(self, parts):
-        half = parts[0].shape[0] // 2
-        first = self.flip(parts[3][:half].astype(BF), 2).astype(F32)
-        second = self.flip(parts[3][half:].astype(BF), 1).astype(F32)
-        one = jnp.concatenate([parts[1][:half] + first, parts[1][half:]]).astype(BF)
-        two = jnp.concatenate([parts[2][:half], parts[2][half:] + second]).astype(BF)
-        return parts[0] + self.flip(one, 1).astype(F32) + self.flip(two, 2).astype(F32)
-
-    def exchange(self, value):
-        return lax.all_to_all(value, ("line", "group"), split_axis=0, concat_axis=0, tiled=True)
 
     def own_half(self, value):
         half = value.shape[-1] // 2
@@ -1040,67 +1287,33 @@
     terms_1 = mat_tn(after(group_h2, half_dh2), grads_1).astype(BF)
     sum_1 = ways.scatter_line(terms_1)
     half_dh2 = after(half_dh2, terms_1)
-    half_result = ways.own_half(middle) + half_ffn
-
-    grad_h2 = ways.join(half_dh2, ways.swap(half_dh2)) + 0.0 * sum_0[0, 0].astype(F32)
-    grad_gf = jnp.sum(grad_h2 * normed2, axis=0)
-    grad_mid = dealt_cot.astype(F32) + norm_back(grad_h2, normed2, scale2, gain_f)
-    mid_low = grad_mid.astype(BF)
-
-    grad_mixed = (
-        mat_nn(mid_low, weight_out).astype(BF).reshape(rows, heads_kv, head_group, HEAD_SIZE)
-    )
-    grad_wo = mat_tn(mid_low, mixed)
-    grad_prob = jnp.einsum("rhgd,chd->hgrc", grad_mixed, value, preferred_element_type=F32)
-    delta = jnp.sum(prob * grad_prob, axis=-1, keepdims=True)
-    grad_scores = (prob * (grad_prob - delta)).astype(BF)
-    grad_qrot = (
-        jnp.einsum("hgrc,chd->rhgd", grad_scores, key_rot, preferred_element_type=F32) * root
-    )
-    grad_krot = (
-        jnp.einsum("hgrc,rhgd->chd", grad_scores, query_rot, preferred_element_type=F32) * root
-    )
-    grad_value = jnp.einsum("hgrc,rhgd->chd", prob_low, grad_mixed, preferred_element_type=F32)
-    grad_q = (
-        unrotate(grad_qrot.reshape(rows, heads_q, HEAD_SIZE), cosine, sine)
-        .reshape(rows, heads_q * HEAD_SIZE)
-        .astype(BF)
-    )
-    grad_k = unrotate(grad_krot, cosine, sine).reshape(rows, heads_kv * HEAD_SIZE).astype(BF)
-    grad_v = grad_value.reshape(rows, heads_kv * HEAD_SIZE).astype(BF)
-
-    grad_qkv = jnp.concatenate([grad_q, grad_k, grad_v], axis=1)
-    part = mat_nt(grad_qkv, weight_qkv)
-    other = ways.swap(part.astype(BF)).astype(F32)
-    terms_qkv = mat_tn(hidden1, grad_qkv).astype(BF)
-    grad_h1 = part + other
-    grad_ga = jnp.sum(grad_h1 * normed1, axis=0)
-    grad_in = grad_mid + norm_back(grad_h1, normed1, scale1, gain_a)
-    slots = mat_tn(
-        into, jnp.concatenate([half_result, ways.own_half(grad_in)], axis=1).astype(BF)
-    ).astype(BF)
-    gain_terms = jnp.pad(
-        jnp.stack([grad_ga, grad_gf]).reshape(2, ways.n, -1).swapaxes(0, 1), ((0, 0), (0, 6), (0, 0))
-    )
-    new_qkv, new_out, new_gate, new_up, new_down, new_gain, norm, back = finish(
-        grad_wo.astype(BF), terms_qkv, sum_0, sum_1, sum_d,
-        slots.reshape(ways.n, -1, width), gain_terms, 3,
-    )
+    half_result = (ways.own_half(middle) + half_ffn).astype(BF)
+    dh2_first = half_dh2 + 0.0 * sum_0[0, 0].astype(F32)
+    new_qkv, new_out, new_gain, back = attend_back(
+        dh2_first,
+        middle,
+        dealt_cot,
+        weight_out,
+        weight_qkv,
+        mixed,
+        query_rot.reshape(rows, -1),
+        key_rot.reshape(rows, -1),
+        value.reshape(rows, -1),
+        prob.reshape(heads_q, rows, rows),
+        dealt,
+        half_result,
+        scale1,
+        scale2,
+        gain_a.reshape(1, width),
+        gain_f.reshape(1, width),
+        cosine[:, 0],
+        sine[:, 0],
+        into,
+        6,
+    )
+    norm, new_ffn, new_down, new_out_t = settle(sum_0, sum_1, sum_d, new_qkv, new_out, new_gain, 7)
     activations = mat_tn(out, back[0].reshape(rows, width)).astype(BF)
     input_grad = mat_tn(out, back[1].reshape(rows, width)).astype(BF)
-    owned = (
-        new_gain[0],
-        new_qkv[:, :wide_q],
-        new_qkv[:, wide_q : wide_q + wide_k],
-        new_qkv[:, wide_q + wide_k :],
-        new_out,
-        new_gain[1],
-        new_gate,
-        new_up,
-        new_down,
-    )
-    grad_norm = norm[0, 0]
-    factor = jnp.minimum(1.0, math.sqrt(PARAMS) / grad_norm)
     weights = (gain_attn, w_query, key_weight, value_weight, w_out, gain_ffn, w_gate, w_up, w_down)
     moments = (
         moment_gain_attn,
@@ -1113,9 +1326,12 @@
         moment_w_up,
         moment_w_down,
     )
-    new_moments = tuple(0.5 * m + 0.5 * factor * g for m, g in zip(moments, owned))
-    new_weights = tuple(w - LEARN * (m + DECAY * w) for w, m in zip(weights, new_moments))
-    return (activations, input_grad, grad_norm, *new_moments, *new_weights)
+    flat = [v if v.ndim == 2 else v.reshape(1, -1) for v in (*weights, *moments)]
+    new = update(
+        norm, new_gain, new_qkv, new_ffn, new_down, new_out_t, flat[:9], flat[9:], math.sqrt(PARAMS)
+    )
+    new = [v.reshape(old.shape) for v, old in zip(new, (*weights, *weights))]
+    return (activations, input_grad, norm[0, 0], *new)
 
 
 def solution(mesh):

time: 892 us -> 845 us (0.947)
  Pallas kernels: 513 us -> 562 us
  matrix products: 133 us -> 99.1 us
  other arithmetic: 90.1 us -> 57.5 us
  waiting for transfers between devices: 47.6 us -> 16.3 us
    pallas_call x1 -> x3, Pallas kernels: 202 us -> 251 us  [the longest x1 193 us: attend_back(): pl.pallas_call(attend_back_kernel, out_shape=[jax.ShapeDtypeStruct((each,...]
    reduce_scatter x3, waiting for transfers between devices: 26.1 us -> 0.01 us  [scatter_line(): return lax.psum_scatter(whole, 'line', scatter_dimension=0, tiled=True)]
    sub x7 -> x1, other arithmetic: 16.7 us -> 0.17 us  [apply_rotary(): first * cosine - second * sine]
    dot_general x8 -> x5, matrix products: 57.4 us -> 42.8 us  [mat_tn(): lax.dot_general(left, right, (((0,), (0,)), ((), ())), preferred_element_...]
    dot_general x2 -> x1, matrix products: 11.9 us -> 2.39 us  [mat_nt(): lax.dot_general(left, right, (((1,), (1,)), ((), ())), preferred_element_...]
    dot_general x11 -> x10, matrix products: 54.9 us -> 52.5 us  [mat_nn(): return jnp.dot(left, right, preferred_element_type=F32)]
    unnamed x175 -> x151, local copies, waits for them, and re-layouts: 36.7 us -> 36.2 us
  transfers between devices with their start and end apart: 13 -> 11, of which waited for: 6 -> 3; matrix products, arithmetic and copies ran while one was open for 24% -> 21% of each run, Pallas kernels for 35% -> 60%
where the time goes in v4:
time: 845 us; the launch traced here: 840 us
  Pallas kernels  562 us (67%)
  matrix products  99.1 us (12%)
  local copies, waits for them, and re-layouts  84.9 us (10%)
  other arithmetic  57.5 us (7%)
  waiting for transfers between devices  16.3 us (2%)
  between operations  15.7 us (2%)
    pallas_call x1, Pallas kernels, attend_back(): pl.pallas_call(attend_back_kernel, out_shape=[jax.ShapeDtypeStruct((each,...  193 us
    pallas_call x1, Pallas kernels, share_weights(): pl.pallas_call(functools.partial(share_weights_kernel, n), out_shape=[jax...  105 us
    pallas_call x1, Pallas kernels, sum_rows(): pl.pallas_call(functools.partial(sum_rows_kernel, sizes), out_shape=[jax....  85.7 us
    pallas_call x1, Pallas kernels, deal(): pl.pallas_call(deal_kernel, out_shape=[jax.ShapeDtypeStruct((count, per,...  78.5 us
    dot_general x10, matrix products, mat_nn(): return jnp.dot(left, right, preferred_element_type=F32)  52.5 us
    pallas_call x1, Pallas kernels, settle(): pl.pallas_call(settle_kernel, out_shape=[jax.ShapeDtypeStruct((8, 128), F...  49.2 us
    dot_general x5, matrix products, mat_tn(): lax.dot_general(left, right, (((0,), (0,)), ((), ())), preferred_element_...  42.8 us
    pallas_call x1, Pallas kernels, share_rows(): pl.pallas_call(share_rows_kernel, out_shape=jax.ShapeDtypeStruct((GROUP *...  41 us
  transfers between devices with their start and end apart: 11, of which 3 were waited for; matrix products, arithmetic and copies ran while one was open for 21% of the time, Pallas kernels for 60%

profile of v4, /device:TPU:0, one launch (start us, length us, event | category | flops | bytes accessed | tf_op | source)
XLA Modules:
  0.0 840.3 jit_solution(8168916935637291274)
XLA Ops:
  24.6 2.6 convolution_convert_fusion.6
  29.1 78.5 %deal.1 = (bf16[16,32,2048]{2,1,0:T(8,128)(2,1)}, bf16[16,32,1024]{2,1,0:T(8,128)(2,1)}, bf16[3,4,128,1024]{3,2,1,0:T(8,128)(2,1)}, f32[16,8,128]{2,1,0:T(8,128)}) custom-call(bf16[16,32,2048]{2,1,0:T(8,128)(2,1)} %bitcast.149, bf16[4,3,128,1024]{3,2,1,0:T(8,128)(2,1)} %pad_maximum_fusion.3.pieces, f32[8,128]{1,0:T(8,128)} %fusion.52.gains), custom_call_target="tpu_custom_call" | custom-call | tf_op jit(solution)/shard_map/deal/pallas_call | solution.py:504
  109.2 3.1 fusion.1
  116.8 7.9 all-gather.3.cloned.1.call-done
  124.7 3.0 slice.234
  127.8 3.9 copy.96
  131.7 2.4 slice.235
  134.1 2.4 copy.97
  136.5 105.3 %share_weights.1 = (bf16[4,4,128,2048]{3,2,1,0:T(8,128)(2,1)}, bf16[4,4,128,1024]{3,2,1,0:T(8,128)(2,1)}) custom-call(bf16[4,128,2048]{2,1,0:T(8,128)(2,1)} %bitcast.139, bf16[4,128,1024]{2,1,0:T(8,128)(2,1)} %bitcast.143), custom_call_target="tpu_custom_call" | custom-call | tf_op jit(solution)/shard_map/share_weights/pallas_call | solution.py:204
  243.8 3.1 fusion.11
  249.2 2.0 copy.126
  251.2 6.0 fusion.4
  257.2 2.2 reshape.313
  262.8 2.3 fusion.67
  265.1 2.6 broadcast_divide_fusion
  267.8 1.9 slice.236
  270.6 2.9 fusion.26.value
  276.0 2.4 constant_dynamic-update-slice_fusion.4
  278.4 2.3 constant_dynamic-update-slice_fusion.3
  280.7 2.3 constant_dynamic-update-slice_fusion.2
  283.0 2.0 constant_dynamic-update-slice_fusion.1
  288.5 2.4 fusion.68
  291.5 6.4 collective-permute-done.5
  299.2 1.9 copy-done.26
  302.9 41.0 %share_rows.1 = bf16[2048,2048]{1,0:T(8,128)(2,1)} custom-call(bf16[512,2048]{1,0:T(8,128)(2,1)} %multiply_convert_fusion.6.h), custom_call_target="tpu_custom_call" | custom-call | tf_op jit(solution)/shard_map/share_rows/pallas_call | solution.py:145
  343.9 11.4 %maximum_select_fusion = bf16[2048,2048]{1,0:T(8,128)(2,1)} fusion(bf16[2048,1024]{1,0:T(8,128)(2,1)} %collective-permute-done.4, bf16[2048,1024]{1,0:T(8,128)(2,1)} %constant_dynamic-update-slice_fusion, pred[]{:T(512)S(6)} %eq.91), kind=kLoop, calls=%fused_computation.2 | loop fusion | flops 37748736 | bytes 16777216 | tf_op jit(solution)/shard_map/jit(_where)/select_n | solution.py:1116
  355.3 7.5 fusion.62
  364.0 11.4 %fusion.69 = f32[2048,1024]{1,0:T(8,128)} fusion(bf16[2048,2048]{1,0:T(8,128)(2,1)S(1)} %copy-done.31, bf16[2048,1024]{1,0:T(8,128)(2,1)S(1)} %bitcast.131), kind=kOutput, calls=%fused_computation.165 | convolution fusion | flops 8589934592 | bytes 20971520 | tf_op jit(solution)/shard_map/dot_general | solution.py:56
  375.5 9.1 %fusion.70 = f32[2048,1024]{1,0:T(8,128)S(1)} fusion(bf16[2048,2048]{1,0:T(8,128)(2,1)S(1)} %bitcast.138, bf16[2048,1024]{1,0:T(8,128)(2,1)S(1)} %bitcast.129), kind=kOutput, calls=%fused_computation.166 | convolution fusion | flops 8589934592 | bytes 20971520 | tf_op jit(solution)/shard_map/dot_general | solution.py:56
  384.6 4.8 multiply_convert_fusion.5
  391.4 11.0 %convolution_convert_fusion.2 = bf16[2048,1024]{1,0:T(8,128)(2,1)} fusion(bf16[2048,2048]{1,0:T(8,128)(2,1)S(1)} %bitcast.138, bf16[2048,512]{1,0:T(8,128)(2,1)S(1)} %get-tuple-element.106, bf16[2048,512]{1,0:T(8,128)(2,1)S(1)} %get-tuple-element.105), kind=kOutput, calls=%fused_computation.30 | convolution fusion | flops 8600420352 | bytes 16777216 | tf_op jit(solution)/shard_map/dot_general | solution.py:64
  402.5 12.5 %fusion.71 = f32[2048,1024]{1,0:T(8,128)S(1)} fusion(bf16[2048,2048]{1,0:T(8,128)(2,1)} %share_rows.1, bf16[2048,1024]{1,0:T(8,128)(2,1)} %bitcast.127), kind=kOutput, calls=%fused_computation.167 | convolution fusion | flops 8589934592 | bytes 20971520 | tf_op jit(solution)/shard_map/dot_general | solution.py:56
  415.0 5.9 multiply_convert_fusion.3
  422.2 12.9 %convolution_convert_fusion.1 = bf16[2048,1024]{1,0:T(8,128)(2,1)} fusion(bf16[2048,2048]{1,0:T(8,128)(2,1)} %maximum_select_fusion, bf16[2048,512]{1,0:T(8,128)(2,1)S(1)} %get-tuple-element.111, bf16[2048,512]{1,0:T(8,128)(2,1)S(1)} %get-tuple-element.110), kind=kOutput, calls=%fused_computation.29 | convolution fusion | flops 8600420352 | bytes 16777216 | tf_op jit(solution)/shard_map/dot_general | solution.py:64
  435.2 5.0 pad_maximum_fusion.1.refs_2_
  440.3 2.7 pad_maximum_fusion.refs_0_
  442.9 2.7 pad_maximum_fusion.2.refs_4_
  445.7 85.7 %sum_rows.1 = (f32[512,1024]{1,0:T(8,128)}, f32[512,1024]{1,0:T(8,128)}) custom-call(bf16[2048,1024]{1,0:T(8,128)(2,1)} %pad_maximum_fusion.refs_0_, bf16[2048,1024]{1,0:T(8,128)(2,1)} %bitcast.130, bf16[2048,1024]{1,0:T(8,128)(2,1)} %pad_maximum_fusion.1.refs_2_, bf16[2048,1024]{1,0:T(8,128)(2,1)} %bitcast.128, ...), custom_call_target="tpu_custom_call" | custom-call | tf_op jit(solution)/shard_map/sum_rows/pallas_call | solution.py:382
  531.4 13.4 %convolution_convert_fusion = bf16[2048,1024]{1,0:T(8,128)(2,1)} fusion(bf16[2048,2048]{1,0:T(8,128)(2,1)} %share_rows.1, bf16[2048,512]{1,0:T(8,128)(2,1)S(1)} %copy-done.40, bf16[2048,512]{1,0:T(8,128)(2,1)S(1)} %copy-done.39), kind=kOutput, calls=%fused_computation.28 | convolution fusion | flops 8600420352 | bytes 16777216 | tf_op jit(solution)/shard_map/dot_general | solution.py:64
  546.6 5.4 copy.114
  556.9 3.3 slice.255.cot
  560.2 3.4 fusion.10.half_result
  566.9 193.0 %attend_back.1 = (f32[128,2048]{1,0:T(8,128)}, f32[128,1024]{1,0:T(8,128)}, f32[8,128]{1,0:T(8,128)}, bf16[2,16,32,2048]{3,2,1,0:T(8,128)(2,1)}) custom-call(f32[512,1024]{1,0:T(8,128)} %broadcast_add_fusion.dh2_half, f32[512,2048]{1,0:T(8,128)} %copy-done.26, bf16[512,2048]{1,0:T(8,128)(2,1)} %slice.255.cot, ...), custom_call_target="tpu_custom_call" | custom-call | tf_op jit(solution)/shard_map/attend_back/pallas_call | solution.py:809
  759.9 2.7 fusion.63
  762.7 2.7 convolution_convert_fusion.3
  765.4 2.7 convolution_convert_fusion.4
  773.0 49.2 %settle.1 = (f32[8,128]{1,0:T(8,128)S(1)}, bf16[2,128,4096]{2,1,0:T(8,128)(2,1)S(1)}, f32[4096,128]{1,0:T(8,128)S(1)}, f32[1024,128]{1,0:T(8,128)S(1)}) custom-call(bf16[512,1024]{1,0:T(8,128)(2,1)S(1)} %copy-done.11, bf16[512,1024]{1,0:T(8,128)(2,1)S(1)} %copy-done.13, bf16[512,1024]{1,0:T(8,128)(2,1)S(1)} %copy-done.12, f32[128,2048]{1,0:T(8,128)S(1)} %copy-done.6, ...), custom_call_target="tpu_custom_call" | custom-call | tf_op jit(solution)/shard_map/settle/pallas_call | solution.py:969
  824.4 9.0 %update.1 = (f32[1,128]{1,0:T(1,128)}, f32[128,1024]{1,0:T(8,128)}, f32[128,512]{1,0:T(8,128)}, f32[128,512]{1,0:T(8,128)}, f32[1024,128]{1,0:T(8,128)}, /*index...) custom-call(f32[8,128]{1,0:T(8,128)S(1)} %get-tuple-element.77.norm,, ...), custom_call_target="tpu_custom_call" | custom-call | flops 13764352 | bytes 39326720 | tf_op jit(solution)/shard_map/update/pallas_call | solution.py:1062
  (235 shorter events, 64.2 us)
Async XLA Ops:
  7.2 100.7 %copy-start = (s32[64]{0:T(128)S(1)}, s32[64]{0:T(128)}, u32[]{:S(2)}) copy-start(s32[64]{0:T(128)} %param.25) | copy-start | bytes 772
  7.2 5.7 copy-start.61
  7.2 6.4 copy-start.4
  7.2 117.5 %all-gather.3.cloned.1.call-start = ((), (), s32[]{:S(2)}) async-start(), calls=%async_computation.3 | async-start | bytes 3932160 | tf_op jit(solution)/shard_map/all_gather | solution.py:1096
  12.8 342.5 %all-gather.5.cloned.1.call-start = ((), (), s32[]{:S(2)}) async-start(), calls=%async_computation.4 | async-start | bytes 15728640 | tf_op jit(solution)/shard_map/all_gather | solution.py:1217
  13.6 11.0 %copy-start.64 = (s32[512]{0:T(512)}, s32[512]{0:T(512)S(1)}, u32[]{:S(2)}) copy-start(s32[512]{0:T(512)S(1)} %eq.88) | copy-start | bytes 6148
  29.1 78.7 %copy-start.67 = (s32[64]{0:T(128)S(1)}, s32[64]{0:T(128)}, u32[]{:S(2)}) copy-start(s32[64]{0:T(128)} %param.26) | copy-start | bytes 772
  107.6 456.0 %reduce-scatter.4.cloned.1.call-start = ((), (), s32[]{:S(2)}) async-start(), calls=%async_computation.5 | async-start | bytes 5242880 | tf_op jit(solution)/shard_map/reduce_scatter | solution.py:1099
  112.3 138.9 %copy-start.33 = (bf16[512,2048]{1,0:T(8,128)(2,1)}, bf16[512,2048]{1,0:T(8,128)(2,1)S(1)}, u32[]{:S(2)}) copy-start(bf16[512,2048]{1,0:T(8,128)(2,1)S(1)} %get-tuple-element.147.tokens) | copy-start | bytes 6291460
  113.5 147.5 %copy-start.47 = (f32[512,128]{1,0:T(8,128)}, f32[512,128]{1,0:T(8,128)S(1)}, u32[]{:S(2)}) copy-start(f32[512,128]{1,0:T(8,128)S(1)} %get-tuple-element.144.cosine) | copy-start | bytes 786436
  113.5 147.5 %copy-start.48 = (f32[512,128]{1,0:T(8,128)}, f32[512,128]{1,0:T(8,128)S(1)}, u32[]{:S(2)}) copy-start(f32[512,128]{1,0:T(8,128)S(1)} %get-tuple-element.145.sine) | copy-start | bytes 786436
  241.7 32.0 %collective-permute-start.1 = (bf16[512,1024]{1,0:T(8,128)(2,1)}, bf16[512,1024]{1,0:T(8,128)(2,1)}, u32[]{:S(2)}, u32[]{:S(2)}) collective-permute-start(bf16[512,1024]{1,0:T(8,128)(2,1)} %convolution_convert_fusion.7), channel_id=1, source_target_pairs={{0,4},{2,6},{4,0},{6,2},{1,5},{3,7},{5,1},{7,3},{8,12},{10,14},{12... | collective-permute-start | bytes 3145736 | tf_op jit(solution)/shard_map/ppermute | solution.py:1090
  242.8 25.0 %collective-permute-start = (bf16[512,1024]{1,0:T(8,128)(2,1)}, bf16[512,1024]{1,0:T(8,128)(2,1)}, u32[]{:S(2)}, u32[]{:S(2)}) collective-permute-start(bf16[512,1024]{1,0:T(8,128)(2,1)} %convolution_convert_fusion.7), channel_id=1, source_target_pairs={{0,2},{2,0},{4,6},{6,4},{1,3},{3,1},{5,7},{7,5},{8,10},{10,8},{12,... | collective-permute-start | bytes 3145736 | tf_op jit(solution)/shard_map/ppermute | solution.py:1090
  265.1 5.5 copy-start.34
  269.7 13.4 %collective-permute-start.2 = (bf16[256,1024]{1,0:T(8,128)(2,1)}, bf16[256,1024]{1,0:T(8,128)(2,1)}, u32[]{:S(2)}, u32[]{:S(2)}) collective-permute-start(bf16[256,1024]{1,0:T(8,128)(2,1)} %slice.236), channel_id=1, source_target_pairs={{0,4},{2,6},{4,0},{6,2},{1,5},{3,7},{5,1},{7,3},{8,12},{10,14},{12... | collective-permute-start | bytes 1572872 | tf_op jit(solution)/shard_map/ppermute | solution.py:1090
  273.5 9.5 %copy-start.56 = (bf16[512,512]{1,0:T(8,128)(2,1)}, bf16[512,512]{1,0:T(8,128)(2,1)S(1)}, u32[]{:S(2)}) copy-start(bf16[512,512]{1,0:T(8,128)(2,1)S(1)} %fusion.26.value) | copy-start | bytes 1572868
  274.9 12.9 %copy-start.28 = (f32[2,2,512,512]{2,3,1,0:T(8,128)S(1)}, f32[2,2,512,512]{2,3,1,0:T(8,128)}, u32[]{:S(2)}) copy-start(f32[2,2,512,512]{2,3,1,0:T(8,128)} %broadcast_divide_fusion) | copy-start | bytes 12582916
  274.9 12.0 %collective-permute-start.3 = (bf16[256,1024]{1,0:T(8,128)(2,1)S(1)}, bf16[256,1024]{1,0:T(8,128)(2,1)S(1)}, u32[]{:S(2)}, u32[]{:S(2)}) collective-permute-start(bf16[256,1024]{1,0:T(8,128)(2,1)S(1)} %slice.237), channel_id=1, source_target_pairs={{0,2},{2,0},{4,6},{6,4},{1,3},{3,1},{5,7},{7,5},{8,10},{10,8},{12,... | collective-permute-start | bytes 1572872 | tf_op jit(solution)/shard_map/ppermute | solution.py:1090
  283.0 5.4 copy-start.49
  287.7 56.2 %collective-permute-start.4 = (bf16[2048,1024]{1,0:T(8,128)(2,1)}, bf16[2048,1024]{1,0:T(8,128)(2,1)}, u32[]{:S(2)}, u32[]{:S(2)}) collective-permute-start(bf16[2048,1024]{1,0:T(8,128)(2,1)} %constant_dynamic-update-slice_fusion), channel_id=1, source_target_pairs={{0,1},{1,0},{2,3},{3,2},{4,5},{5,4},{6,7},{7,6},{8,9},{9,8},{10,11... | collective-permute-start | bytes 12582920 | tf_op jit(solution)/shard_map/ppermute | solution.py:1093
  290.9 7.0 collective-permute-start.5
  355.3 8.7 %copy-start.31 = (bf16[2048,2048]{1,0:T(8,128)(2,1)S(1)}, bf16[2048,2048]{1,0:T(8,128)(2,1)}, u32[]{:S(2)}) copy-start(bf16[2048,2048]{1,0:T(8,128)(2,1)} %maximum_select_fusion) | copy-start | bytes 25165828
  355.3 20.2 %slice-start = ((s8[8388608]{0:T(1024)(128)(4,1)}), s8[4194304]{0:T(1024)(128)(4,1)S(1)}, s32[]{:S(2)}) async-start(s8[8388608]{0:T(1024)(128)(4,1)} %bitcast.137), calls=%async_computation.8 | async-start | bytes 8388608
  362.8 12.7 %copy-start.30 = (bf16[1,4,512,1024]{3,2,1,0:T(8,128)(2,1)}, bf16[1,4,512,1024]{3,2,1,0:T(8,128)(2,1)S(1)}, u32[]{:S(2)}) copy-start(bf16[1,4,512,1024]{3,2,1,0:T(8,128)(2,1)S(1)} %get-tuple-element.109) | copy-start | bytes 12582916
  362.8 12.7 %copy-start.29 = (bf16[1,4,512,1024]{3,2,1,0:T(8,128)(2,1)}, bf16[1,4,512,1024]{3,2,1,0:T(8,128)(2,1)S(1)}, u32[]{:S(2)}) copy-start(bf16[1,4,512,1024]{3,2,1,0:T(8,128)(2,1)S(1)} %get-tuple-element.108) | copy-start | bytes 12582916
  364.0 11.4 %slice-start.1 = ((s8[8388608]{0:T(1024)(128)(4,1)}), s8[4194304]{0:T(1024)(128)(4,1)S(1)}, s32[]{:S(2)}) async-start(s8[8388608]{0:T(1024)(128)(4,1)} %bitcast.137), calls=%async_computation.9 | async-start | bytes 8388608
  402.5 365.7 %reduce-scatter.8.cloned.1.call-start = ((), (), s32[]{:S(2)}) async-start(), calls=%async_computation.7 | async-start | bytes 5242880 | tf_op jit(solution)/shard_map/reduce_scatter | solution.py:1099
  435.2 333.0 %reduce-scatter.6.cloned.1.call-start = ((), (), s32[]{:S(2)}) async-start(), calls=%async_computation.6 | async-start | bytes 5242880 | tf_op jit(solution)/shard_map/reduce_scatter | solution.py:1099
  445.7 85.7 %copy-start.39 = (bf16[2048,512]{1,0:T(8,128)(2,1)S(1)}, bf16[2048,512]{1,0:T(8,128)(2,1)}, u32[]{:S(2)}) copy-start(bf16[2048,512]{1,0:T(8,128)(2,1)} %get-tuple-element.103) | copy-start | bytes 6291460
  445.7 85.7 %copy-start.40 = (bf16[2048,512]{1,0:T(8,128)(2,1)S(1)}, bf16[2048,512]{1,0:T(8,128)(2,1)}, u32[]{:S(2)}) copy-start(bf16[2048,512]{1,0:T(8,128)(2,1)} %get-tuple-element.104) | copy-start | bytes 6291460
  546.6 5.4 copy-start.51
  546.6 6.8 copy-start.53
  546.6 6.8 copy-start.55
  560.2 5.2 copy-start.59
  765.4 57.4 %copy-start.5 = (f32[128,4096]{1,0:T(8,128)S(1)}, f32[128,4096]{1,0:T(8,128)}, u32[]{:S(2)}) copy-start(f32[128,4096]{1,0:T(8,128)} %refs_6_.1) | copy-start | bytes 6291460
  765.4 57.4 %copy-start.9 = (f32[128,512]{1,0:T(8,128)S(1)}, f32[128,512]{1,0:T(8,128)}, u32[]{:S(2)}) copy-start(f32[128,512]{1,0:T(8,128)} %refs_3_.1) | copy-start | bytes 786436
  765.4 57.4 %copy-start.21 = (f32[128]{0:T(128)S(1)}, f32[128]{0:T(128)}, u32[]{:S(2)}) copy-start(f32[128]{0:T(128)} %param.33) | copy-start | bytes 1540
  765.4 57.4 %copy-start.23 = (f32[128]{0:T(128)S(1)}, f32[128]{0:T(128)}, u32[]{:S(2)}) copy-start(f32[128]{0:T(128)} %param.28) | copy-start | bytes 1540
  765.4 57.4 %copy-start.24 = (f32[128]{0:T(128)S(1)}, f32[128]{0:T(128)}, u32[]{:S(2)}) copy-start(f32[128]{0:T(128)} %param.37) | copy-start | bytes 1540
  765.4 57.4 %copy-start.25 = (f32[128]{0:T(128)S(1)}, f32[128]{0:T(128)}, u32[]{:S(2)}) copy-start(f32[128]{0:T(128)} %param.42) | copy-start | bytes 1540
  768.1 54.7 %copy-start.7 = (f32[1024,128]{1,0:T(8,128)S(1)}, f32[1024,128]{1,0:T(8,128)}, u32[]{:S(2)}) copy-start(f32[1024,128]{1,0:T(8,128)} %refs_4_.1) | copy-start | bytes 1572868
  768.1 54.7 %copy-start.8 = (f32[128,1024]{1,0:T(8,128)S(1)}, f32[128,1024]{1,0:T(8,128)}, u32[]{:S(2)}) copy-start(f32[128,1024]{1,0:T(8,128)} %refs_1_.1) | copy-start | bytes 1572868
  768.1 54.7 %copy-start.10 = (f32[128,512]{1,0:T(8,128)S(1)}, f32[128,512]{1,0:T(8,128)}, u32[]{:S(2)}) copy-start(f32[128,512]{1,0:T(8,128)} %refs_2_.1) | copy-start | bytes 786436
  773.0 49.8 %copy-start.14 = (f32[128,1024]{1,0:T(8,128)S(1)}, f32[128,1024]{1,0:T(8,128)}, u32[]{:S(2)}) copy-start(f32[128,1024]{1,0:T(8,128)} %refs_10_.1) | copy-start | bytes 1572868
  773.0 49.8 %copy-start.15 = (f32[1024,128]{1,0:T(8,128)S(1)}, f32[1024,128]{1,0:T(8,128)}, u32[]{:S(2)}) copy-start(f32[1024,128]{1,0:T(8,128)} %refs_13_.1) | copy-start | bytes 1572868
  773.0 49.8 %copy-start.17 = (f32[128,512]{1,0:T(8,128)S(1)}, f32[128,512]{1,0:T(8,128)}, u32[]{:S(2)}) copy-start(f32[128,512]{1,0:T(8,128)} %refs_11_.1) | copy-start | bytes 786436
  773.0 49.9 %copy-start.18 = (f32[128,512]{1,0:T(8,128)S(1)}, f32[128,512]{1,0:T(8,128)}, u32[]{:S(2)}) copy-start(f32[128,512]{1,0:T(8,128)} %refs_12_.1) | copy-start | bytes 786436
  824.4 9.1 %copy-start.1 = (s32[64]{0:T(128)S(1)}, s32[64]{0:T(128)}, u32[]{:S(2)}) copy-start(s32[64]{0:T(128)} %param.25) | copy-start | bytes 772
  (33 other events, 76.1 us)
Sparse Core Ops, SparseCore 0:
  12.9 111.7 all-gather.2
  126.3 217.3 all-gather.4
  402.6 84.2 reduce-scatter.3
  489.2 77.2 reduce-scatter.7
  568.6 112.8 reduce-scatter.5

commit v5 on v4

--- a/solution.py
+++ b/solution.py
@@ -24,15 +24,7 @@
     half = head // 2
     freq = THETA ** (-(2.0 * jnp.arange(half, dtype=F32)) / head)
     turned = position[:, None] * freq[None, :]
-    return (jnp.cos(turned)[:, None, :], jnp.sin(turned)[:, None, :])
-
-
-def apply_rotary(value, cosine, sine):
-    half = value.shape[-1] // 2
-    first, second = value[..., :half], value[..., half:]
-    return jnp.concatenate(
-        [first * cosine - second * sine, second * cosine + first * sine], axis=-1
-    )
+    return (jnp.cos(turned), jnp.sin(turned))
 
 
 def layout(block_len, rows):
@@ -43,13 +35,7 @@
     inside = (index[:, None] >= starts[None, :]) & (index[:, None] < ends[None, :])
     segment = jnp.sum(jnp.where(inside, rank[None, :], 0), axis=1)
     position = jnp.sum(jnp.where(inside, index[:, None] - starts[None, :], 0), axis=1)
-    mask = (segment[:, None] == segment[None, :]) & (index[None, :] <= index[:, None])
-    return (position.astype(F32), mask)
-
-
-def normalize(value):
-    scale_inv = lax.rsqrt(jnp.mean(value * value, axis=-1, keepdims=True) + EPS)
-    return (value * scale_inv, scale_inv)
+    return (position.astype(F32), segment.astype(jnp.int32))
 
 
 def mat_nn(left, right):
@@ -95,129 +81,58 @@
     )
 
 
-def share_rows_kernel(h, out, send, recv, local):
+def share_weights_kernel(line, out, held, send, recv, local):
     z, p, core, one, two, _ = places()
-    rows, width = h.shape
-    half, wide = rows // 2, width // 2
-    cols = pl.ds(pl.multiple_of(core * wide, wide), wide)
-    x, y, twin = (z, one, core), (z, two, core), (z, p, 1 - core)
-    meet([x, y, twin])
-    own = pltpu.make_async_copy(h, out.at[pl.ds(0, rows)], local)
-    own.start()
-    first, second = pl.ds(0, half), pl.ds(half, half)
-
-    def part(k, b):
-        return out.at[pl.ds(k * rows + b * half, half), cols]
-
-    copies = {}
-
-    def go(name, i, src, dst, partner):
-        copies[name] = to(src, dst, send.at[i], recv.at[i], partner)
-        copies[name].start()
-
-    go("1a", 0, h.at[first, cols], part(1, 0), x)
-    go("2b", 3, h.at[second, cols], part(2, 1), y)
-    go("1b", 1, h.at[second, cols], part(1, 1), x)
-    go("2a", 2, h.at[first, cols], part(2, 0), y)
-    copies["1a"].wait_recv()
-    go("3a", 4, part(1, 0), part(3, 0), y)
-    copies["2b"].wait_recv()
-    go("3b", 5, part(2, 1), part(3, 1), x)
-    go("t0", 6, part(1, 0), part(1, 0), twin)
-    go("t3", 9, part(2, 1), part(2, 1), twin)
-    copies["1b"].wait_recv()
-    go("t1", 7, part(1, 1), part(1, 1), twin)
-    copies["2a"].wait_recv()
-    go("t2", 8, part(2, 0), part(2, 0), twin)
-    copies["3a"].wait_recv()
-    go("t4", 10, part(3, 0), part(3, 0), twin)
-    copies["3b"].wait_recv()
-    go("t5", 11, part(3, 1), part(3, 1), twin)
-    for i in range(6):
-        copies["t%d" % i].wait_recv()
-    for c in copies.values():
-        c.wait_send()
-    own.wait()
-
-
-def share_rows(h, ident):
-    rows, width = h.shape
-    return pl.pallas_call(
-        share_rows_kernel,
-        out_shape=jax.ShapeDtypeStruct((GROUP * rows, width), h.dtype),
-        in_specs=[WHOLE],
+    x, y = (z, one, core), (z, two, core)
+    half = line.shape[0] // 2
+    cols = pl.ds(0, out.shape[3])
+    low, high = pl.ds(0, half), pl.ds(half, half)
+    load = pltpu.make_async_copy(line.at[:, :, cols], held, local.at[0])
+    load.start()
+    meet([x, y])
+    copies = []
+
+    def go(src, dst, partner):
+        i = len(copies)
+        copies.append(to(src, dst, send.at[i], recv.at[i], partner))
+        copies[i].start()
+
+    go(line.at[low, :, cols], out.at[low, p], x)
+    go(line.at[high, :, cols], out.at[high, p], y)
+    go(line.at[high, :, cols], out.at[high, p], x)
+    go(line.at[low, :, cols], out.at[low, p], y)
+    load.wait()
+    store = pltpu.make_async_copy(held, out.at[:, p], local.at[1])
+    store.start()
+    copies[0].wait_recv()
+    go(out.at[low, one], out.at[low, one], y)
+    copies[1].wait_recv()
+    go(out.at[high, two], out.at[high, two], x)
+    for i in range(2, 6):
+        copies[i].wait_recv()
+    for copy in copies:
+        copy.wait_send()
+    store.wait()
+
+
+def share_weights(line, cols, ident):
+    depth = lax.axis_size("line")
+    each = line.shape[0] // depth
+    out = pl.pallas_call(
+        share_weights_kernel,
+        out_shape=jax.ShapeDtypeStruct((depth, GROUP, each, cols), line.dtype),
+        in_specs=[ANY],
         out_specs=ANY,
         scratch_shapes=[
-            pltpu.SemaphoreType.DMA((12,)),
-            pltpu.SemaphoreType.DMA((12,)),
-            pltpu.SemaphoreType.DMA,
-        ],
-        compiler_params=pltpu.CompilerParams(collective_id=ident, has_side_effects=True),
-        name="share_rows",
-    )(h)
-
-
-def share_weights_kernel(n, *refs):
-    owns, outs, helds, (send, recv, local) = refs[:n], refs[n : 2 * n], refs[2 * n : 3 * n], refs[3 * n :]
-    z, p, core, one, two, _ = places()
-    x, y = (z, one, core), (z, two, core)
-    half = owns[0].shape[0] // 2
-    low, high = pl.ds(0, half), pl.ds(half, half)
-    loads = [pltpu.make_async_copy(owns[i], helds[i], local.at[0, i]) for i in range(n)]
-    stores = [pltpu.make_async_copy(helds[i], outs[i].at[:, p], local.at[1, i]) for i in range(n)]
-    for load in loads:
-        load.start()
-    meet([x, y])
-    copies = {}
-
-    def go(i, c, src, dst, partner):
-        copies[i, c] = to(src, dst, send.at[i, c], recv.at[i, c], partner)
-        copies[i, c].start()
-
-    for i in range(n):
-        own, out = owns[i], outs[i]
-        go(i, 0, own.at[low], out.at[low, p], x)
-        go(i, 1, own.at[high], out.at[high, p], y)
-        go(i, 2, own.at[high], out.at[high, p], x)
-        go(i, 3, own.at[low], out.at[low, p], y)
-    for i in range(n):
-        loads[i].wait()
-        stores[i].start()
-    for i in range(n):
-        copies[i, 0].wait_recv()
-        go(i, 4, outs[i].at[low, one], outs[i].at[low, one], y)
-        copies[i, 1].wait_recv()
-        go(i, 5, outs[i].at[high, two], outs[i].at[high, two], x)
-    for (_, c), copy in copies.items():
-        if c > 1:
-            copy.wait_recv()
-    for copy in copies.values():
-        copy.wait_send()
-    for store in stores:
-        store.wait()
-
-
-def share_weights(lines, ident):
-    depth = lax.axis_size("line")
-    n = len(lines)
-    each = lines[0].shape[0] // depth
-    outs = pl.pallas_call(
-        functools.partial(share_weights_kernel, n),
-        out_shape=[
-            jax.ShapeDtypeStruct((depth, GROUP, each, v.shape[1]), v.dtype) for v in lines
-        ],
-        in_specs=[ANY] * n,
-        out_specs=[ANY] * n,
-        scratch_shapes=[pltpu.VMEM((depth, each, v.shape[1]), v.dtype) for v in lines]
-        + [
-            pltpu.SemaphoreType.DMA((n, 6)),
-            pltpu.SemaphoreType.DMA((n, 6)),
-            pltpu.SemaphoreType.DMA((2, n)),
+            pltpu.VMEM((depth, each, cols), line.dtype),
+            pltpu.SemaphoreType.DMA((6,)),
+            pltpu.SemaphoreType.DMA((6,)),
+            pltpu.SemaphoreType.DMA((2,)),
         ],
         compiler_params=pltpu.CompilerParams(collective_id=ident, has_side_effects=True),
         name="share_weights",
-    )(*[v.reshape(depth, each, v.shape[1]) for v in lines])
-    return [v.reshape(depth * GROUP * each, v.shape[3]) for v in outs]
+    )(line.reshape(depth, each, line.shape[1]))
+    return out.reshape(depth * GROUP * each, cols)
 
 
 TILE = 256
@@ -409,7 +324,7 @@
 WIDTH = 512
 
 
-def deal_kernel(sent, pieces, gains, tokens, cots, units, all_gains, held, send, recv, ends, local):
+def deal_kernel(sent, pieces, gains, tokens, cots, units_0, units_1, all_gains, held, send, recv, ends, local):
     z, p, core, one, two, three = places()
     count, per, both = sent.shape
     wide = both // 2
@@ -440,44 +355,47 @@
         copy.start()
     pl.semaphore_wait(barrier, count)
 
-    def rows(s):
+    def row(i, s):
         t, who = partner(s)
-        return (
-            to(sent.at[t, :, pl.ds(0, wide)], tokens.at[me, :, cols], send.at[0, s], recv.at[0, s], who),
-            to(sent.at[t, :, pl.ds(wide, wide)], cots.at[me], send.at[1, s], recv.at[1, s], who),
-            to(gains, all_gains.at[me], send.at[2, s], recv.at[2, s], who),
-        )
+        src = (sent.at[t, :, pl.ds(0, wide)], sent.at[t, :, pl.ds(wide, wide)], gains)[i]
+        dst = (tokens.at[me, :, cols], cots.at[me], all_gains.at[me])[i]
+        return to(src, dst, send.at[i, s], recv.at[i, s], who)
 
     def start(i):
         def step(s, carry):
-            rows(s)[i].start()
+            row(i, s).start()
             return carry
 
         lax.fori_loop(1, count, step, 0)
 
     start(0)
     start(2)
+    units = (units_0.at[0], units_0.at[1], units_1)
     shares = [
-        to(pieces.at[q], units.at[:, p], ends.at[0, k], ends.at[1, k], (z, q, core))
-        for k, q in ((1, one), (2, two), (3, three))
+        to(pieces.at[q, i], units[i].at[p], ends.at[0, k, i], ends.at[1, k, i], (z, q, core))
+        for i in range(3)
+        for k, q in ((3, three), (1, one), (2, two))
     ]
     for copy in shares:
         copy.start()
     start(1)
     mine.wait()
-    store = pltpu.make_async_copy(held, units.at[:, p], local.at[4])
-    store.start()
+    stores = [
+        pltpu.make_async_copy(held.at[i], units[i].at[p], local.at[4 + i]) for i in range(3)
+    ]
+    for store in stores:
+        store.start()
     keep[0].wait()
 
     def arrived(i):
         def step(s, carry):
-            rows(s)[i].wait_recv()
+            row(i, s).wait_recv()
             return carry
 
         lax.fori_loop(1, count, step, 0)
 
     arrived(0)
-    pass_on = to(tokens.at[:, :, cols], tokens.at[:, :, cols], ends.at[0, 0], ends.at[1, 0], twin)
+    pass_on = to(tokens.at[:, :, cols], tokens.at[:, :, cols], ends.at[0, 0, 0], ends.at[1, 0, 0], twin)
     pass_on.start()
     arrived(2)
     for copy in shares:
@@ -486,16 +404,15 @@
     pass_on.wait_recv()
 
     def leave(s, carry):
-        for copy in rows(s):
-            copy.wait_send()
+        for i in range(3):
+            row(i, s).wait_send()
         return carry
 
     lax.fori_loop(1, count, leave, 0)
     for copy in [*shares, pass_on]:
         copy.wait_send()
-    keep[1].wait()
-    keep[2].wait()
-    store.wait()
+    for copy in [*keep[1:], *stores]:
+        copy.wait()
 
 
 def deal(sent, pieces, gains, ident):
@@ -506,17 +423,18 @@
         out_shape=[
             jax.ShapeDtypeStruct((count, per, both), BF),
             jax.ShapeDtypeStruct((count, per, both // 2), BF),
-            jax.ShapeDtypeStruct((three, GROUP, rows, units), BF),
+            jax.ShapeDtypeStruct((2, GROUP, rows, units), BF),
+            jax.ShapeDtypeStruct((GROUP, rows, units), BF),
             jax.ShapeDtypeStruct((count, *gains.shape), F32),
         ],
         in_specs=[WHOLE, ANY, WHOLE],
-        out_specs=[ANY] * 4,
+        out_specs=[ANY] * 5,
         scratch_shapes=[
             pltpu.VMEM((three, rows, units), BF),
             pltpu.SemaphoreType.DMA((3, count)),
             pltpu.SemaphoreType.DMA((3, count)),
-            pltpu.SemaphoreType.DMA((2, 4)),
-            pltpu.SemaphoreType.DMA((5,)),
+            pltpu.SemaphoreType.DMA((2, 4, 3)),
+            pltpu.SemaphoreType.DMA((7,)),
         ],
         compiler_params=pltpu.CompilerParams(collective_id=ident, has_side_effects=True),
         name="deal",
@@ -527,12 +445,12 @@
 
 
 def attend_back_kernel(
-    dh2_half, middle, cot, w_out, w_qkv, mixed, q_rot, k_rot, value, prob, tokens, half_result,
+    dh2_half, middle, cot, w_out, w_qkv, mixed, q_rot, k_rot, value, prob, tokens, half_result, sum_0, sum_d,
     scale1, scale2, gain_a, gain_f, cosine, sine, into,
-    new_qkv, new_out, new_gain, back,
+    new_qkv, new_out, new_gain, back, ffn, down,
     dh2, mid, low_mid, xs, hidden, w_part, g, mix, d_mix, qs, ks, vs, pb, gq, got_part,
     from_x, from_y, diag_x, diag_y, own, line, slots, half_rows, gain_terms, gain_got,
-    send, recv, loads, row_send, row_recv, ends, keeps,
+    send, recv, loads, row_send, row_recv, ends, keeps, unit_send, unit_recv,
 ):
     z, p, core, one, two, three = places()
     chunks, depth, _, each, _ = g.shape
@@ -540,7 +458,7 @@
     wide = width // 2
     query_cols, key_cols = qs.shape[1], ks.shape[1]
     outs = query_cols // WIDTH
-    count, per, _ = slots.shape[1:]
+    count, per, _ = slots.shape
     me = z * GROUP + p
     half = depth // 2
     low, high = pl.ds(0, half), pl.ds(half, half)
@@ -557,7 +475,7 @@
     load("half", 0, half_result, half_rows)
     load("dh2", 1, dh2_half, dh2.at[:, columns])
     load("mid", 2, middle, mid)
-    load("cot", 3, cot, low_mid)
+    load("cot", 3, cot.at[pl.ds(0, rows)], low_mid)
     load("x", 4, tokens, xs)
     load("mix", 5, mixed, mix)
     for i in range(outs):
@@ -598,7 +516,7 @@
     def row(i, s):
         t, who = partner(s)
         if i < 2:
-            return to(slots.at[i, t], back.at[i, me, :, columns], row_send.at[i, s], row_recv.at[i, s], who)
+            return to(slots.at[t], back.at[i, me, :, columns], row_send.at[i, s], row_recv.at[i, s], who)
         return to(gain_terms.at[t], gain_got.at[me], row_send.at[2, s], row_recv.at[2, s], who)
 
     def each_row(kinds, act):
@@ -612,8 +530,8 @@
     kept = []
 
     def give_rows(i):
-        slots[i] = mat_tn(into[...], half_rows[...]).reshape(count, per, wide).astype(BF)
-        kept.append(pltpu.make_async_copy(slots.at[i, me], back.at[i, me, :, columns], keeps.at[i]))
+        slots[...] = mat_tn(into[...], half_rows[...]).reshape(count, per, wide).astype(BF)
+        kept.append(pltpu.make_async_copy(slots.at[me], back.at[i, me, :, columns], keeps.at[i]))
         kept[-1].start()
         each_row((i,), lambda copy: copy.start())
 
@@ -651,11 +569,43 @@
             g[c, j] = part.reshape(GROUP, each, WIDTH).astype(BF)
         first(c)
 
+    units = sum_d.shape[1]
+    span = units // 2
+
+    def unit_parts(q, of):
+        at = pl.multiple_of(of * units, units)
+        rows_0 = unit_rows(sum_0, q, each)
+        return [
+            (unit_rows(sum_d, q, each), down.at[:, pl.ds(at, units)]),
+            (rows_0.at[:, pl.ds(0, span)], ffn.at[0, :, pl.ds(at, span)]),
+            (rows_0.at[:, pl.ds(span, span)], ffn.at[1, :, pl.ds(at, span)]),
+        ]
+
+    shared = []
+
+    def collect():
+        for i in range(3):
+            for k, q in ((3, three), (1, one), (2, two)):
+                src, dst = unit_parts(q, p)[i]
+                copy = to(src, dst, unit_send.at[k, i], unit_recv.at[k, i], (z, q, core))
+                copy.start()
+                shared.append(copy)
+
+    stay = []
+    for i, (src, dst) in enumerate(unit_parts(p, p)):
+        held = gq.at[pl.ds(0, each), pl.ds(i * span + (span if i else 0), units if i == 0 else span)]
+        copy = pltpu.make_async_copy(src, held, keeps.at[3 + i])
+        copy.start()
+        stay.append((copy, pltpu.make_async_copy(held, dst, keeps.at[6 + i])))
     pending["dh2"].wait()
     swap = to(dh2.at[:, columns], dh2.at[:, columns], ends.at[0, 0], ends.at[1, 0], twin)
     swap.start()
     pending["half"].wait()
     give_rows(0)
+    collect()
+    for first_copy, second_copy in stay:
+        first_copy.wait()
+        second_copy.start()
     for name in ("mid", "cot", "x"):
         pending[name].wait()
     swap.wait_recv()
@@ -691,6 +641,8 @@
 
     for name in ("q", "k", "v"):
         pending[name].wait()
+    for _, copy in stay:
+        copy.wait()
     heads, kv_heads = query_cols // HEAD_SIZE, key_cols // HEAD_SIZE
     each_kv = heads // kv_heads
     for h in range(kv_heads):
@@ -735,6 +687,7 @@
         along(c)
     relay(outs)
     each_row((0,), lambda copy: copy.wait_send())
+    kept[0].wait()
     pass_part.wait_recv()
 
     def norm_1(i, total):
@@ -760,7 +713,7 @@
     for c in range(outs + 1, chunks):
         relay(c)
         along(c - 1)
-    for copy in kept:
+    for copy in kept[1:]:
         copy.wait()
     each_row((0, 1, 2), lambda copy: copy.wait_recv())
     pass_on = to(
@@ -782,7 +735,9 @@
         else:
             new_qkv[:, (c - outs) * WIDTH : (c - outs + 1) * WIDTH] = total
     pass_on.wait_recv()
-    for copy in copies.values():
+    for copy in shared:
+        copy.wait_recv()
+    for copy in [*copies.values(), *shared]:
         copy.wait_send()
     each_row((1, 2), lambda copy: copy.wait_send())
     pass_part.wait_send()
@@ -790,7 +745,7 @@
 
 
 def attend_back(
-    dh2_half, middle, cot, w_out, w_qkv, mixed, q_rot, k_rot, value, prob, tokens, half_result,
+    dh2_half, middle, cot, w_out, w_qkv, mixed, q_rot, k_rot, value, prob, tokens, half_result, sum_0, sum_d,
     scale1, scale2, gain_a, gain_f, cosine, sine, into, ident,
 ):
     depth = lax.axis_size("line")
@@ -802,6 +757,7 @@
     cols = query_cols + 2 * key_cols
     chunks = (query_cols + cols) // WIDTH
     block = min(512, width)
+    units = sum_d.shape[1]
 
     def vmem(*shape, dtype=BF):
         return pltpu.VMEM(shape, dtype)
@@ -813,9 +769,11 @@
             jax.ShapeDtypeStruct((each, query_cols), F32),
             jax.ShapeDtypeStruct((8, each), F32),
             jax.ShapeDtypeStruct((2, count, rows // count, width), BF),
+            jax.ShapeDtypeStruct((2, each, GROUP * units), BF),
+            jax.ShapeDtypeStruct((each, GROUP * units), BF),
         ],
-        in_specs=[ANY] * 12 + [WHOLE] * 7,
-        out_specs=[WHOLE] * 3 + [ANY],
+        in_specs=[ANY] * 14 + [WHOLE] * 7,
+        out_specs=[WHOLE] * 3 + [ANY] * 3,
         scratch_shapes=[
             vmem(rows, width, dtype=F32),
             vmem(rows, width, dtype=F32),
@@ -838,7 +796,7 @@
             vmem(chunks, depth // 2, each, WIDTH),
             vmem(chunks, each, WIDTH, dtype=F32),
             vmem(chunks, depth - 1, each, WIDTH),
-            vmem(2, count, rows // count, wide),
+            vmem(count, rows // count, wide),
             vmem(rows, wide),
             vmem(count, 8, each, dtype=F32),
             vmem(count, 8, each, dtype=F32),
@@ -848,26 +806,32 @@
             pltpu.SemaphoreType.DMA((3, count)),
             pltpu.SemaphoreType.DMA((3, count)),
             pltpu.SemaphoreType.DMA((2, 3)),
-            pltpu.SemaphoreType.DMA((3,)),
+            pltpu.SemaphoreType.DMA((9,)),
+            pltpu.SemaphoreType.DMA((4, 3)),
+            pltpu.SemaphoreType.DMA((4, 3)),
         ],
         compiler_params=pltpu.CompilerParams(
             collective_id=ident, has_side_effects=True, vmem_limit_bytes=62 << 20
         ),
         name="attend_back",
     )(
-        dh2_half, middle, cot, w_out.reshape(depth, GROUP, each, query_cols), w_qkv, mixed, q_rot, k_rot, value,
-        prob, tokens, half_result, scale1, scale2, gain_a, gain_f, cosine, sine, into,
+        dh2_half, middle, cot, w_out, w_qkv, mixed, q_rot, k_rot, value,
+        prob, tokens, half_result, sum_0, sum_d, scale1, scale2, gain_a, gain_f, cosine, sine, into,
     )
 
 
+def unit_rows(ref, q, each):
+    return ref.at[pl.ds(pl.multiple_of(q * each, each), each)]
+
+
 def settle_kernel(
-    sum_0, sum_1, sum_d, grad_qkv, grad_out, grad_gain, norm, new_ffn, new_down, new_out,
-    ffn, shares, store, unit_send, unit_recv, unit_local, all_send, all_recv,
+    sum_1, ffn, down, grad_qkv, grad_out, grad_gain, norm, new_ffn, new_down, new_out,
+    rest, held, shares, local, unit_send, unit_recv, all_send, all_recv,
 ):
     z, p, core, one, two, three = places()
     count = shares.shape[0] // 2
     me = z * GROUP + p
-    each, units = ffn.shape[1], sum_d.shape[1]
+    each, units = rest.shape[2], sum_1.shape[1]
     span = units // 2
 
     def anyone(s):
@@ -883,28 +847,21 @@
     lax.fori_loop(1, 2 * count, greet, 0)
 
     def unit_parts(q, of):
-        rows = pl.ds(pl.multiple_of(q * each, each), each)
-
-        def place(i, shift, size):
-            return ffn.at[i, :, pl.ds(pl.multiple_of(of * units + shift, span), size)]
-
-        return [
-            (sum_d.at[rows], place(2, 0, units)),
-            (sum_0.at[rows, pl.ds(0, span)], place(0, 0, span)),
-            (sum_0.at[rows, pl.ds(span, span)], place(1, 0, span)),
-            (sum_1.at[rows, pl.ds(0, span)], place(0, span, span)),
-            (sum_1.at[rows, pl.ds(span, span)], place(1, span, span)),
-        ]
+        rows = unit_rows(sum_1, q, each)
+        return [(rows.at[:, pl.ds(i * span, span)], rest.at[i, of]) for i in range(2)]
 
     stay = [
-        pltpu.make_async_copy(src, dst, unit_local.at[i])
+        pltpu.make_async_copy(src, dst, local.at[i])
         for i, (src, dst) in enumerate(unit_parts(p, p))
+    ] + [
+        pltpu.make_async_copy(ffn, held.at[pl.ds(0, 2)], local.at[2]),
+        pltpu.make_async_copy(down, held.at[2], local.at[3]),
     ]
     for copy in stay:
         copy.start()
     pl.semaphore_wait(barrier, 2 * count - 1)
     shared = []
-    for i in range(5):
+    for i in range(2):
         for k, q in ((3, three), (1, one), (2, two)):
             src, dst = unit_parts(q, p)[i]
             copy = to(src, dst, unit_send.at[k, i], unit_recv.at[k, i], (z, q, core))
@@ -924,19 +881,20 @@
         new_out[at : at + 128, :] = value.T
     for copy in stay:
         copy.wait()
-    for copy in shared[:3]:
-        copy.wait_recv()
     for at in range(0, new_down.shape[0], 128):
-        value = ffn[2, :, at : at + 128].astype(F32)
+        value = held[2, :, at : at + 128].astype(F32)
         total = total + squares(value)
         new_down[at : at + 128, :] = value.T
-    for copy in shared[3:]:
+    for i in range(2):
+        for q in range(GROUP):
+            total = total + squares(held[i, :, q * units : q * units + span].astype(F32))
+    for copy in shared:
         copy.wait_recv()
-    keep = pltpu.make_async_copy(ffn.at[pl.ds(0, 2)], new_ffn, store)
-    keep.start()
     for i in range(2):
-        for at in range(0, GROUP * units, WIDTH):
-            total = total + squares(ffn[i, :, at : at + WIDTH].astype(F32))
+        for q in range(GROUP):
+            value = rest[i, q]
+            total = total + squares(value.astype(F32))
+            held[i, :, q * units + span : (q + 1) * units] = value
     shares[0] = jnp.broadcast_to(total, (8, 128))
 
     def tell(s):
@@ -955,6 +913,8 @@
         return carry
 
     lax.fori_loop(1, 2 * count, tell_start, 0)
+    keep = pltpu.make_async_copy(held.at[pl.ds(0, 2)], new_ffn, local.at[4])
+    keep.start()
     lax.fori_loop(1, 2 * count, tell_end, 0)
     norm[...] = jnp.sqrt(jnp.sum(shares[...], axis=0))
     lax.fori_loop(1, 2 * count, tell_left, 0)
@@ -963,9 +923,9 @@
     keep.wait()
 
 
-def settle(sum_0, sum_1, sum_d, grad_qkv, grad_out, grad_gain, ident):
+def settle(sum_1, ffn, down, grad_qkv, grad_out, grad_gain, ident):
     count = lax.axis_size("line") * GROUP
-    each, units = grad_qkv.shape[0], sum_d.shape[1]
+    each, units = grad_qkv.shape[0], sum_1.shape[1]
     return pl.pallas_call(
         settle_kernel,
         out_shape=[
@@ -977,12 +937,12 @@
         in_specs=[ANY] * 3 + [WHOLE] * 3,
         out_specs=[WHOLE, ANY, WHOLE, WHOLE],
         scratch_shapes=[
+            pltpu.VMEM((2, GROUP, each, units // 2), BF),
             pltpu.VMEM((3, each, GROUP * units), BF),
             pltpu.VMEM((2 * count, 8, 128), F32),
-            pltpu.SemaphoreType.DMA,
-            pltpu.SemaphoreType.DMA((4, 5)),
-            pltpu.SemaphoreType.DMA((4, 5)),
             pltpu.SemaphoreType.DMA((5,)),
+            pltpu.SemaphoreType.DMA((4, 2)),
+            pltpu.SemaphoreType.DMA((4, 2)),
             pltpu.SemaphoreType.DMA((2 * count,)),
             pltpu.SemaphoreType.DMA((2 * count,)),
         ],
@@ -990,13 +950,14 @@
             collective_id=ident, has_side_effects=True, vmem_limit_bytes=24 << 20
         ),
         name="settle",
-    )(sum_0, sum_1, sum_d, grad_qkv, grad_out, grad_gain)
-
-
-def update_kernel(limit, norm, gain, qkv, ffn, down, out, *refs):
-    weights, moments, new_moments, new_weights = refs[:9], refs[9:18], refs[18:27], refs[27:36]
-    w_buf, m_buf = refs[36:45], refs[45:54]
-    qkv_buf, ffn_buf, down_buf, out_buf, loads, stores, grads = refs[54:]
+    )(sum_1, ffn, down, grad_qkv, grad_out, grad_gain)
+
+
+def update_kernel(limit, norm, gain, moves, qkv, ffn, down, out, back, *refs):
+    weights, moments, placed = refs[:9], refs[9:18], refs[18:20]
+    new_moments, new_weights = refs[20:29], refs[29:38]
+    w_buf, m_buf = refs[38:47], refs[47:56]
+    qkv_buf, ffn_buf, down_buf, out_buf, rows_buf, loads, stores, grads = refs[56:]
     sources = {
         6: pltpu.make_async_copy(ffn, ffn_buf, grads.at[0]),
         8: pltpu.make_async_copy(down, down_buf, grads.at[1]),
@@ -1005,6 +966,11 @@
     }
     order = (0, 5, 2, 3, 1, 4, 8, 6, 7)
     pending = {}
+    returned = [
+        pltpu.make_async_copy(back.at[i], rows_buf.at[i], grads.at[4 + i]) for i in range(2)
+    ]
+    for copy in returned:
+        copy.start()
     for i in order:
         if i in sources and i != 1:
             sources[i].start()
@@ -1027,6 +993,12 @@
         m_buf[i][at] = m
         w_buf[i][at] = w - LEARN * (m + DECAY * w)
 
+    placing = []
+    for i in range(2):
+        returned[i].wait()
+        rows_buf[i] = mat_tn(moves[...], rows_buf[i]).astype(BF)
+        placing.append(pltpu.make_async_copy(rows_buf.at[i], placed[i], grads.at[6 + i]))
+        placing[i].start()
     for i in order:
         if i in sources and i != 1:
             sources[i].wait()
@@ -1052,29 +1024,312 @@
         for buf, new, j in ((m_buf, new_moments, 0), (w_buf, new_weights, 1)):
             writes.append(pltpu.make_async_copy(buf[i], new[i], stores.at[j, i]))
             writes[-1].start()
-    for copy in writes:
+    for copy in [*placing, *writes]:
         copy.wait()
 
 
-def update(norm, gain, qkv, ffn, down, out, weights, moments, limit):
+def update(norm, gain, moves, qkv, ffn, down, out, back, weights, moments, limit):
     like = [jax.ShapeDtypeStruct(v.shape, F32) for v in weights]
     size = sum(v.size for v in weights)
     return pl.pallas_call(
         functools.partial(update_kernel, limit),
-        out_shape=[*like, *like],
-        in_specs=[WHOLE] * 2 + [ANY] * 22,
-        out_specs=[ANY] * 18,
+        out_shape=[*[jax.ShapeDtypeStruct(back.shape[1:], BF)] * 2, *like, *like],
+        in_specs=[WHOLE] * 3 + [ANY] * 23,
+        out_specs=[ANY] * 20,
         scratch_shapes=[pltpu.VMEM(v.shape, F32) for v in (*weights, *moments)]
-        + [pltpu.VMEM(v.shape, v.dtype) for v in (qkv, ffn, down, out)]
+        + [pltpu.VMEM(v.shape, v.dtype) for v in (qkv, ffn, down, out, back)]
         + [
             pltpu.SemaphoreType.DMA((2, 9)),
             pltpu.SemaphoreType.DMA((2, 9)),
-            pltpu.SemaphoreType.DMA((4,)),
+            pltpu.SemaphoreType.DMA((8,)),
         ],
-        compiler_params=pltpu.CompilerParams(vmem_limit_bytes=40 << 20),
+        compiler_params=pltpu.CompilerParams(vmem_limit_bytes=44 << 20),
         cost_estimate=pl.CostEstimate(flops=7 * size, bytes_accessed=20 * size, transcendentals=0),
         name="update",
-    )(norm, gain, qkv, ffn, down, out, *weights, *moments)
+    )(norm, gain, moves, qkv, ffn, down, out, back, *weights, *moments)
+
+
+class Sharing:
+    def __init__(self, out, rows, send, recv):
+        self.z, self.p, self.core, self.one, self.two, _ = places()
+        self.out, self.rows, self.half = out, rows, rows // 2
+        wide = out.shape[1] // 2
+        self.cols = pl.ds(pl.multiple_of(self.core * wide, wide), wide)
+        self.send, self.recv, self.copies = send, recv, {}
+        self.x, self.y = (self.z, self.one, self.core), (self.z, self.two, self.core)
+        self.twin = (self.z, self.p, 1 - self.core)
+
+    def part(self, k, b):
+        return self.out.at[pl.ds(k * self.rows + b * self.half, self.half), self.cols]
+
+    def go(self, name, i, src, dst, partner):
+        self.copies[name] = to(src, dst, self.send.at[i], self.recv.at[i], partner)
+        self.copies[name].start()
+
+    def start(self, source):
+        self.go("1a", 0, source(0), self.part(1, 0), self.x)
+        self.go("2b", 3, source(1), self.part(2, 1), self.y)
+        self.go("1b", 1, source(1), self.part(1, 1), self.x)
+        self.go("2a", 2, source(0), self.part(2, 0), self.y)
+
+    def own(self, source):
+        for b in range(2):
+            self.go("o%d" % b, 12 + b, source(b), self.part(0, b), self.twin)
+
+    def pass_on(self, name, i, k, b):
+        self.copies[name].wait_recv()
+        self.go("t" + name, i, self.part(k, b), self.part(k, b), self.twin)
+
+    def relay(self):
+        self.copies["1a"].wait_recv()
+        self.go("3a", 4, self.part(1, 0), self.part(3, 0), self.y)
+        self.go("t1a", 6, self.part(1, 0), self.part(1, 0), self.twin)
+        self.copies["2b"].wait_recv()
+        self.go("3b", 5, self.part(2, 1), self.part(3, 1), self.x)
+        self.go("t2b", 9, self.part(2, 1), self.part(2, 1), self.twin)
+
+    def end(self):
+        self.pass_on("1b", 7, 1, 1)
+        self.pass_on("2a", 8, 2, 0)
+        self.pass_on("3a", 10, 3, 0)
+        self.pass_on("3b", 11, 3, 1)
+        for name, copy in self.copies.items():
+            if name[0] in "to":
+                copy.wait_recv()
+        for copy in self.copies.values():
+            copy.wait_send()
+
+
+def attend_kernel(
+    line, w_qkv, tokens, cot, gain_a, gain_f, cosine, sine, segment, segment_row,
+    w_out, group_h2, group_cot, middle, q_rot, k_rot, value, mixed, prob, scale1, scale2,
+    xs, hidden, w_part, held, wo, mid, packed, got, pb, qs, ks, vs, mix,
+    sends, recvs, out_send, out_recv, ends, loads, stores,
+):
+    z, p, core, one, two, _ = places()
+    rows, width = xs.shape
+    wide = width // 2
+    depth, each, _ = line.shape
+    query_cols, key_cols = qs.shape[1], ks.shape[1]
+    half = depth // 2
+    low, high = pl.ds(0, half), pl.ds(half, half)
+    x, y, twin = (z, one, core), (z, two, core), (z, p, 1 - core)
+    root = HEAD_SIZE ** (-0.5)
+    pending = {}
+    out_cols = pl.ds(query_cols + 2 * key_cols, query_cols)
+
+    def load(name, i, src, dst):
+        pending[name] = pltpu.make_async_copy(src, dst, loads.at[i])
+        pending[name].start()
+
+    load("x", 0, tokens, xs)
+    order = [query_cols // WIDTH + i for i in range(2 * key_cols // WIDTH)]
+    order += list(range(query_cols // WIDTH))
+
+    def load_part(i):
+        load(("w", i), 1 + i % 2, w_qkv.at[:, pl.ds(order[i] * WIDTH, WIDTH)], w_part.at[i % 2])
+
+    load_part(0)
+    load_part(1)
+    load("held", 3, line.at[:, :, out_cols], held)
+    meet([x, y, twin])
+    outs = []
+
+    def go(src, dst, partner):
+        i = len(outs)
+        outs.append(to(src, dst, out_send.at[i], out_recv.at[i], partner))
+        outs[i].start()
+
+    go(line.at[low, :, out_cols], w_out.at[low, p], x)
+    go(line.at[high, :, out_cols], w_out.at[high, p], y)
+    go(line.at[high, :, out_cols], w_out.at[high, p], x)
+    go(line.at[low, :, out_cols], w_out.at[low, p], y)
+    cots = Sharing(group_cot, rows, sends.at[0], recvs.at[0])
+    shares = Sharing(group_h2, rows, sends.at[1], recvs.at[1])
+    halves = [pl.ds(0, rows // 2), pl.ds(rows // 2, rows // 2)]
+    cots.own(lambda b: cot.at[halves[b]])
+    kept = []
+
+    def keep(src, dst):
+        kept.append(pltpu.make_async_copy(src, dst, stores.at[len(kept)]))
+        kept[-1].start()
+
+    keep(cot, group_cot.at[pl.ds(0, rows), cots.cols])
+    pending["x"].wait()
+
+    def norm_1(i, carry):
+        strip = pl.ds(pl.multiple_of(i * STRIP, STRIP), STRIP)
+        v = xs[strip, :].astype(F32)
+        r = lax.rsqrt(jnp.sum(v * v, axis=1, keepdims=True) * (1.0 / width) + EPS)
+        scale1[strip, :] = r
+        hidden[strip, :] = (v * r * gain_a[...]).astype(BF)
+        return carry
+
+    lax.fori_loop(0, rows // STRIP, norm_1, 0)
+
+    def turned(v):
+        a, b = v[:, : HEAD_SIZE // 2], v[:, HEAD_SIZE // 2 :]
+        c, s = cosine[...], sine[...]
+        return jnp.concatenate([a * c - b * s, b * c + a * s], axis=1).astype(BF)
+
+    def project(i):
+        pending["w", i].wait()
+        v = mat_nn(hidden[...], w_part[i % 2])
+        at = order[i] * WIDTH
+        if at >= query_cols + key_cols:
+            at -= query_cols + key_cols
+            vs[:, at : at + WIDTH] = v.astype(BF)
+        else:
+            ref, at = (qs, at) if at < query_cols else (ks, at - query_cols)
+            for j in range(0, WIDTH, HEAD_SIZE):
+                ref[:, at + j : at + j + HEAD_SIZE] = turned(v[:, j : j + HEAD_SIZE])
+        if i + 2 < len(order):
+            load_part(i + 2)
+
+    for i in range(2 * key_cols // WIDTH):
+        project(i)
+    pending["held"].wait()
+    keep(held, w_out.at[:, p])
+    index = lax.broadcasted_iota(jnp.int32, (rows, rows), 0)
+    seen = (segment[...] == segment_row[...]) & (
+        lax.broadcasted_iota(jnp.int32, (rows, rows), 1) <= index
+    )
+    heads, kv_heads = query_cols // HEAD_SIZE, key_cols // HEAD_SIZE
+    puts = []
+
+    def attend_head(j):
+        h = j // (heads // kv_heads)
+        kv = slice(h * HEAD_SIZE, (h + 1) * HEAD_SIZE)
+        cols = slice(j * HEAD_SIZE, (j + 1) * HEAD_SIZE)
+        s = mat_nt(qs[:, cols], ks[:, kv]) * root
+        s = jnp.where(seen, s, -1e30)
+        e = jnp.exp(s - jnp.max(s, axis=1, keepdims=True))
+        pr = e / jnp.sum(e, axis=1, keepdims=True)
+        if j >= 2:
+            puts[j - 2].wait()
+        pb[j % 2] = pr
+        puts.append(pltpu.make_async_copy(pb.at[j % 2], prob.at[j], stores.at[8 + j]))
+        puts[j].start()
+        mix[:, cols] = mat_nn(pr.astype(BF), vs[:, kv]).astype(BF)
+
+    relayed = False
+    for i in range(2 * key_cols // WIDTH, len(order)):
+        project(i)
+        if not relayed:
+            relayed = True
+            outs[0].wait_recv()
+            go(w_out.at[low, one], w_out.at[low, one], y)
+            outs[1].wait_recv()
+            go(w_out.at[high, two], w_out.at[high, two], x)
+        for j in range(order[i] * WIDTH // HEAD_SIZE, (order[i] + 1) * WIDTH // HEAD_SIZE):
+            attend_head(j)
+    keep(ks, k_rot)
+    keep(vs, value)
+    keep(qs, q_rot)
+    keep(mix, mixed)
+    for i in range(2, 6):
+        outs[i].wait_recv()
+    cots.start(lambda b: cot.at[halves[b]])
+    kept[1].wait()
+    load("wo", 4, w_out, wo)
+    pending["wo"].wait()
+    span = GROUP * each
+    for j in range(depth):
+        v = mat_nt(mix[...], wo[j].reshape(span, query_cols))
+        mid[:, j * span : (j + 1) * span] = v
+        packed[:, j * span : (j + 1) * span] = v.astype(BF)
+    swap = to(packed, got, ends.at[0], ends.at[1], twin)
+    swap.start()
+    swap.wait_recv()
+    swap.wait_send()
+
+    def norm_2(i, carry):
+        strip = pl.ds(pl.multiple_of(i * STRIP, STRIP), STRIP)
+        v = xs[strip, :].astype(F32) + (mid[strip, :] + got[strip, :].astype(F32))
+        mid[strip, :] = v
+        r = lax.rsqrt(jnp.sum(v * v, axis=1, keepdims=True) * (1.0 / width) + EPS)
+        scale2[strip, :] = r
+        packed[strip, :] = (v * r * gain_f[...]).astype(BF)
+        return carry
+
+    lax.fori_loop(0, rows // STRIP, norm_2, 0)
+    shares.start(lambda b: packed.at[halves[b], shares.cols])
+    keep(packed, group_h2.at[pl.ds(0, rows)])
+    keep(mid, middle)
+    shares.relay()
+    cots.relay()
+    shares.end()
+    cots.end()
+    for copy in outs:
+        copy.wait_send()
+    for i, copy in enumerate(kept):
+        if i != 1:
+            copy.wait()
+    for copy in puts[-2:]:
+        copy.wait()
+
+
+def attend(line, w_qkv, tokens, cot, gain_a, gain_f, cosine, sine, segment, key_cols, ident):
+    depth = lax.axis_size("line")
+    rows, width = tokens.shape
+    each = line.shape[0] // depth
+    cols = w_qkv.shape[1]
+    query_cols = cols - 2 * key_cols
+    heads = query_cols // HEAD_SIZE
+
+    def vmem(*shape, dtype=BF):
+        return pltpu.VMEM(shape, dtype)
+
+    def like(*shape, dtype=BF):
+        return jax.ShapeDtypeStruct(shape, dtype)
+
+    return pl.pallas_call(
+        attend_kernel,
+        out_shape=[
+            like(depth, GROUP, each, query_cols),
+            like(GROUP * rows, width),
+            like(GROUP * rows, width),
+            like(rows, width, dtype=F32),
+            like(rows, query_cols),
+            like(rows, key_cols),
+            like(rows, key_cols),
+            like(rows, query_cols),
+            like(heads, rows, rows, dtype=F32),
+            like(rows, 1, dtype=F32),
+            like(rows, 1, dtype=F32),
+        ],
+        in_specs=[ANY] * 3 + [WHOLE] * 7,
+        out_specs=[ANY] * 9 + [WHOLE] * 2,
+        scratch_shapes=[
+            vmem(rows, width),
+            vmem(rows, width),
+            vmem(2, width, WIDTH),
+            vmem(depth, each, query_cols),
+            vmem(depth, GROUP, each, query_cols),
+            vmem(rows, width, dtype=F32),
+            vmem(rows, width),
+            vmem(rows, width),
+            vmem(2, rows, rows, dtype=F32),
+            vmem(rows, query_cols),
+            vmem(rows, key_cols),
+            vmem(rows, key_cols),
+            vmem(rows, query_cols),
+            pltpu.SemaphoreType.DMA((2, 14)),
+            pltpu.SemaphoreType.DMA((2, 14)),
+            pltpu.SemaphoreType.DMA((6,)),
+            pltpu.SemaphoreType.DMA((6,)),
+            pltpu.SemaphoreType.DMA((2,)),
+            pltpu.SemaphoreType.DMA((5,)),
+            pltpu.SemaphoreType.DMA((8 + heads,)),
+        ],
+        compiler_params=pltpu.CompilerParams(
+            collective_id=ident, has_side_effects=True, vmem_limit_bytes=56 << 20
+        ),
+        name="attend",
+    )(
+        line.reshape(depth, each, line.shape[1]), w_qkv, tokens, cot, gain_a, gain_f, cosine, sine,
+        segment[:, None], segment[None, :],
+    )
 
 
 class Ways:
@@ -1086,38 +1341,15 @@
         self.me = self.z * GROUP + self.p
         self.core = lax.axis_index("mp")
 
-    def flip(self, value, k):
-        return lax.ppermute(value, "group", [(i, i ^ k) for i in range(GROUP)])
-
-    def swap(self, value):
-        return lax.ppermute(value, "mp", [(0, 1), (1, 0)])
-
     def gather_line(self, value):
         return lax.all_gather(value, "line", axis=0, tiled=True)
 
     def scatter_line(self, whole):
         return lax.psum_scatter(whole, "line", scatter_dimension=0, tiled=True)
-
-    def gather_group(self, value):
-        half = value.shape[0] // 2
-        one, two = self.flip(value, 1), self.flip(value, 2)
-        three = jnp.concatenate([self.flip(one[:half], 2), self.flip(two[half:], 1)])
-        return [value, one, two, three]
 
     def own_half(self, value):
         half = value.shape[-1] // 2
         return jnp.where(self.core == 0, value[..., :half], value[..., half:])
-
-    def other_half(self, value):
-        half = value.shape[-1] // 2
-        return jnp.where(self.core == 0, value[..., half:], value[..., :half])
-
-    def join(self, mine, other):
-        return jnp.where(
-            self.core == 0,
-            jnp.concatenate([mine, other], axis=-1),
-            jnp.concatenate([other, mine], axis=-1),
-        )
 
 
 def unit_pieces(down, gate, upper):
@@ -1187,9 +1419,7 @@
         [w_query.astype(BF), key_weight.astype(BF), value_weight.astype(BF)], axis=1
     )
     shard_out = w_out.astype(BF).T
-    line_all = ways.gather_line(jnp.concatenate([shard_qkv, shard_out], axis=1))
-    line_qkv = line_all[:, : shard_qkv.shape[1]]
-    line_out = line_all[:, shard_qkv.shape[1] :]
+    line = ways.gather_line(jnp.concatenate([shard_qkv, shard_out], axis=1))
 
     into, out = deal_tables(token_order, me, rows)
     sent = mat_nn(
@@ -1199,7 +1429,7 @@
     gains = jnp.pad(
         jnp.stack([gain_attn, gain_ffn]).astype(BF).astype(F32), ((0, 6), (0, 0))
     )
-    got_tokens, got_cot, units, all_gains = deal(
+    got_tokens, got_cot, units_0, units_1, all_gains = deal(
         sent.reshape(ways.n, rows // ways.n, width), pieces, gains, 5
     )
     gain_a = all_gains[:, 0].reshape(width)
@@ -1207,60 +1437,35 @@
     dealt = mat_nn(into, got_tokens.reshape(rows, width)).astype(BF)
     half_cot = mat_nn(into, got_cot.reshape(rows, width // 2)).astype(BF)
 
-    weight_qkv, weight_out = share_weights([line_qkv, line_out], 4)
-    wide_q = w_query.shape[1]
     wide_k = key_weight.shape[1]
-    query_w = weight_qkv[:, :wide_q]
-    key_w = weight_qkv[:, wide_q : wide_q + wide_k]
-    value_w = weight_qkv[:, wide_q + wide_k :]
-
-    line_units = lax.all_gather(
-        units.reshape(3, -1, units.shape[-1]), "line", axis=1, tiled=False
-    )
-    down_t, first_w, second_w = (line_units[i].reshape(width, -1) for i in range(3))
-
-    cot_parts = jnp.concatenate(ways.gather_group(after(half_cot, weight_out)))
-    group_cot = ways.join(cot_parts, ways.swap(cot_parts))
-    dealt_cot = group_cot[:rows]
+    weight_qkv = share_weights(line, shard_qkv.shape[1], 4)
+
+    units = units_1.shape[-1]
+    first_units = lax.all_gather(
+        units_0.reshape(2, -1, units), "line", axis=1, tiled=False
+    ).reshape(2, width, units)
+    down_t, first_w = first_units[0], first_units[1]
+    second_w = ways.gather_line(units_1.reshape(-1, units))
 
     seq_dev = seq_deal.shape[0] // ways.n
     mine = lax.dynamic_slice_in_dim(seq_deal, me * seq_dev, seq_dev)
-    position, mask = layout(lengths[mine], rows)
+    position, segment = layout(lengths[mine], rows)
     cosine, sine = angles(position, HEAD_SIZE)
-
-    heads_q = query_w.shape[1] // HEAD_SIZE
-    heads_kv = key_w.shape[1] // HEAD_SIZE
-    head_group = heads_q // heads_kv
-    root = HEAD_SIZE ** (-0.5)
-    inputs = dealt.astype(F32)
-    normed1, scale1 = normalize(inputs)
-    hidden1 = (normed1 * gain_a).astype(BF)
-    query = mat_nn(hidden1, query_w).reshape(rows, heads_q, HEAD_SIZE)
-    key = mat_nn(hidden1, key_w).reshape(rows, heads_kv, HEAD_SIZE)
-    value = mat_nn(hidden1, value_w).astype(BF).reshape(rows, heads_kv, HEAD_SIZE)
-    query_rot = (
-        apply_rotary(query, cosine, sine)
-        .astype(BF)
-        .reshape(rows, heads_kv, head_group, HEAD_SIZE)
-    )
-    key_rot = apply_rotary(key, cosine, sine).astype(BF)
-    scores = jnp.einsum("rhgd,chd->hgrc", query_rot, key_rot, preferred_element_type=F32) * root
-    scores = jnp.where(mask[None, None], scores, -1e30)
-    top = jnp.max(scores, axis=-1, keepdims=True)
-    expo = jnp.exp(scores - top)
-    prob = expo / jnp.sum(expo, axis=-1, keepdims=True)
-    prob_low = prob.astype(BF)
-    mixed = (
-        jnp.einsum("hgrc,chd->rhgd", prob_low, value, preferred_element_type=F32)
-        .reshape(rows, heads_q * HEAD_SIZE)
-        .astype(BF)
-    )
-    part = mat_nt(mixed, weight_out)
-    middle = inputs + (part + ways.swap(part.astype(BF)).astype(F32))
-    normed2, scale2 = normalize(middle)
-    hidden2 = (normed2 * gain_f).astype(BF)
-
-    group_h2 = share_rows(hidden2, 1)
+    gain_a, gain_f = gain_a.reshape(1, width), gain_f.reshape(1, width)
+    (
+        weight_out,
+        group_h2,
+        group_cot,
+        middle,
+        query_rot,
+        key_rot,
+        value,
+        mixed,
+        prob,
+        scale1,
+        scale2,
+    ) = attend(line, weight_qkv, dealt, half_cot, gain_a, gain_f, cosine, sine, segment, wide_k, 8)
+
     grad_inner = mat_nn(group_cot, down_t)
     span = grad_inner.shape[1] // 2
 
@@ -1288,32 +1493,31 @@
     sum_1 = ways.scatter_line(terms_1)
     half_dh2 = after(half_dh2, terms_1)
     half_result = (ways.own_half(middle) + half_ffn).astype(BF)
-    dh2_first = half_dh2 + 0.0 * sum_0[0, 0].astype(F32)
-    new_qkv, new_out, new_gain, back = attend_back(
-        dh2_first,
+    new_qkv, new_out, new_gain, back, ffn, down = attend_back(
+        half_dh2,
         middle,
-        dealt_cot,
+        group_cot,
         weight_out,
         weight_qkv,
         mixed,
-        query_rot.reshape(rows, -1),
-        key_rot.reshape(rows, -1),
-        value.reshape(rows, -1),
-        prob.reshape(heads_q, rows, rows),
+        query_rot,
+        key_rot,
+        value,
+        prob,
         dealt,
         half_result,
+        sum_0,
+        sum_d,
         scale1,
         scale2,
-        gain_a.reshape(1, width),
-        gain_f.reshape(1, width),
-        cosine[:, 0],
-        sine[:, 0],
+        gain_a,
+        gain_f,
+        cosine,
+        sine,
         into,
         6,
     )
-    norm, new_ffn, new_down, new_out_t = settle(sum_0, sum_1, sum_d, new_qkv, new_out, new_gain, 7)
-    activations = mat_tn(out, back[0].reshape(rows, width)).astype(BF)
-    input_grad = mat_tn(out, back[1].reshape(rows, width)).astype(BF)
+    norm, new_ffn, new_down, new_out_t = settle(sum_1, ffn, down, new_qkv, new_out, new_gain, 7)
     weights = (gain_attn, w_query, key_weight, value_weight, w_out, gain_ffn, w_gate, w_up, w_down)
     moments = (
         moment_gain_attn,
@@ -1327,8 +1531,18 @@
         moment_w_down,
     )
     flat = [v if v.ndim == 2 else v.reshape(1, -1) for v in (*weights, *moments)]
-    new = update(
-        norm, new_gain, new_qkv, new_ffn, new_down, new_out_t, flat[:9], flat[9:], math.sqrt(PARAMS)
+    activations, input_grad, *new = update(
+        norm,
+        new_gain,
+        out,
+        new_qkv,
+        new_ffn,
+        new_down,
+        new_out_t,
+        back.reshape(2, rows, width),
+        flat[:9],
+        flat[9:],
+        math.sqrt(PARAMS),
     )
     new = [v.reshape(old.shape) for v, old in zip(new, (*weights, *weights))]
     return (activations, input_grad, norm[0, 0], *new)

time: 845 us -> 776 us (0.918)
  local copies, waits for them, and re-layouts: 84.9 us -> 34.3 us
  other arithmetic: 57.5 us -> 35.4 us
  matrix products: 99.1 us -> 83.6 us
  Pallas kernels: 562 us -> 576 us
  waiting for transfers between devices: 16.3 us -> 27.1 us
    pallas_call x3, Pallas kernels: 155 us -> 197 us  [the longest x1 111 us: attend(): pl.pallas_call(attend_kernel, out_shape=[like(depth, GROUP, each, query_c...]
    slice x11 -> x1, local copies, waits for them, and re-layouts: 30.4 us -> 4.51 us  [on_device(): down_t, first_w = (first_units[0], first_units[1])]
    pallas_call x1, Pallas kernels: 49.2 us -> 25.1 us  [settle(): pl.pallas_call(settle_kernel, out_shape=[jax.ShapeDtypeStruct((8, 128), F...]
    reduce_scatter x3, waiting for transfers between devices: 0.01 us -> 20.3 us  [scatter_line(): return lax.psum_scatter(whole, 'line', scatter_dimension=0, tiled=True)]
    unnamed x151 -> x90, local copies, waits for them, and re-layouts: 36.2 us -> 19.9 us
    select_n x2 -> x1, other arithmetic: 11.5 us -> 0.08 us  [on_device(): position, segment = layout(lengths[mine], rows)]
    dot_general x10 -> x7, matrix products: 52.5 us -> 44.8 us  [mat_nn(): return jnp.dot(left, right, preferred_element_type=F32)]
    dot_general x5 -> x3, matrix products: 42.8 us -> 38.9 us  [mat_tn(): lax.dot_general(left, right, (((0,), (0,)), ((), ())), preferred_element_...]
  transfers between devices with their start and end apart: 11 -> 6, of which waited for: 3 -> 2; matrix products, arithmetic and copies ran while one was open for 21% -> 17% of each run, Pallas kernels for 60% -> 70%
where the time goes in v5:
time: 776 us; the launch traced here: 772 us
  Pallas kernels  576 us (74%)
  matrix products  83.6 us (11%)
  other arithmetic  35.4 us (5%)
  local copies, waits for them, and re-layouts  34.3 us (4%)
  waiting for transfers between devices  27.1 us (3%)
  between operations  15.1 us (2%)
    pallas_call x1, Pallas kernels, attend_back(): pl.pallas_call(attend_back_kernel, out_shape=[jax.ShapeDtypeStruct((each,...  191 us
    pallas_call x1, Pallas kernels, attend(): pl.pallas_call(attend_kernel, out_shape=[like(depth, GROUP, each, query_c...  111 us
    pallas_call x1, Pallas kernels, sum_rows(): pl.pallas_call(functools.partial(sum_rows_kernel, sizes), out_shape=[jax....  84.6 us
    pallas_call x1, Pallas kernels, deal(): pl.pallas_call(deal_kernel, out_shape=[jax.ShapeDtypeStruct((count, per,...  78.5 us
    pallas_call x1, Pallas kernels, share_weights(): pl.pallas_call(share_weights_kernel, out_shape=jax.ShapeDtypeStruct((dept...  72.9 us
    dot_general x7, matrix products, mat_nn(): return jnp.dot(left, right, preferred_element_type=F32)  44.8 us
    dot_general x3, matrix products, mat_tn(): lax.dot_general(left, right, (((0,), (0,)), ((), ())), preferred_element_...  38.9 us
    pallas_call x1, Pallas kernels, settle(): pl.pallas_call(settle_kernel, out_shape=[jax.ShapeDtypeStruct((8, 128), F...  25.1 us
  transfers between devices with their start and end apart: 6, of which 2 were waited for; matrix products, arithmetic and copies ran while one was open for 17% of the time, Pallas kernels for 70%

profile of v5, /device:TPU:0, one launch (start us, length us, event | category | flops | bytes accessed | tf_op | source)
XLA Modules:
  0.0 771.7 jit_solution(3252219680227160379)
XLA Ops:
  7.3 1.2 copy.70
  8.5 1.1 copy.71
  9.6 1.2 copy.69
  10.8 1.1 convert_bitcast_fusion.1
  11.9 0.9 pad_maximum_fusion.4
  13.6 2.7 convert_element_type.83
  16.4 1.8 copy.73
  18.9 1.4 fusion.24
  21.1 1.1 copy-done.37
  23.2 2.6 convolution_convert_fusion.4
  25.9 1.9 pad_maximum_fusion.3.pieces
  27.8 78.5 %deal.1 = (bf16[16,32,2048]{2,1,0:T(8,128)(2,1)}, bf16[16,32,1024]{2,1,0:T(8,128)(2,1)}, bf16[2,4,128,1024]{3,2,1,0:T(8,128)(2,1)}, bf16[4,128,1024]{2,1,0:T(8,128)(2,1)}, f32[16,8,128]{2,1,0:T(8,128)}) custom-call(bf16[16,32,2048]{2,1,0:T(8,128)(2,1)} %bitcast.93, bf16[4,3,128,1024]{3,2,1,0:T(8,128)(2,1)} %pad_maximum_fusion.3.pieces, f32[8,128]{1,0:T(8,128)} %fusion.20.gains), custom_call_target="tpu_custom_call" | custom-call | tf_op jit(solution)/shard_map/deal/pallas_call | solution.py:421
  108.7 0.9 copy.74.segment
  109.5 4.3 convolution_convert_fusion.3.tokens
  113.9 1.7 convolution_convert_fusion.5.cot
  115.6 1.5 slice_bitcast_fusion.4
  117.1 1.8 multiply_sine_fusion
  118.9 6.0 all-gather.4.cloned.1.call-done
  124.9 4.7 copy.72
  129.7 72.9 %share_weights.1 = bf16[4,4,128,2048]{3,2,1,0:T(8,128)(2,1)} custom-call(bf16[4,128,3072]{2,1,0:T(8,128)(2,1)} %bitcast.84), custom_call_target="tpu_custom_call" | custom-call | tf_op jit(solution)/shard_map/share_weights/pallas_call | solution.py:121
  202.6 111.2 %attend.1 = (bf16[4,4,128,1024]{3,2,1,0:T(8,128)(2,1)}, bf16[2048,2048]{1,0:T(8,128)(2,1)}, bf16[2048,2048]{1,0:T(8,128)(2,1)}, f32[512,2048]{1,0:T(8,128)}, bf1...) custom-call(bf16[4,128,3072]{2,1,0:T(8,128)(2,1)} %bitcast.85, ...), custom_call_target="tpu_custom_call" | custom-call | tf_op jit(solution)/shard_map/attend/pallas_call | solution.py:1286
  313.8 4.5 fusion.23
  318.4 2.3 copy-done.35
  320.7 9.1 %fusion.26 = f32[2048,1024]{1,0:T(8,128)S(1)} fusion(bf16[2048,2048]{1,0:T(8,128)(2,1)S(1)} %copy-done.35, bf16[2048,1024]{1,0:T(8,128)(2,1)S(1)} %bitcast.88), kind=kOutput, calls=%fused_computation.103 | convolution fusion | flops 8589934592 | bytes 20971520 | tf_op jit(solution)/shard_map/dot_general | solution.py:42
  329.9 14.3 %fusion.27 = f32[2048,1024]{1,0:T(8,128)S(1)} fusion(bf16[2048,2048]{1,0:T(8,128)(2,1)} %get-tuple-element.83, bf16[2048,1024]{1,0:T(8,128)(2,1)S(1)} %bitcast.86), kind=kOutput, calls=%fused_computation.104 | convolution fusion | flops 8589934592 | bytes 20971520 | tf_op jit(solution)/shard_map/dot_general | solution.py:42
  344.2 3.1 multiply_convert_fusion.5
  347.3 1.3 copy-done.27
  349.3 13.0 %convolution_convert_fusion.2 = bf16[2048,1024]{1,0:T(8,128)(2,1)} fusion(bf16[2048,2048]{1,0:T(8,128)(2,1)} %get-tuple-element.83, bf16[2048,512]{1,0:T(8,128)(2,1)S(1)} %get-tuple-element.130, bf16[2048,512]{1,0:T(8,128)(2,1)S(1)} %get-tuple-element.129), kind=kOutput, calls=%fused_computation.16 | convolution fusion | flops 8600420352 | bytes 16777216 | tf_op jit(solution)/shard_map/dot_general | solution.py:50
  362.3 12.5 %fusion.28 = f32[2048,1024]{1,0:T(8,128)S(1)} fusion(bf16[2048,2048]{1,0:T(8,128)(2,1)} %get-tuple-element.83, bf16[2048,1024]{1,0:T(8,128)(2,1)} %all-gather.8.cloned.1.call-done.refs_3_), kind=kOutput, calls=%fused_computation.105 | convolution fusion | flops 8589934592 | bytes 20971520 | tf_op jit(solution)/shard_map/dot_general | solution.py:42
  374.8 5.4 multiply_convert_fusion.3
  380.2 1.3 copy-done.33
  381.5 12.9 %convolution_convert_fusion.1 = bf16[2048,1024]{1,0:T(8,128)(2,1)} fusion(bf16[2048,2048]{1,0:T(8,128)(2,1)} %get-tuple-element.77.cot, bf16[2048,512]{1,0:T(8,128)(2,1)S(1)} %get-tuple-element.132, bf16[2048,512]{1,0:T(8,128)(2,1)S(1)} %get-tuple-element.131), kind=kOutput, calls=%fused_computation.15 | convolution fusion | flops 8600420352 | bytes 16777216 | tf_op jit(solution)/shard_map/dot_general | solution.py:50
  394.5 4.9 pad_maximum_fusion.1.refs_2_
  399.4 2.7 pad_maximum_fusion.refs_0_
  402.2 2.7 pad_maximum_fusion.2.refs_4_
  404.8 84.6 %sum_rows.1 = (f32[512,1024]{1,0:T(8,128)}, f32[512,1024]{1,0:T(8,128)}) custom-call(bf16[2048,1024]{1,0:T(8,128)(2,1)} %pad_maximum_fusion.refs_0_, bf16[2048,1024]{1,0:T(8,128)(2,1)} %bitcast.87, bf16[2048,1024]{1,0:T(8,128)(2,1)} %pad_maximum_fusion.1.refs_2_, bf16[2048,1024]{1,0:T(8,128)(2,1)} %all-gather.8.cloned.1.call-done.refs_3_, ...), custom_call_target="tpu_custom_call" | custom-call | tf_op jit(solution)/shard_map/sum_rows/pallas_call | solution.py:297
  489.4 13.0 %convolution_convert_fusion = bf16[2048,1024]{1,0:T(8,128)(2,1)} fusion(bf16[2048,2048]{1,0:T(8,128)(2,1)} %get-tuple-element.83, bf16[2048,512]{1,0:T(8,128)(2,1)S(1)} %copy-done.32, bf16[2048,512]{1,0:T(8,128)(2,1)S(1)} %copy-done.31), kind=kOutput, calls=%fused_computation.14 | convolution fusion | flops 8600420352 | bytes 16777216 | tf_op jit(solution)/shard_map/dot_general | solution.py:50
  502.6 0.9 fusion.6.into
  503.6 4.4 add_convert_fusion.half_result
  508.0 20.2 %reduce-scatter.8.cloned.1.call-done.sum_d = bf16[512,1024]{1,0:T(8,128)(2,1)} async-done(((bf16[2048,1024]{1,0:T(8,128)(2,1)}), bf16[512,1024]{1,0:T(8,128)(2,1)}) %reduce-scatter.8.cloned.1.call-update) | async-done | bytes 1048592 | tf_op jit(solution)/shard_map/reduce_scatter | solution.py:1348
  528.2 190.7 %attend_back.1 = (f32[128,2048]{1,0:T(8,128)}, f32[128,1024]{1,0:T(8,128)}, f32[8,128]{1,0:T(8,128)}, bf16[2,16,32,2048]{3,2,1,0:T(8,128)(2,1)}, bf16[2,128,4096...) custom-call(f32[512,1024]{1,0:T(8,128)} %get-tuple-element.84.dh2_half, f32[512,2048]{1,0:T(8,128)} %get-tuple-element.85.middle, ...), custom_call_target="tpu_custom_call" | custom-call | tf_op jit(solution)/shard_map/attend_back/pallas_call | solution.py:765
  719.0 1.2 copy-done.2
  720.2 1.6 copy-done.6
  721.8 1.2 copy-done.9
  723.0 1.2 copy-done.10
  724.3 1.0 copy-done.13
  726.0 25.1 %settle.1 = (f32[8,128]{1,0:T(8,128)S(1)}, bf16[2,128,4096]{2,1,0:T(8,128)(2,1)S(1)}, f32[4096,128]{1,0:T(8,128)S(1)}, f32[1024,128]{1,0:T(8,128)S(1)}) custom-call(bf16[512,1024]{1,0:T(8,128)(2,1)S(1)} %copy-done.9, bf16[2,128,4096]{2,1,0:T(8,128)(2,1)S(1)} %copy-done.6, bf16[128,4096]{1,0:T(8,128)(2,1)S(1)} %copy-done.10, f32[128,2048]{1,0:T(8,128)S(1)} %copy-done.2, ...), custom_call_target="tpu_custom_call" | custom-call | tf_op jit(solution)/shard_map/settle/pallas_call | solution.py:929
  751.7 12.9 %update.1 = (bf16[512,2048]{1,0:T(8,128)(2,1)}, bf16[512,2048]{1,0:T(8,128)(2,1)}, f32[1,128]{1,0:T(1,128)}, f32[128,1024]{1,0:T(8,128)}, f32[128,512]{1,0:T(8,1...) custom-call(f32[8,128]{1,0:T(8,128)S(1)} %get-tuple-element.100.norm, ...), custom_call_target="tpu_custom_call" | custom-call | flops 13764352 | bytes 39326720 | tf_op jit(solution)/shard_map/update/pallas_call | solution.py:1034
  (126 shorter events, 8.0 us)
Async XLA Ops:
  7.2 100.6 %copy-start = (s32[64]{0:T(128)S(1)}, s32[64]{0:T(128)}, u32[]{:S(2)}) copy-start(s32[64]{0:T(128)} %param.25) | copy-start | bytes 772
  7.2 5.7 copy-start.39
  7.2 9.1 %copy-start.26 = (f32[128,4096]{1,0:T(8,128)S(1)}, f32[128,4096]{1,0:T(8,128)}, u32[]{:S(2)}) copy-start(f32[128,4096]{1,0:T(8,128)} %refs_7_.1) | copy-start | bytes 6291460
  7.2 117.7 %all-gather.4.cloned.1.call-start = ((), (), s32[]{:S(2)}) async-start(), calls=%async_computation.3 | async-start | bytes 3932160 | tf_op jit(solution)/shard_map/all_gather | solution.py:1345
  12.8 301.0 %all-gather.6.cloned.1.call-start = ((), (), s32[]{:S(2)}) async-start(), calls=%async_computation.4 | async-start | bytes 10485760 | tf_op jit(solution)/shard_map/all_gather | solution.py:1444
  13.6 4.6 copy-start.18
  13.6 4.6 copy-start.20
  20.6 1.6 copy-start.37
  20.6 2.4 copy-start.38
  27.8 79.9 %copy-start.42 = (s32[64]{0:T(128)S(1)}, s32[64]{0:T(128)}, u32[]{:S(2)}) copy-start(s32[64]{0:T(128)} %param.26) | copy-start | bytes 772
  106.3 256.0 %all-gather.8.cloned.1.call-start = ((), (), s32[]{:S(2)}) async-start(), calls=%async_computation.5 | async-start | bytes 5242880 | tf_op jit(solution)/shard_map/all_gather | solution.py:1345
  107.0 400.9 %reduce-scatter.6.cloned.1.call-start = ((), (), s32[]{:S(2)}) async-start(), calls=%async_computation.7 | async-start | bytes 5242880 | tf_op jit(solution)/shard_map/reduce_scatter | solution.py:1348
  108.6 5.2 copy-start.40
  109.5 4.3 copy-start.41
  313.8 6.9 copy-start.35
  318.4 11.5 %copy-start.25 = (bf16[1,4,512,1024]{3,2,1,0:T(8,128)(2,1)}, bf16[1,4,512,1024]{3,2,1,0:T(8,128)(2,1)S(1)}, u32[]{:S(2)}) copy-start(bf16[1,4,512,1024]{3,2,1,0:T(8,128)(2,1)S(1)} %get-tuple-element.134) | copy-start | bytes 12582916
  318.4 11.5 %copy-start.24 = (bf16[1,4,512,1024]{3,2,1,0:T(8,128)(2,1)}, bf16[1,4,512,1024]{3,2,1,0:T(8,128)(2,1)S(1)}, u32[]{:S(2)}) copy-start(bf16[1,4,512,1024]{3,2,1,0:T(8,128)(2,1)S(1)} %get-tuple-element.133) | copy-start | bytes 12582916
  329.8 14.3 %copy-start.36 = (f32[2048,1024]{1,0:T(8,128)}, f32[2048,1024]{1,0:T(8,128)S(1)}, u32[]{:S(2)}) copy-start(f32[2048,1024]{1,0:T(8,128)S(1)} %fusion.26) | copy-start | bytes 25165828
  347.3 1.3 copy-start.27
  347.3 2.0 copy-start.29
  362.3 165.9 %reduce-scatter.8.cloned.1.call-start = ((), (), s32[]{:S(2)}) async-start(), calls=%async_computation.8 | async-start | bytes 5242880 | tf_op jit(solution)/shard_map/reduce_scatter | solution.py:1348
  380.2 1.3 copy-start.33
  394.4 324.6 %reduce-scatter.4.cloned.1.call-start = ((), (), s32[]{:S(2)}) async-start(), calls=%async_computation.6 | async-start | bytes 5242880 | tf_op jit(solution)/shard_map/reduce_scatter | solution.py:1348
  394.5 4.9 copy-start.28
  394.5 4.9 copy-start.30
  399.4 2.7 copy-start.34
  404.8 84.6 %copy-start.31 = (bf16[2048,512]{1,0:T(8,128)(2,1)S(1)}, bf16[2048,512]{1,0:T(8,128)(2,1)}, u32[]{:S(2)}) copy-start(bf16[2048,512]{1,0:T(8,128)(2,1)} %get-tuple-element.127) | copy-start | bytes 6291460
  404.8 84.6 %copy-start.32 = (bf16[2048,512]{1,0:T(8,128)(2,1)S(1)}, bf16[2048,512]{1,0:T(8,128)(2,1)}, u32[]{:S(2)}) copy-start(bf16[2048,512]{1,0:T(8,128)(2,1)} %get-tuple-element.128) | copy-start | bytes 6291460
  528.2 223.4 %copy-start.4 = (f32[1024,128]{1,0:T(8,128)S(1)}, f32[1024,128]{1,0:T(8,128)}, u32[]{:S(2)}) copy-start(f32[1024,128]{1,0:T(8,128)} %refs_4_.1) | copy-start | bytes 1572868
  528.2 223.4 %copy-start.5 = (f32[128,1024]{1,0:T(8,128)S(1)}, f32[128,1024]{1,0:T(8,128)}, u32[]{:S(2)}) copy-start(f32[128,1024]{1,0:T(8,128)} %refs_1_.1) | copy-start | bytes 1572868
  528.2 223.4 %copy-start.7 = (f32[128,512]{1,0:T(8,128)S(1)}, f32[128,512]{1,0:T(8,128)}, u32[]{:S(2)}) copy-start(f32[128,512]{1,0:T(8,128)} %refs_3_.1) | copy-start | bytes 786436
  718.9 32.7 %copy-start.17 = (f32[8,128]{1,0:T(8,128)S(1)}, f32[8,128]{1,0:T(8,128)}, u32[]{:S(2)}) copy-start(f32[8,128]{1,0:T(8,128)} %get-tuple-element.99.grad_gain.gain) | copy-start | bytes 12292
  718.9 32.7 %copy-start.19 = (f32[128]{0:T(128)S(1)}, f32[128]{0:T(128)}, u32[]{:S(2)}) copy-start(f32[128]{0:T(128)} %param.33) | copy-start | bytes 1540
  718.9 32.7 %copy-start.21 = (f32[128]{0:T(128)S(1)}, f32[128]{0:T(128)}, u32[]{:S(2)}) copy-start(f32[128]{0:T(128)} %param.28) | copy-start | bytes 1540
  718.9 32.7 %copy-start.22 = (f32[128]{0:T(128)S(1)}, f32[128]{0:T(128)}, u32[]{:S(2)}) copy-start(f32[128]{0:T(128)} %param.37) | copy-start | bytes 1540
  718.9 32.7 %copy-start.23 = (f32[128]{0:T(128)S(1)}, f32[128]{0:T(128)}, u32[]{:S(2)}) copy-start(f32[128]{0:T(128)} %param.42) | copy-start | bytes 1540
  719.0 1.2 copy-start.2
  720.2 1.6 copy-start.6
  721.8 1.2 copy-start.9
  723.0 1.2 copy-start.10
  724.3 1.0 copy-start.13
  726.0 25.7 %copy-start.3 = (f32[128,2048]{1,0:T(8,128)S(1)}, f32[128,2048]{1,0:T(8,128)}, u32[]{:S(2)}) copy-start(f32[128,2048]{1,0:T(8,128)} %get-tuple-element.97.grad_qkv.qkv) | copy-start | bytes 3145732
  726.0 25.7 %copy-start.8 = (f32[128,512]{1,0:T(8,128)S(1)}, f32[128,512]{1,0:T(8,128)}, u32[]{:S(2)}) copy-start(f32[128,512]{1,0:T(8,128)} %refs_2_.1) | copy-start | bytes 786436
  726.0 25.7 %copy-start.11 = (f32[128,1024]{1,0:T(8,128)S(1)}, f32[128,1024]{1,0:T(8,128)}, u32[]{:S(2)}) copy-start(f32[128,1024]{1,0:T(8,128)} %refs_10_.1) | copy-start | bytes 1572868
  726.0 25.7 %copy-start.12 = (f32[1024,128]{1,0:T(8,128)S(1)}, f32[1024,128]{1,0:T(8,128)}, u32[]{:S(2)}) copy-start(f32[1024,128]{1,0:T(8,128)} %refs_13_.1) | copy-start | bytes 1572868
  726.0 25.7 %copy-start.14 = (f32[128,512]{1,0:T(8,128)S(1)}, f32[128,512]{1,0:T(8,128)}, u32[]{:S(2)}) copy-start(f32[128,512]{1,0:T(8,128)} %refs_11_.1) | copy-start | bytes 786436
  726.0 25.7 %copy-start.15 = (f32[128,512]{1,0:T(8,128)S(1)}, f32[128,512]{1,0:T(8,128)}, u32[]{:S(2)}) copy-start(f32[128,512]{1,0:T(8,128)} %refs_12_.1) | copy-start | bytes 786436
  751.7 12.9 %copy-start.1 = (s32[64]{0:T(128)S(1)}, s32[64]{0:T(128)}, u32[]{:S(2)}) copy-start(s32[64]{0:T(128)} %param.25) | copy-start | bytes 772
  (1 other events, 0.7 us)
Sparse Core Ops, SparseCore 0:
  12.9 111.9 all-gather.3
  126.5 148.2 all-gather.5
  276.4 78.9 all-gather.7
  362.4 86.2 reduce-scatter.5
  450.9 77.2 reduce-scatter.7
  530.3 101.1 reduce-scatter.3
